TPU v7x, 32 devices: a whole 2x2x4 slice. The times are simulated.
32 devices in a mesh: tm: 8 (over z, y), emit: 4 (over x, core).
Axes of the slice: x: 2, y: 2, z: 4, core: 2. Of those that a mesh axis runs over, the one named last changes fastest.
Arguments:
- observed: int32 [8, 512], P('emit', 'tm'), may hold values from 0 to 4095
- starts: int32 [8], P('emit'), may hold values from 0 to 255
- initial: float32 [256], replicated, may hold values from 0.1 to 1
- transition: float32 [256, 256], replicated, may hold values from 0 to 1, as said below
- emission: float32 [4096, 256], P('emit'), may hold values from 0.5 to 2
Outputs:
- posterior: float32 [8, 512, 256], P('emit', 'tm')
- new_emission: float32 [4096, 256], P(('tm', 'emit'))
- loglik: float32 [8], P('emit')
Inputs may be any that keep to these rules, and one draw needn't show every extreme that they name: `transition`: entries positive.
All inputs are finite; a program needn't handle non-finite values.
Results may differ from a plain program's by a relative error of at most 0.0003.
Values sent between devices are 32-bit elements; how exact they have to be, the bound alone decides.
No kernel may reach another device: no remote copies, remote signals or barrier semaphores. Data moves between devices by JAX's collectives and lax.ppermute only.
A program may use at most 128 MiB of HBM per device.

v0:
```python
import jax
import jax.numpy as jnp
from jax import lax
from jax.sharding import PartitionSpec as P

highest = lax.Precision.HIGHEST
pseudo_count = 0.01


def from_behind(value, axis, by):
    peers = lax.axis_size(axis)
    pairs = [(i, i + by) for i in range(peers) if 0 <= i + by < peers]
    return lax.ppermute(value, axis, pairs)


def normalize_rows(values):
    return values / jnp.sum(values, axis=-1, keepdims=True)


def normalize_blocks(matrices):
    return matrices / jnp.sum(matrices, axis=(1, 2), keepdims=True)


def shards(observed, starts, initial, transition, emission):
    traj_rows, frame_count = observed.shape
    states = transition.shape[0]
    tm_count = lax.axis_size("tm")
    tm_place = lax.axis_index("tm")
    emit_count = lax.axis_size("emit")
    own_rows = emission.shape[0]
    total_rows = own_rows * emit_count
    positions = tm_place * frame_count + jnp.arange(frame_count, dtype=jnp.int32)
    active = positions[None, :] >= starts[:, None]
    block_rows = lax.all_gather(emission, "emit", axis=0, tiled=True)
    local_ids = observed
    inside = (local_ids >= 0) & (local_ids < block_rows.shape[0])
    taken = jnp.take(block_rows, jnp.clip(local_ids, 0, block_rows.shape[0] - 1), axis=0)
    weights = jnp.where(inside[:, :, None], taken, 0.0)
    weight_seq = jnp.swapaxes(weights, 0, 1)
    active_seq = active.T
    eye_block = jnp.broadcast_to(jnp.eye(states, dtype=jnp.float32), (traj_rows, states, states))

    def product_step(carried, inputs):
        weight_now, active_now = inputs
        moved = (
            jnp.einsum("nij,jk->nik", carried, transition, precision=highest)
            * weight_now[:, None, :]
        )
        moved = normalize_blocks(moved)
        return (jnp.where(active_now[:, None, None], moved, carried), None)

    transfer, _ = lax.scan(product_step, eye_block, (weight_seq, active_seq))
    prior_state = jnp.broadcast_to(initial / jnp.sum(initial), (traj_rows, states))
    final_state = jnp.full((traj_rows, states), 1.0 / states, jnp.float32)

    def relay_round(round_index, carried):
        forward_in, backward_in = carried
        forward_out = normalize_rows(
            jnp.einsum("ni,nij->nj", forward_in, transfer, precision=highest)
        )
        backward_out = normalize_rows(
            jnp.einsum("nij,nj->ni", transfer, backward_in, precision=highest)
        )
        from_left = from_behind(forward_out, "tm", 1)
        from_right = from_behind(backward_out, "tm", -1)
        forward_in = jnp.where(tm_place == 0, prior_state, from_left)
        backward_in = jnp.where(tm_place == tm_count - 1, final_state, from_right)
        return (forward_in, backward_in)

    forward_in, backward_in = lax.fori_loop(
        0, tm_count - 1, relay_round, (prior_state, final_state)
    )

    def forward_step(previous, inputs):
        weight_now, active_now = inputs
        moved = jnp.dot(previous, transition, precision=highest) * weight_now
        scaling = jnp.sum(moved, axis=1)
        updated = jnp.where(active_now[:, None], moved / scaling[:, None], previous)
        return (updated, (updated, jnp.where(active_now, jnp.log(scaling), 0.0)))

    _, (forward, log_scales) = lax.scan(forward_step, forward_in, (weight_seq, active_seq))

    def backward_step(later_msg, inputs):
        weight_now, active_now = inputs
        moved = jnp.dot(later_msg * weight_now, transition.T, precision=highest)
        earlier = jnp.where(active_now[:, None], normalize_rows(moved), later_msg)
        return (earlier, later_msg)

    _, backward = lax.scan(backward_step, backward_in, (weight_seq, active_seq), reverse=True)
    joint_prob = forward * backward
    occupancy = jnp.where(active_seq[:, :, None], normalize_rows(joint_prob), 0.0)
    posterior = jnp.swapaxes(states * occupancy, 0, 1)
    loglik_local = jnp.sum(log_scales, axis=0)
    occ_rows = jnp.swapaxes(occupancy, 0, 1).reshape(-1, states)
    frame_list = observed.reshape(-1)
    block = total_rows // (tm_count * emit_count)
    local_ids = frame_list
    inside = (local_ids >= 0) & (local_ids < block * lax.axis_size(("tm", "emit")))
    counts = lax.psum_scatter(
        jax.ops.segment_sum(
            jnp.where(inside[:, None], occ_rows, 0.0),
            jnp.clip(local_ids, 0, block * lax.axis_size(("tm", "emit")) - 1),
            num_segments=block * lax.axis_size(("tm", "emit")),
        ),
        ("tm", "emit"),
        scatter_dimension=0,
        tiled=True,
    )
    totals = lax.psum(jnp.sum(counts, axis=0), ("tm", "emit"))
    loglik_sum = lax.psum(loglik_local, "tm")
    new_emission = total_rows * (counts + pseudo_count) / (totals + total_rows * pseudo_count)
    loglik = loglik_sum / (frame_count * tm_count - starts).astype(jnp.float32)
    return (posterior, new_emission, loglik)


def solution(mesh):
    in_specs = (P("emit", "tm"), P("emit"), P(), P(), P("emit", None))
    out_specs = (P("emit", "tm", None), P(("tm", "emit"), None), P("emit"))
    return jax.shard_map(shards, mesh=mesh, in_specs=in_specs, out_specs=out_specs, check_vma=False)
```

profile of v0, /device:TPU:0, one launch (start us, length us, event | category | flops | bytes accessed | tf_op | source)
XLA Modules:
  0.0 506.2 jit_solution(13056474050517089215)
XLA Ops:
  13.1 33.7 %all-gather.2.cloned.1.call-done = f32[4096,256]{1,0:T(8,128)} async-done(((f32[1024,256]{1,0:T(8,128)}), f32[4096,256]{1,0:T(8,128)}) %all-gather.2.cloned.1.call-update) | async-done | bytes 4194320 | tf_op jit(solution)/shard_map/all_gather | solution.py:34
  46.7 2.9 gather_fusion
  49.9 117.4 %while.55 = (s32[]{:T(128)}, f32[2,256,256]{2,1,0:T(8,128)S(1)}, pred[64,2]{1,0:T(8,128)(4,1)S(1)}, f32[256,256]{1,0:T(8,128)}, f32[64,2,256]{2,1,0:T(2,128)S(1)}, /*index=5*/s32[]{:T(128)}) while((s32[]{:T(128)}, f32[2,256,256]{2,1,0:T(8,128)S(1)}, pred[64,2]{1,0:T(8,128)(4,1)S(1)}, f32[256,256]{1,0:T(8,128)}, f32[64,2,256]{2,1,0:T(2,128)S(1)}, ...), condition=%wide.region_3.4_spmd, body=%wide.region_1.3_spmd.sunk | while | flops 403177472 | bytes 2889835 | solution.py:52
  50.0 1.6 fusion.42
  51.8 1.6 fusion.42
  55.5 1.6 fusion.42
  57.3 1.6 fusion.42
  66.5 1.6 fusion.42
  75.7 1.6 fusion.42
  84.8 1.6 fusion.42
  94.0 1.6 fusion.42
  103.2 1.6 fusion.42
  112.4 1.6 fusion.42
  121.5 1.6 fusion.42
  130.7 1.6 fusion.42
  139.9 1.6 fusion.42
  149.0 1.6 fusion.42
  158.2 1.6 fusion.42
  167.4 65.4 %while.58 = (s32[]{:T(128)}, f32[2,256]{1,0:T(2,128)S(1)}, f32[2,256]{1,0:T(2,128)S(1)}, pred[]{:T(512)}, f32[2,256,256]{2,1,0:T(8,128)S(1)}, /*index=5*/pred[]{:T(512)}, f32[256]{0:T(256)S(1)}, s32[]{:T(128)}, s32[]{:T(128)}) while((s32[]{:T(128)}, f32[2,256]{1,0:T(2,128)S(1)}, f32[2,256]{1,0:T(2,128)S(1)}, pred[]{:T(512)}, ...), condition=%wide.region_7.8_spmd.clone, body=%wide.region_4.7_spmd.clone.sunk | while | flops 3149311 | bytes 1098969 | solution.py:70
  170.0 4.5 collective-permute-start
  178.4 4.9 collective-permute-start
  187.3 5.7 %collective-permute-start = (f32[2,256]{1,0:T(2,128)S(1)}, f32[2,256]{1,0:T(2,128)S(1)}, u32[]{:S(2)}, u32[]{:S(2)}) collective-permute-start(f32[2,256]{1,0:T(2,128)S(1)} %bitcast_divide_fusion.4), channel_id=1, source_target_pairs={{0,4},{4,8},{8,12},{12,16},{16,20},{20,24},{24,28},{1,5},{5,9},{9,... | collective-permute-start | bytes 6152 | tf_op jit(solution)/shard_map/while/body/eval_jaxpr/ppermute | solution.py:13
  196.9 5.7 %collective-permute-start = (f32[2,256]{1,0:T(2,128)S(1)}, f32[2,256]{1,0:T(2,128)S(1)}, u32[]{:S(2)}, u32[]{:S(2)}) collective-permute-start(f32[2,256]{1,0:T(2,128)S(1)} %bitcast_divide_fusion.4), channel_id=1, source_target_pairs={{0,4},{4,8},{8,12},{12,16},{16,20},{20,24},{24,28},{1,5},{5,9},{9,... | collective-permute-start | bytes 6152 | tf_op jit(solution)/shard_map/while/body/eval_jaxpr/ppermute | solution.py:13
  206.5 5.7 %collective-permute-start = (f32[2,256]{1,0:T(2,128)S(1)}, f32[2,256]{1,0:T(2,128)S(1)}, u32[]{:S(2)}, u32[]{:S(2)}) collective-permute-start(f32[2,256]{1,0:T(2,128)S(1)} %bitcast_divide_fusion.4), channel_id=1, source_target_pairs={{0,4},{4,8},{8,12},{12,16},{16,20},{20,24},{24,28},{1,5},{5,9},{9,... | collective-permute-start | bytes 6152 | tf_op jit(solution)/shard_map/while/body/eval_jaxpr/ppermute | solution.py:13
  216.1 5.7 %collective-permute-start = (f32[2,256]{1,0:T(2,128)S(1)}, f32[2,256]{1,0:T(2,128)S(1)}, u32[]{:S(2)}, u32[]{:S(2)}) collective-permute-start(f32[2,256]{1,0:T(2,128)S(1)} %bitcast_divide_fusion.4), channel_id=1, source_target_pairs={{0,4},{4,8},{8,12},{12,16},{16,20},{20,24},{24,28},{1,5},{5,9},{9,... | collective-permute-start | bytes 6152 | tf_op jit(solution)/shard_map/while/body/eval_jaxpr/ppermute | solution.py:13
  225.7 5.7 %collective-permute-start = (f32[2,256]{1,0:T(2,128)S(1)}, f32[2,256]{1,0:T(2,128)S(1)}, u32[]{:S(2)}, u32[]{:S(2)}) collective-permute-start(f32[2,256]{1,0:T(2,128)S(1)} %bitcast_divide_fusion.4), channel_id=1, source_target_pairs={{0,4},{4,8},{8,12},{12,16},{16,20},{20,24},{24,28},{1,5},{5,9},{9,... | collective-permute-start | bytes 6152 | tf_op jit(solution)/shard_map/while/body/eval_jaxpr/ppermute | solution.py:13
  232.8 38.5 %while.57 = (s32[]{:T(128)}, f32[2,256]{1,0:T(2,128)S(1)}, f32[64,2,256]{2,0,1:T(8,128)S(1)}, pred[64,2]{1,0:T(8,128)(4,1)S(1)}, f32[64,2,256]{2,1,0:T(2,128)S(1...) while((s32[]{:T(128)}, f32[2,256]{1,0:T(2,128)S(1)}, f32[64,2,256]{2,0,1:T(8,128)S(1)}, ...), condition=%wide.region_13.14_spmd, body=%wide.region_11.13_spmd.sunk | while | flops 1574913 | bytes 282763 | solution.py:89
  271.3 36.6 %while.56 = (s32[]{:T(128)}, f32[2,256]{1,0:T(2,128)S(1)}, f32[64,2,256]{2,0,1:T(8,128)S(1)}, f32[64,2]{1,0:T(8,128)S(1)}, pred[64,2]{1,0:T(8,128)(4,1)S(1)}, /*...) while((s32[]{:T(128)}, f32[2,256]{1,0:T(2,128)S(1)}, ...), condition=%wide.region_10.11_spmd, body=%wide.region_8.10_spmd.sunk | while | flops 1574914 | bytes 282801 | solution.py:81
  308.4 3.4 scatter_custom_fusion
  311.8 26.6 %psum.15 = f32[2]{0:T(128)S(1)} all-reduce(f32[2]{0:T(128)S(1)} %reduce_sum.94), channel_id=1, replica_groups=mesh['tm'=8,'emit'=4] {'tm'}, use_global_device_ids=true, to_apply=%region_20.21 | all-reduce | flops 2 | bytes 16 | tf_op jit(solution)/shard_map/psum | solution.py:110
  339.6 120.4 %reduce-scatter.2.cloned.1.call-done = f32[128,256]{1,0:T(8,128)} async-done(((f32[4096,256]{1,0:T(8,128)}), f32[128,256]{1,0:T(8,128)}) %reduce-scatter.2.cloned.1.call-update) | async-done | bytes 131088 | tf_op jit(solution)/shard_map/reduce_scatter | solution.py:99
  461.0 36.9 %psum.14 = f32[256]{0:T(256)S(1)} all-reduce(f32[256]{0:T(256)S(1)} %reduce_sum.93), channel_id=1, replica_groups=mesh['tm'=8,'emit'=4] {'tm','emit'}, use_global_device_ids=true, to_apply=%region_18.19 | all-reduce | flops 256 | bytes 2048 | tf_op jit(solution)/shard_map/psum | solution.py:109
  (1129 shorter events, 197.4 us)
Async XLA Ops:
  7.2 39.6 %all-gather.2.cloned.1.call-start = ((), (), s32[]{:S(2)}) async-start(), calls=%async_computation.1 | async-start | bytes 5242880 | tf_op jit(solution)/shard_map/all_gather | solution.py:34
  7.9 452.1 %reduce-scatter.2.cloned.1.call-start = ((), (), s32[]{:S(2)}) async-start(), calls=%async_computation.2 | async-start | bytes 4325376 | tf_op jit(solution)/shard_map/reduce_scatter | solution.py:99
  167.3 65.4 %copy-start = (f32[256,256]{1,0:T(8,128)S(1)}, f32[256,256]{1,0:T(8,128)}, u32[]{:S(2)}) copy-start(f32[256,256]{1,0:T(8,128)} %get-tuple-element.664) | copy-start | bytes 786436
  168.1 6.4 %collective-permute-start.1 = (f32[2,256]{1,0:T(2,128)S(1)}, f32[2,256]{1,0:T(2,128)S(1)}, u32[]{:S(2)}, u32[]{:S(2)}) collective-permute-start(f32[2,256]{1,0:T(2,128)S(1)} %bitcast_divide_fusion.5), channel_id=1, source_target_pairs={{4,0},{8,4},{12,8},{16,12},{20,16},{24,20},{28,24},{5,1},{9,5},{13... | collective-permute-start | bytes 6152 | tf_op jit(solution)/shard_map/while/body/eval_jaxpr/ppermute | solution.py:13
  170.0 5.8 %collective-permute-start = (f32[2,256]{1,0:T(2,128)S(1)}, f32[2,256]{1,0:T(2,128)S(1)}, u32[]{:S(2)}, u32[]{:S(2)}) collective-permute-start(f32[2,256]{1,0:T(2,128)S(1)} %bitcast_divide_fusion.4), channel_id=1, source_target_pairs={{0,4},{4,8},{8,12},{12,16},{16,20},{20,24},{24,28},{1,5},{5,9},{9,... | collective-permute-start | bytes 6152 | tf_op jit(solution)/shard_map/while/body/eval_jaxpr/ppermute | solution.py:13
  176.6 6.8 %collective-permute-start.1 = (f32[2,256]{1,0:T(2,128)S(1)}, f32[2,256]{1,0:T(2,128)S(1)}, u32[]{:S(2)}, u32[]{:S(2)}) collective-permute-start(f32[2,256]{1,0:T(2,128)S(1)} %bitcast_divide_fusion.5), channel_id=1, source_target_pairs={{4,0},{8,4},{12,8},{16,12},{20,16},{24,20},{28,24},{5,1},{9,5},{13... | collective-permute-start | bytes 6152 | tf_op jit(solution)/shard_map/while/body/eval_jaxpr/ppermute | solution.py:13
  178.4 6.2 %collective-permute-start = (f32[2,256]{1,0:T(2,128)S(1)}, f32[2,256]{1,0:T(2,128)S(1)}, u32[]{:S(2)}, u32[]{:S(2)}) collective-permute-start(f32[2,256]{1,0:T(2,128)S(1)} %bitcast_divide_fusion.4), channel_id=1, source_target_pairs={{0,4},{4,8},{8,12},{12,16},{16,20},{20,24},{24,28},{1,5},{5,9},{9,... | collective-permute-start | bytes 6152 | tf_op jit(solution)/shard_map/while/body/eval_jaxpr/ppermute | solution.py:13
  185.4 7.6 %collective-permute-start.1 = (f32[2,256]{1,0:T(2,128)S(1)}, f32[2,256]{1,0:T(2,128)S(1)}, u32[]{:S(2)}, u32[]{:S(2)}) collective-permute-start(f32[2,256]{1,0:T(2,128)S(1)} %bitcast_divide_fusion.5), channel_id=1, source_target_pairs={{4,0},{8,4},{12,8},{16,12},{20,16},{24,20},{28,24},{5,1},{9,5},{13... | collective-permute-start | bytes 6152 | tf_op jit(solution)/shard_map/while/body/eval_jaxpr/ppermute | solution.py:13
  187.3 7.0 %collective-permute-start = (f32[2,256]{1,0:T(2,128)S(1)}, f32[2,256]{1,0:T(2,128)S(1)}, u32[]{:S(2)}, u32[]{:S(2)}) collective-permute-start(f32[2,256]{1,0:T(2,128)S(1)} %bitcast_divide_fusion.4), channel_id=1, source_target_pairs={{0,4},{4,8},{8,12},{12,16},{16,20},{20,24},{24,28},{1,5},{5,9},{9,... | collective-permute-start | bytes 6152 | tf_op jit(solution)/shard_map/while/body/eval_jaxpr/ppermute | solution.py:13
  195.0 7.6 %collective-permute-start.1 = (f32[2,256]{1,0:T(2,128)S(1)}, f32[2,256]{1,0:T(2,128)S(1)}, u32[]{:S(2)}, u32[]{:S(2)}) collective-permute-start(f32[2,256]{1,0:T(2,128)S(1)} %bitcast_divide_fusion.5), channel_id=1, source_target_pairs={{4,0},{8,4},{12,8},{16,12},{20,16},{24,20},{28,24},{5,1},{9,5},{13... | collective-permute-start | bytes 6152 | tf_op jit(solution)/shard_map/while/body/eval_jaxpr/ppermute | solution.py:13
  196.9 7.0 %collective-permute-start = (f32[2,256]{1,0:T(2,128)S(1)}, f32[2,256]{1,0:T(2,128)S(1)}, u32[]{:S(2)}, u32[]{:S(2)}) collective-permute-start(f32[2,256]{1,0:T(2,128)S(1)} %bitcast_divide_fusion.4), channel_id=1, source_target_pairs={{0,4},{4,8},{8,12},{12,16},{16,20},{20,24},{24,28},{1,5},{5,9},{9,... | collective-permute-start | bytes 6152 | tf_op jit(solution)/shard_map/while/body/eval_jaxpr/ppermute | solution.py:13
  204.6 7.6 %collective-permute-start.1 = (f32[2,256]{1,0:T(2,128)S(1)}, f32[2,256]{1,0:T(2,128)S(1)}, u32[]{:S(2)}, u32[]{:S(2)}) collective-permute-start(f32[2,256]{1,0:T(2,128)S(1)} %bitcast_divide_fusion.5), channel_id=1, source_target_pairs={{4,0},{8,4},{12,8},{16,12},{20,16},{24,20},{28,24},{5,1},{9,5},{13... | collective-permute-start | bytes 6152 | tf_op jit(solution)/shard_map/while/body/eval_jaxpr/ppermute | solution.py:13
  206.5 7.0 %collective-permute-start = (f32[2,256]{1,0:T(2,128)S(1)}, f32[2,256]{1,0:T(2,128)S(1)}, u32[]{:S(2)}, u32[]{:S(2)}) collective-permute-start(f32[2,256]{1,0:T(2,128)S(1)} %bitcast_divide_fusion.4), channel_id=1, source_target_pairs={{0,4},{4,8},{8,12},{12,16},{16,20},{20,24},{24,28},{1,5},{5,9},{9,... | collective-permute-start | bytes 6152 | tf_op jit(solution)/shard_map/while/body/eval_jaxpr/ppermute | solution.py:13
  214.2 7.6 %collective-permute-start.1 = (f32[2,256]{1,0:T(2,128)S(1)}, f32[2,256]{1,0:T(2,128)S(1)}, u32[]{:S(2)}, u32[]{:S(2)}) collective-permute-start(f32[2,256]{1,0:T(2,128)S(1)} %bitcast_divide_fusion.5), channel_id=1, source_target_pairs={{4,0},{8,4},{12,8},{16,12},{20,16},{24,20},{28,24},{5,1},{9,5},{13... | collective-permute-start | bytes 6152 | tf_op jit(solution)/shard_map/while/body/eval_jaxpr/ppermute | solution.py:13
  216.1 7.0 %collective-permute-start = (f32[2,256]{1,0:T(2,128)S(1)}, f32[2,256]{1,0:T(2,128)S(1)}, u32[]{:S(2)}, u32[]{:S(2)}) collective-permute-start(f32[2,256]{1,0:T(2,128)S(1)} %bitcast_divide_fusion.4), channel_id=1, source_target_pairs={{0,4},{4,8},{8,12},{12,16},{16,20},{20,24},{24,28},{1,5},{5,9},{9,... | collective-permute-start | bytes 6152 | tf_op jit(solution)/shard_map/while/body/eval_jaxpr/ppermute | solution.py:13
  223.9 7.6 %collective-permute-start.1 = (f32[2,256]{1,0:T(2,128)S(1)}, f32[2,256]{1,0:T(2,128)S(1)}, u32[]{:S(2)}, u32[]{:S(2)}) collective-permute-start(f32[2,256]{1,0:T(2,128)S(1)} %bitcast_divide_fusion.5), channel_id=1, source_target_pairs={{4,0},{8,4},{12,8},{16,12},{20,16},{24,20},{28,24},{5,1},{9,5},{13... | collective-permute-start | bytes 6152 | tf_op jit(solution)/shard_map/while/body/eval_jaxpr/ppermute | solution.py:13
  225.7 7.0 %collective-permute-start = (f32[2,256]{1,0:T(2,128)S(1)}, f32[2,256]{1,0:T(2,128)S(1)}, u32[]{:S(2)}, u32[]{:S(2)}) collective-permute-start(f32[2,256]{1,0:T(2,128)S(1)} %bitcast_divide_fusion.4), channel_id=1, source_target_pairs={{0,4},{4,8},{8,12},{12,16},{16,20},{20,24},{24,28},{1,5},{5,9},{9,... | collective-permute-start | bytes 6152 | tf_op jit(solution)/shard_map/while/body/eval_jaxpr/ppermute | solution.py:13
  308.4 30.1 %copy-start.1 = (s32[2]{0:T(128)S(1)}, s32[2]{0:T(128)}, u32[]{:S(2)}) copy-start(s32[2]{0:T(128)} %param.14) | copy-start | bytes 28
Sparse Core Ops, SparseCore 0:
  9.5 37.1 all-gather.1
  311.9 148.0 reduce-scatter.1
where the time goes:
time: 510 us; the launch traced here: 506 us
  waiting for transfers between devices  164 us (32%)
  matrix products  159 us (31%)
  blocking collectives  63.5 us (12%)
  starting transfers between devices  47.2 us (9%)
  other arithmetic  36.2 us (7%)
  local copies, waits for them, and re-layouts  14.3 us (3%)
  between operations  14.2 us (3%)
  loops' own time  8.46 us (2%)
    reduce_scatter x1, waiting for transfers between devices, shards(): lax.psum_scatter(jax.ops.segment_sum(jnp.where(inside[:, None], occ_rows,...  120 us
    dot_general x64, matrix products, product_step(): jnp.einsum('nij,jk->nik', carried, transition, precision=highest)  104 us
    ppermute x14, starting transfers between devices, from_behind(): return lax.ppermute(value, axis, pairs)  47.1 us
    psum x1, blocking collectives, shards(): totals = lax.psum(jnp.sum(counts, axis=0), ('tm', 'emit'))  36.9 us
    all_gather x1, waiting for transfers between devices, shards(): block_rows = lax.all_gather(emission, 'emit', axis=0, tiled=True)  33.7 us
    dot_general x64, matrix products, backward_step(): moved = jnp.dot(later_msg * weight_now, transition.T, precision=highest)  27.4 us
    psum x1, blocking collectives, shards(): loglik_sum = lax.psum(loglik_local, 'tm')  26.6 us
    dot_general x64, matrix products, forward_step(): moved = jnp.dot(previous, transition, precision=highest) * weight_now  21.3 us
  transfers between devices with their start and end apart: 16, of which 9 were waited for; matrix products, arithmetic and copies ran while one was open for 2% of the time, Pallas kernels for 0%

commit v1 on v0

v1 whole, which is shorter than its diff:
```python
import jax
import jax.numpy as jnp
from jax import lax
from jax.experimental import pallas as pl
from jax.experimental.pallas import tpu as pltpu
from jax.sharding import PartitionSpec as P

pseudo_count = 0.01
f32 = jnp.float32
bf16 = jnp.bfloat16
chunks = 8
slots = 16
rows_sent = 14


def split2(x):
    high = x.astype(bf16)
    return high, (x - high.astype(f32)).astype(bf16)


def split3(x):
    high = x.astype(bf16)
    rest = x - high.astype(f32)
    mid = rest.astype(bf16)
    return high, mid, (rest - mid.astype(f32)).astype(bf16)


def iota(shape, dim):
    return lax.broadcasted_iota(jnp.int32, shape, dim)


def dot(a, b):
    return lax.dot_general(a, b, (((1,), (0,)), ((), ())), preferred_element_type=f32)


def dot_nt(a, b):
    return lax.dot_general(a, b, (((1,), (1,)), ((), ())), preferred_element_type=f32)


def stack3(x):
    high = x.astype(bf16).astype(f32)
    rest = x - high
    mid = rest.astype(bf16).astype(f32)
    return jnp.concatenate([high, mid, rest - mid], axis=0).astype(bf16)


def combine(y, rows, states, terms):
    def part(i, j):
        return y[i * rows : (i + 1) * rows, j * states : (j + 1) * states]

    small = part(1, 1) + part(2, 0)
    if terms == 3:
        small = small + part(0, 2)
    return part(0, 0) + ((part(0, 1) + part(1, 0)) + small)


def row_times(x, cat, states, terms):
    return combine(dot(stack3(x), cat), x.shape[0], states, terms)


def times_col(x, cat, states, terms):
    return combine(dot_nt(stack3(x), cat), x.shape[0], states, terms)


def take(ref, start, steps):
    return jnp.concatenate([ref.at[h][pl.ds(start, chunks, stride=steps), :] for h in range(ref.shape[0])], axis=1)


def put(ref, start, steps, x):
    for h in range(ref.shape[0]):
        ref.at[h][pl.ds(start, chunks, stride=steps), :] = x[:, h * 128 : (h + 1) * 128]


def whole(ref):
    return jnp.concatenate([ref[h] for h in range(ref.shape[0])], axis=1)


def normalize(x):
    return x / jnp.sum(x, axis=1, keepdims=True)


def gather_kernel(ids_ref, table_ref, out_ref):
    groups, frames = ids_ref.shape
    rows, states = table_ref.shape
    high, mid, low = split3(table_ref[...])
    eye = iota((frames, frames), 0) == iota((frames, frames), 1)
    lanes = iota((frames, rows), 1)
    for k in range(groups):
        wide = jnp.where(eye, jnp.broadcast_to(ids_ref[k : k + 1, :], (frames, frames)), 0)
        column = jnp.sum(wide, axis=1, keepdims=True)
        pick = jnp.where(column == lanes, 1.0, 0.0).astype(bf16)
        out_ref[k] = dot(pick, high) + (dot(pick, mid) + dot(pick, low))


def product_kernel(scal_ref, own_ref, *refs):
    count = len(refs) - 8
    recv_refs = refs[:count]
    trans_ref, init_ref, w_ref, high_ref, low_ref, state_ref, msg_ref, x_ref = refs[count:]
    frames, states = w_ref.shape
    steps = frames // chunks
    first = scal_ref[0]
    w = own_ref[0]
    for r in recv_refs:
        w = w + r[...]
    w_ref[...] = w
    trans = trans_ref[...]
    t1, t2 = split2(trans)
    eye = jnp.where(iota((states, states), 0) == iota((states, states), 1), 1.0, 0.0)

    def inverse_sum(x):
        return 1.0 / jnp.sum(jnp.sum(x, axis=0, keepdims=True), axis=1, keepdims=True)

    scales = []
    for c in range(chunks):
        x = jnp.where(c * steps >= first, trans * w_ref[c * steps : c * steps + 1, :], eye)
        x_ref[c] = x
        scales.append(inverse_sum(x))

    def step(k, scales):
        after = []
        for c in range(chunks):
            x = x_ref[c] * scales[c]
            x1, x2 = split2(x)
            y = dot(x1, t1) + (dot(x1, t2) + dot(x2, t1))
            y = y * w_ref[pl.ds(c * steps + k, 1), :]
            y = jnp.where(c * steps + k >= first, y, x)
            x_ref[c] = y
            after.append(inverse_sum(y))
        return tuple(after)

    scales = lax.fori_loop(1, steps, step, tuple(scales))
    at = 0
    level = []
    for c in range(chunks):
        x1, x2 = split2(x_ref[c] * scales[c])
        high_ref[at] = x1
        low_ref[at] = x2
        level.append(at)
        at += 1
    while len(level) > 1:
        upper = []
        for i in range(0, len(level), 2):
            a1, a2 = high_ref[level[i]], low_ref[level[i]]
            b1, b2 = high_ref[level[i + 1]], low_ref[level[i + 1]]
            y = dot(a1, b1) + (dot(a1, b2) + dot(a2, b1))
            y1, y2 = split2(y * inverse_sum(y))
            high_ref[at] = y1
            low_ref[at] = y2
            upper.append(at)
            at += 1
        level = upper
    init = init_ref[...]
    prior = jnp.broadcast_to(init / jnp.sum(init, axis=1, keepdims=True), (8, states))
    final = jnp.full((8, states), 1.0 / states, f32)
    root1, root2 = high_ref[level[0]], low_ref[level[0]]
    ahead = row_times(prior, jnp.concatenate([root1, root2], axis=1), states, 2)
    behind = times_col(final, jnp.concatenate([root1, root2], axis=0), states, 2)
    top = iota((8, states), 0) == 0
    state_ref[...] = jnp.where(top, prior, final)
    msg_ref[...] = jnp.where(top, normalize(ahead), normalize(behind))


def merge_state(state, recv, part, parts, turn):
    spot = iota(state.shape, 0)
    take = ((spot == 0) & (part == turn + 1)) | ((spot == 1) & (part == parts - 2 - turn))
    return jnp.where(take, recv, state)


def relay_kernel(parts, turn, scal_ref, state_ref, recv_ref, high_ref, low_ref, out_ref, msg_ref):
    states = state_ref.shape[1]
    state = merge_state(state_ref[...], recv_ref[...], scal_ref[1], parts, turn - 1)
    out_ref[...] = state
    root1, root2 = high_ref[0], low_ref[0]
    ahead = row_times(state, jnp.concatenate([root1, root2], axis=1), states, 2)
    behind = times_col(state, jnp.concatenate([root1, root2], axis=0), states, 2)
    msg_ref[...] = jnp.where(iota((8, states), 0) == 0, normalize(ahead), normalize(behind))


def place(ids_ref, scal_ref, block, turn):
    frames = ids_ref.shape[1]
    square = (frames, frames)
    bits = block.bit_length() - 1
    down, across = iota(square, 0), iota(square, 1)
    row = jnp.broadcast_to(ids_ref[0:1, :], square)
    live = across >= scal_ref[0]
    column = jnp.broadcast_to(jnp.sum(jnp.where(down == across, row, 0), axis=1, keepdims=True), square)
    live_column = down >= scal_ref[0]
    owner_row = jnp.where(live, lax.shift_right_logical(row, bits), -1)
    owner_column = jnp.where(live_column, lax.shift_right_logical(column, bits), -1)
    same = owner_row == owner_column
    rank_row = jnp.sum(jnp.where(same & (down < across), 1, 0), axis=0, keepdims=True)
    rank_column = jnp.sum(jnp.where(same & (across < down), 1, 0), axis=1, keepdims=True)
    most = jnp.max(jnp.where(live[0:1, :], rank_row + 1, 0))
    rank_row = rank_row - rows_sent * turn
    rank_column = rank_column - rows_sent * turn
    fits_row = (rank_row >= 0) & (rank_row < rows_sent) & live[0:1, :]
    fits_column = (rank_column >= 0) & (rank_column < rows_sent) & live_column[:, 0:1]
    local = (column - lax.shift_left(lax.shift_right_logical(column, bits), bits))[:, 0:1]
    return owner_row[0:1, :], rank_row, fits_row, rank_column, fits_column, local, most


def pack(ids_ref, scal_ref, occupancy, send_ref, block, turn, log_sum):
    frames, states = occupancy.shape
    devices = send_ref.shape[0] // slots
    owner, rank, fits, rank_column, fits_column, local, most = place(ids_ref, scal_ref, block, turn)
    spot = jnp.where(fits, owner * slots + rank, -1)
    lines = iota((devices * slots, frames), 0)
    pick = lines == spot
    totals = (lax.bitwise_and(lines, slots - 1) == rows_sent) & (turn == 0)
    pick = jnp.where(pick | totals, 1.0, 0.0).astype(bf16)
    high, mid, low = split3(occupancy)
    base = scal_ref[2]
    lanes = iota((frames, states), 1)
    ranked = jnp.where(fits_column & (lanes == base + rank_column), (local + 1).astype(f32), 0.0).astype(bf16)
    mine = jnp.where((lines == owner * slots + slots - 1) & fits, 1.0, 0.0).astype(bf16)
    sent = dot(pick, high) + (dot(pick, mid) + (dot(pick, low) + dot(mine, ranked)))
    lines = lax.bitwise_and(iota((devices * slots, 1), 0), slots - 1) == slots - 1
    lanes = iota((1, states), 1)
    sent = jnp.where(lines & (lanes == base + rows_sent), log_sum, sent)
    send_ref[...] = jnp.where(lines & (lanes == base + rows_sent + 1), most.astype(f32), sent)


def chain_kernel(parts, block, scal_ref, state_ref, recv_ref, w_ref, high_ref, low_ref, trans_ref, ids_ref,
                 keep_ref, away_ref, occ_ref, send_ref, split_ref, fore_ref, back_ref,
                 start_ref, end_ref, post_ref):
    frames, states = w_ref.shape
    steps = frames // chunks
    first = scal_ref[0]
    state = merge_state(state_ref[...], recv_ref[...], scal_ref[1], parts, parts - 2)
    start_ref[0:1, :] = state[0:1, :]
    end_ref[chunks - 1 : chunks, :] = state[1:2, :]
    width = chunks
    offsets = {}
    at = 0
    size = chunks
    while size >= 1:
        offsets[chunks // size] = at
        at += size
        size //= 2
    while width > 1:
        half = width // 2
        for g in range(chunks // width):
            left = offsets[half] + 2 * g
            lead = jnp.broadcast_to(start_ref[g * width : g * width + 1, :], (8, states))
            cat = jnp.concatenate([high_ref[left], low_ref[left]], axis=1)
            made = normalize(row_times(lead, cat, states, 2))
            start_ref[g * width + half : g * width + half + 1, :] = made[0:1, :]
            last = g * width + width - 1
            tail = jnp.broadcast_to(end_ref[last : last + 1, :], (8, states))
            cat = jnp.concatenate([high_ref[left + 1], low_ref[left + 1]], axis=0)
            made = normalize(times_col(tail, cat, states, 2))
            end_ref[last - half : last - half + 1, :] = made[0:1, :]
        width = half
    trans = trans_ref[...]
    ahead = jnp.concatenate(split3(trans), axis=1)
    behind = jnp.concatenate(split3(trans), axis=0)
    for h in range(states // 128):
        split_ref[h] = w_ref[:, h * 128 : (h + 1) * 128]
    fore = start_ref[...]
    back = end_ref[...]
    logs = jnp.zeros((chunks, 1), f32)
    spots = iota((chunks, 1), 0) * steps
    for k in range(steps):
        moved = row_times(fore, ahead, states, 3) * take(split_ref, k, steps)
        scaling = jnp.sum(moved, axis=1, keepdims=True)
        active = spots + k >= first
        fore = jnp.where(active, moved / scaling, fore)
        logs = logs + jnp.where(active, jnp.log(scaling), 0.0)
        put(fore_ref, k, steps, fore)
        j = steps - 1 - k
        put(back_ref, j, steps, back)
        moved = times_col(back * take(split_ref, j, steps), behind, states, 3)
        back = jnp.where(spots + j >= first, normalize(moved), back)
    joint = whole(fore_ref) * whole(back_ref)
    occupancy = jnp.where(iota((frames, 1), 0) >= first, normalize(joint), 0.0)
    occ_ref[...] = occupancy
    post_ref[...] = states * occupancy
    side = scal_ref[3]
    half = frames // 2
    keep_ref[...] = post_ref[pl.ds(pl.multiple_of(side * half, half), half), :]
    away_ref[...] = post_ref[pl.ds(pl.multiple_of((1 - side) * half, half), half), :]
    pack(ids_ref, scal_ref, occupancy, send_ref, block, 0, jnp.sum(logs))


def counted(recv_ref, block):
    lines, states = recv_ref.shape
    counts = jnp.zeros((block, states), f32)
    totals = jnp.zeros((1, states), f32)
    slot = lax.bitwise_and(iota((block, states), 1), slots - 1)
    line = lax.bitwise_and(iota((states, states), 0), slots - 1)
    row = (iota((block, states), 0) + 1).astype(f32)
    metas = []
    for g in range(lines // states):
        came = recv_ref[g * states : (g + 1) * states, :]
        meta = jnp.sum(jnp.where(line == slots - 1, came, 0.0), axis=0, keepdims=True)
        totals = totals + jnp.sum(jnp.where(line == rows_sent, came, 0.0), axis=0, keepdims=True)
        pick = jnp.where((meta == row) & (slot < rows_sent), 1.0, 0.0).astype(bf16)
        high, mid, low = split3(came)
        counts = counts + (dot(pick, high) + (dot(pick, mid) + dot(pick, low)))
        metas.append(meta)
    return counts, totals, metas


def emit_update(counts, totals, total_rows):
    return total_rows * (counts + pseudo_count) / (totals + total_rows * pseudo_count)


def final_kernel(block, total_rows, emit_count, length, scal_ref, recv_ref, keep_ref, other_ref,
                 post_ref, new_ref, log_ref, counts_ref, totals_ref, most_ref):
    states = recv_ref.shape[1]
    counts, totals, metas = counted(recv_ref, block)
    counts_ref[...] = counts
    totals_ref[...] = totals
    new_ref[...] = emit_update(counts, totals, total_rows)
    lanes = iota((1, states), 1)
    slot = lax.bitwise_and(lanes, slots - 1)
    most = 0.0
    sums = [0.0, 0.0]
    for g, meta in enumerate(metas):
        most = jnp.maximum(most, jnp.max(jnp.where(slot == rows_sent + 1, meta, 0.0)))
        source = g * (states // slots) + lax.shift_right_logical(lanes, slots.bit_length() - 1)
        column = (lax.bitwise_and(source, emit_count - 1) == scal_ref[4]) & (slot == rows_sent)
        odd = lax.bitwise_and(lax.shift_right_logical(source, emit_count.bit_length() - 1), 1)
        for j in range(2):
            sums[j] = sums[j] + jnp.sum(jnp.where(column & (odd == j), meta, 0.0))
    most_ref[0] = most.astype(jnp.int32)
    for j in range(2):
        log_ref[j] = sums[j] / (length - scal_ref[5 + j]).astype(f32)
    side = scal_ref[3]
    post_ref[side] = keep_ref[...]
    post_ref[1 - side] = other_ref[...]


def pack_kernel(block, scal_ref, turn_ref, occ_ref, ids_ref, send_ref):
    pack(ids_ref, scal_ref, occ_ref[...], send_ref, block, turn_ref[0], 0.0)


def more_kernel(block, recv_ref, counts_ref, out_ref):
    counts, _, _ = counted(recv_ref, block)
    out_ref[...] = counts_ref[...] + counts


vmem = pl.BlockSpec(memory_space=pltpu.MemorySpace.VMEM)
smem = pl.BlockSpec(memory_space=pltpu.MemorySpace.SMEM)


def call(kernel, name, in_specs, out_specs, out_shape, scratch=()):
    return pl.pallas_call(kernel, name=name, in_specs=in_specs, out_specs=out_specs, out_shape=out_shape,
                          scratch_shapes=scratch)


def shape(*dims, dtype=f32):
    return jax.ShapeDtypeStruct(dims, dtype)


def shards(observed, starts, initial, transition, emission):
    traj_rows, frame_count = observed.shape
    states = transition.shape[0]
    tm_count = lax.axis_size("tm")
    tm_place = lax.axis_index("tm")
    emit_count = lax.axis_size("emit")
    emit_place = lax.axis_index("emit")
    both = ("tm", "emit")
    devices = tm_count * emit_count
    own_rows = emission.shape[0]
    total_rows = own_rows * emit_count
    block = total_rows // devices
    length = frame_count * tm_count
    assert traj_rows == 2 and tm_count % 2 == 0
    frames = 2 * frame_count
    parts = tm_count // 2
    part = tm_place // 2
    side = tm_place % 2
    flat = tm_place * emit_count + emit_place

    kept = jnp.where(side == 0, observed[0:1], observed[1:2])
    given = jnp.where(side == 0, observed[1:2], observed[0:1])
    taken = lax.ppermute(given, "tm", [(i, i ^ 1) for i in range(tm_count)])
    ids = jnp.where(side == 0, jnp.concatenate([kept, taken], axis=1), jnp.concatenate([taken, kept], axis=1))
    first = jnp.where(side == 0, starts[0], starts[1]) - part * frames
    scal = jnp.stack([first, part, (flat % (states // slots)) * slots, side, emit_place, starts[0], starts[1]])
    scal = scal.astype(jnp.int32)

    def swaps(k):
        return [(i, i ^ k) for i in range(emit_count)]

    others = [lax.ppermute(ids, "emit", swaps(k)) for k in range(1, emit_count)]
    wanted = jnp.concatenate([ids] + others, axis=0) - emit_place * own_rows
    rows = call(gather_kernel, "gather", [vmem, vmem], vmem, shape(emit_count, frames, states))(wanted, emission)
    came = [lax.ppermute(rows[k], "emit", swaps(k)) for k in range(1, emit_count)]
    nodes = 2 * chunks - 1
    weights, high, low, state, message = pl.pallas_call(
        product_kernel, name="product", grid=(1,),
        in_specs=[smem, pl.BlockSpec((1, frames, states), lambda i: (0, 0, 0))]
        + [pl.BlockSpec((frames, states), lambda i: (0, 0))] * (emit_count - 1)
        + [pl.BlockSpec((states, states), lambda i: (0, 0)), pl.BlockSpec((1, states), lambda i: (0, 0))],
        out_specs=[vmem] * 5,
        out_shape=[shape(frames, states), shape(nodes, states, states, dtype=bf16),
                   shape(nodes, states, states, dtype=bf16), shape(8, states), shape(8, states)],
        scratch_shapes=[pltpu.VMEM((chunks, states, states), f32)],
    )(scal, rows, *came, transition, initial.reshape(1, states))

    def relay_pairs(turn):
        pairs = []
        for y in range(2):
            pairs.append((2 * turn + y, 2 * turn + 2 + y))
            pairs.append((2 * (parts - 1 - turn) + y, 2 * (parts - 2 - turn) + y))
        return pairs

    root = pl.BlockSpec((1, states, states), lambda i: (nodes - 1, 0, 0))
    line = pl.BlockSpec((8, states), lambda i: (0, 0))
    recv = lax.ppermute(message, "tm", relay_pairs(0))
    for turn in range(1, parts - 1):
        def relay(*refs, turn=turn):
            relay_kernel(parts, turn, *refs)

        state, message = pl.pallas_call(
            relay, name="relay", grid=(1,), in_specs=[smem, line, line, root, root],
            out_specs=[vmem, vmem], out_shape=[shape(8, states), shape(8, states)],
        )(scal, state, recv, high, low)
        recv = lax.ppermute(message, "tm", relay_pairs(turn))

    def chain(*refs):
        chain_kernel(parts, block, *refs)

    keep, away, occupancy, send = call(
        chain, "chain", [smem] + [vmem] * 7, [vmem] * 4,
        [shape(frame_count, states), shape(frame_count, states), shape(frames, states), shape(devices * slots, states)],
        [pltpu.VMEM((states // 128, frames, 128), f32)] * 3
        + [pltpu.VMEM((chunks, states), f32)] * 2 + [pltpu.VMEM((frames, states), f32)],
    )(scal, state, recv, weights, high, low, transition, ids)
    other = lax.ppermute(away, "tm", [(i, i ^ 1) for i in range(tm_count)])

    def exchange(sent):
        got = lax.all_to_all(sent.reshape(devices, slots, states), both, 0, 0, tiled=True)
        return got.reshape(devices * slots, states)

    def final(*refs):
        final_kernel(block, total_rows, emit_count, length, *refs)

    posterior, new_emission, loglik, counts, totals, most = call(
        final, "final", [smem, vmem, vmem, vmem], [vmem, vmem, smem, vmem, vmem, smem],
        [shape(2, frame_count, states), shape(block, states), shape(2), shape(block, states), shape(1, states),
         shape(1, dtype=jnp.int32)],
    )(scal, exchange(send), keep, other)

    def another(carried):
        turn, counts, _ = carried

        def packs(*refs):
            pack_kernel(block, *refs)

        def more(*refs):
            more_kernel(block, *refs)

        sent = call(packs, "pack", [smem, smem, vmem, vmem], vmem, shape(devices * slots, states))(
            scal, turn.reshape(1), occupancy, ids
        )
        counts = call(more, "more", [vmem, vmem], vmem, shape(block, states))(exchange(sent), counts)
        return turn + 1, counts, emit_update(counts, totals, total_rows)

    _, _, new_emission = lax.while_loop(
        lambda carried: carried[0] * rows_sent < most[0], another, (jnp.int32(1), counts, new_emission)
    )
    return (posterior, new_emission, loglik)


def solution(mesh):
    in_specs = (P("emit", "tm"), P("emit"), P(), P(), P("emit", None))
    out_specs = (P("emit", "tm", None), P(("tm", "emit"), None), P("emit"))
    return jax.shard_map(shards, mesh=mesh, in_specs=in_specs, out_specs=out_specs, check_vma=False)
```

time: 510 us -> 102 us (0.20)
  matrix products: 159 us -> 0 us
  waiting for transfers between devices: 164 us -> 33.3 us
  blocking collectives: 63.5 us -> 0 us
  Pallas kernels: 0 us -> 40.7 us
  other arithmetic: 36.2 us -> 1.42 us
  starting transfers between devices: 47.2 us -> 18.1 us
  between operations: 14.2 us -> 2.05 us
  local copies, waits for them, and re-layouts: 14.3 us -> 4.95 us
  loops' own time: 8.46 us -> 0.63 us
    dot_general x206 -> x0, matrix products: 159 us -> none  [the longest x64 104 us: product_step(): jnp.einsum('nij,jk->nik', carried, transition, precision=highest)]
    reduce_scatter x1 -> x0, waiting for transfers between devices: 120 us -> none  [shards(): lax.psum_scatter(jax.ops.segment_sum(jnp.where(inside[:, None], occ_rows,...]
    psum x2 -> x0, blocking collectives: 63.5 us -> none  [the longest x1 36.9 us: shards(): totals = lax.psum(jnp.sum(counts, axis=0), ('tm', 'emit'))]
    pallas_call x0 -> x6, Pallas kernels: none -> 40.7 us  [the longest x1 22.4 us: shards(): pl.pallas_call(product_kernel, name='product', grid=(1,), in_specs=[smem,...]
    all_gather x1 -> x0, waiting for transfers between devices: 33.7 us -> none  [shards(): block_rows = lax.all_gather(emission, 'emit', axis=0, tiled=True)]
    ppermute x14 -> x11, starting transfers between devices: 47.1 us -> 14.3 us  [the longest x1 3.46 us: shards(): recv = lax.ppermute(message, 'tm', relay_pairs(0))]
    select_n x272 -> x2, other arithmetic: 21.2 us -> 0.84 us  [the longest x1 0.76 us: shards(): kept = jnp.where(side == 0, observed[0:1], observed[1:2])]
    ppermute x14 -> x11, waiting for transfers between devices: 8.89 us -> 24.5 us  [the longest x2 9.17 us: shards(): recv = lax.ppermute(message, 'tm', relay_pairs(turn))]
  transfers between devices with their start and end apart: 16 -> 12, of which waited for: 9 -> 9; matrix products, arithmetic and copies ran while one was open for 2% -> 1% of each run, Pallas kernels for 0% -> 0%
where the time goes in v1:
time: 102 us; the launch traced here: 101 us
  Pallas kernels  40.7 us (40%)
  waiting for transfers between devices  33.3 us (33%)
  starting transfers between devices  18.1 us (18%)
  local copies, waits for them, and re-layouts  4.95 us (5%)
  between operations  2.05 us (2%)
  other arithmetic  1.42 us (1%)
    pallas_call x1, Pallas kernels, shards(): pl.pallas_call(product_kernel, name='product', grid=(1,), in_specs=[smem,...  22.4 us
    ppermute x2, waiting for transfers between devices, shards(): recv = lax.ppermute(message, 'tm', relay_pairs(turn))  9.17 us
    pallas_call x1, Pallas kernels, shards(): call(chain, 'chain', [smem] + [vmem] * 7, [vmem] * 4, [shape(frame_count,...  9.12 us
    all_to_all x1, waiting for transfers between devices, exchange(): lax.all_to_all(sent.reshape(devices, slots, states), both, 0, 0, tiled=True)  8.8 us
    ppermute x1, waiting for transfers between devices, shards(): other = lax.ppermute(away, 'tm', [(i, i ^ 1) for i in range(tm_count)])  4.97 us
    ppermute x3, waiting for transfers between devices, shards(): lax.ppermute(rows[k], 'emit', swaps(k))  4.26 us
    pallas_call x2, Pallas kernels, shards(): pl.pallas_call(relay, name='relay', grid=(1,), in_specs=[smem, line, line...  3.86 us
    all_to_all x1, starting transfers between devices, exchange(): lax.all_to_all(sent.reshape(devices, slots, states), both, 0, 0, tiled=True)  3.85 us
  transfers between devices with their start and end apart: 12, of which 9 were waited for; matrix products, arithmetic and copies ran while one was open for 1% of the time, Pallas kernels for 0%

profile of v1, /device:TPU:0, one launch (start us, length us, event | category | flops | bytes accessed | tf_op | source)
XLA Modules:
  0.0 101.1 jit_solution(11480637389209074746)
XLA Ops:
  0.7 0.8 broadcast_select_fusion.1
  1.4 3.0 %collective-permute-start = (s32[1,64]{1,0:T(1,128)S(1)}, s32[1,64]{1,0:T(1,128)S(1)}, u32[]{:S(2)}, u32[]{:S(2)}) collective-permute-start(s32[1,64]{1,0:T(1,128)S(1)} %get-tuple-element.104), channel_id=1, source_target_pairs={{0,4},{4,0},{8,12},{12,8},{16,20},{20,16},{24,28},{28,24},{1,5},{5... | collective-permute-start | bytes 776 | tf_op jit(solution)/shard_map/ppermute | solution.py:378
  4.4 1.5 %collective-permute-done = s32[1,64]{1,0:T(1,128)S(1)} collective-permute-done((s32[1,64]{1,0:T(1,128)S(1)}, s32[1,64]{1,0:T(1,128)S(1)}, u32[]{:S(2)}, u32[]{:S(2)}) %collective-permute-start) | collective-permute-done | bytes 288 | tf_op jit(solution)/shard_map/ppermute | solution.py:378
  6.1 2.1 %collective-permute-start.2 = (s32[1,128]{1,0:T(1,128)S(1)}, s32[1,128]{1,0:T(1,128)S(1)}, u32[]{:S(2)}, u32[]{:S(2)}) collective-permute-start(s32[1,128]{1,0:T(1,128)S(1)} %broadcast_select_fusion.2.refs_7_), channel_id=1, source_target_pairs={{0,2},{1,3},{2,0},{3,1},{4,6},{5,7},{6,4},{7,5},{8,10},{9,11},{10,... | collective-permute-start | bytes 1544 | tf_op jit(solution)/shard_map/ppermute | solution.py:387
  8.2 1.5 %collective-permute-done.2 = s32[1,128]{1,0:T(1,128)S(1)} collective-permute-done((s32[1,128]{1,0:T(1,128)S(1)}, s32[1,128]{1,0:T(1,128)S(1)}, u32[]{:S(2)}, u32[]{:S(2)}) %collective-permute-start.2) | collective-permute-done | bytes 544 | tf_op jit(solution)/shard_map/ppermute | solution.py:387
  9.7 1.4 %collective-permute-done.3 = s32[1,128]{1,0:T(1,128)S(1)} collective-permute-done((s32[1,128]{1,0:T(1,128)S(1)}, s32[1,128]{1,0:T(1,128)S(1)}, u32[]{:S(2)}, u32[]{:S(2)}) %collective-permute-start.3) | collective-permute-done | bytes 544 | tf_op jit(solution)/shard_map/ppermute | solution.py:387
  11.1 0.6 add_subtract_fusion.ids_ref
  11.7 3.2 %gather.1.own_ref = f32[4,128,256]{2,1,0:T(8,128)} custom-call(s32[4,128]{1,0:T(4,128)} %add_subtract_fusion.ids_ref, f32[1024,256]{1,0:T(8,128)} %table_ref.1), custom_call_target="tpu_custom_call" | custom-call | tf_op jit(solution)/shard_map/gather/pallas_call | solution.py:389
  14.9 1.1 %slice_bitcast_fusion = (f32[128,256]{1,0:T(8,128)S(1)}, f32[128,256]{1,0:T(8,128)S(1)}, f32[128,256]{1,0:T(8,128)S(1)}) fusion(f32[4,128,256]{2,1,0:T(8,128)} %gather.1.own_ref), kind=kLoop, calls=%fused_computation.2 | loop fusion | bytes 786432 | tf_op jit(solution)/shard_map/squeeze | solution.py:390
  16.7 1.2 %collective-permute-start.6 = (f32[128,256]{1,0:T(8,128)S(1)}, f32[128,256]{1,0:T(8,128)S(1)}, u32[]{:S(2)}, u32[]{:S(2)}) collective-permute-start(f32[128,256]{1,0:T(8,128)S(1)} %get-tuple-element.100), channel_id=1, source_target_pairs={{0,3},{1,2},{2,1},{3,0},{4,7},{5,6},{6,5},{7,4},{8,11},{9,10},{10,... | collective-permute-start | bytes 393224 | tf_op jit(solution)/shard_map/ppermute | solution.py:390
  19.9 2.7 %collective-permute-done.5.refs_1_ = f32[128,256]{1,0:T(8,128)S(1)} collective-permute-done((f32[128,256]{1,0:T(8,128)S(1)}, f32[128,256]{1,0:T(8,128)S(1)}, u32[]{:S(2)}, u32[]{:S(2)}) %collective-permute-start.5) | collective-permute-done | bytes 131104 | tf_op jit(solution)/shard_map/ppermute | solution.py:390
  22.5 1.6 %collective-permute-done.6.refs_2_ = f32[128,256]{1,0:T(8,128)S(1)} collective-permute-done((f32[128,256]{1,0:T(8,128)S(1)}, f32[128,256]{1,0:T(8,128)S(1)}, u32[]{:S(2)}, u32[]{:S(2)}) %collective-permute-start.6) | collective-permute-done | bytes 131104 | tf_op jit(solution)/shard_map/ppermute | solution.py:390
  24.1 0.6 copy-done.4
  24.8 22.4 %product.1 = (f32[128,256]{1,0:T(8,128)}, bf16[15,256,256]{2,1,0:T(8,128)(2,1)}, bf16[15,256,256]{2,1,0:T(8,128)(2,1)}, f32[8,256]{1,0:T(8,128)}, f32[8,256]{1,0:T(8,128)}) custom-call(s32[7]{0:T(128)S(1)} %stack.23.scal_ref.refs_0_, f32[4,128,256]{2,1,0:T(8,128)} %gather.1.own_ref, f32[128,256]{1,0:T(8,128)} %copy-done.2, f32[128,256]{1,0:T(8,128)} %copy-done.3, ...), custom_call_target="tpu_custom_call" | custom-call | tf_op jit(solution)/shard_map/product/pallas_call | solution.py:392
  47.1 3.5 %collective-permute-start.7 = (f32[8,256]{1,0:T(8,128)}, f32[8,256]{1,0:T(8,128)S(1)}, u32[]{:S(2)}, u32[]{:S(2)}) collective-permute-start(f32[8,256]{1,0:T(8,128)} %get-tuple-element.65), channel_id=1, source_target_pairs={{0,8},{24,16},{4,12},{28,20},{1,9},{25,17},{5,13},{29,21},{2,10},{... | collective-permute-start | bytes 24584 | tf_op jit(solution)/shard_map/ppermute | solution.py:412
  50.6 1.6 %collective-permute-done.7.refs_2_ = f32[8,256]{1,0:T(8,128)S(1)} collective-permute-done((f32[8,256]{1,0:T(8,128)}, f32[8,256]{1,0:T(8,128)S(1)}, u32[]{:S(2)}, u32[]{:S(2)}) %collective-permute-start.7) | collective-permute-done | bytes 8224 | tf_op jit(solution)/shard_map/ppermute | solution.py:412
  52.1 0.6 copy-done.8
  52.7 1.9 %relay.2 = (f32[8,256]{1,0:T(8,128)}, f32[8,256]{1,0:T(8,128)}) custom-call(s32[7]{0:T(128)S(1)} %stack.23.scal_ref.refs_0_, f32[8,256]{1,0:T(8,128)} %get-tuple-element.64.refs_1_, f32[8,256]{1,0:T(8,128)} %copy-done.8, bf16[15,256,256]{2,1,0:T(8,128)(2,1)} %get-tuple-element.66.refs_3_.refs_4_, bf16[15,256,256]{2,1,0:T(8,128)(2,1)} %get-tuple-element.67.refs_4_.refs_5_), custom_call_target="tpu_custom_call" | custom-call | tf_op jit(solution)/shard_map/relay/pallas_call | solution.py:417
  54.7 0.6 collective-permute-start.8
  55.3 0.6 copy-done.7
  55.9 1.9 %relay.3 = (f32[8,256]{1,0:T(8,128)}, f32[8,256]{1,0:T(8,128)}) custom-call(s32[7]{0:T(128)S(1)} %stack.23.scal_ref.refs_0_, f32[8,256]{1,0:T(8,128)} %get-tuple-element.68.refs_1_, f32[8,256]{1,0:T(8,128)} %copy-done.7, bf16[15,256,256]{2,1,0:T(8,128)(2,1)} %get-tuple-element.66.refs_3_.refs_4_, bf16[15,256,256]{2,1,0:T(8,128)(2,1)} %get-tuple-element.67.refs_4_.refs_5_), custom_call_target="tpu_custom_call" | custom-call | tf_op jit(solution)/shard_map/relay/pallas_call | solution.py:417
  57.9 1.3 %collective-permute-start.9 = (f32[8,256]{1,0:T(8,128)}, f32[8,256]{1,0:T(8,128)S(1)}, u32[]{:S(2)}, u32[]{:S(2)}) collective-permute-start(f32[8,256]{1,0:T(8,128)} %get-tuple-element.71), channel_id=1, source_target_pairs={{16,24},{8,0},{20,28},{12,4},{17,25},{9,1},{21,29},{13,5},{18,26},... | collective-permute-start | bytes 24584 | tf_op jit(solution)/shard_map/ppermute | solution.py:421
  59.2 9.2 %collective-permute-done.9.refs_2_ = f32[8,256]{1,0:T(8,128)S(1)} collective-permute-done((f32[8,256]{1,0:T(8,128)}, f32[8,256]{1,0:T(8,128)S(1)}, u32[]{:S(2)}, u32[]{:S(2)}) %collective-permute-start.9) | collective-permute-done | bytes 8224 | tf_op jit(solution)/shard_map/ppermute | solution.py:421
  68.3 0.6 copy-done.6
  68.9 9.1 %chain.1 = (f32[64,256]{1,0:T(8,128)}, f32[64,256]{1,0:T(8,128)}, f32[128,256]{1,0:T(8,128)S(1)}, f32[512,256]{1,0:T(8,128)}) custom-call(s32[7]{0:T(128)S(1)} %stack.23.scal_ref.refs_0_, f32[8,256]{1,0:T(8,128)} %get-tuple-element.70.refs_1_, f32[8,256]{1,0:T(8,128)} %copy-done.6, f32[128,256]{1,0:T(8,128)} %get-tuple-element.72.refs_3_, ...), custom_call_target="tpu_custom_call" | custom-call | tf_op jit(solution)/shard_map/chain/pallas_call | solution.py:426
  78.0 3.9 %all-to-all-start.1 = ((f32[32,16,256]{2,1,0:T(8,128)}), f32[32,16,256]{2,1,0:T(8,128)S(1)}, u32[]{:S(2)}, u32[]{:S(2)}) async-start(f32[32,16,256]{2,1,0:T(8,128)} %bitcast.33), calls=%async_computation.1 | async-start | bytes 1048576 | tf_op jit(solution)/shard_map/all_to_all | solution.py:435
  81.9 1.8 %collective-permute-start.10 = (f32[64,256]{1,0:T(8,128)}, f32[64,256]{1,0:T(8,128)S(1)}, u32[]{:S(2)}, u32[]{:S(2)}) collective-permute-start(f32[64,256]{1,0:T(8,128)} %get-tuple-element.75), channel_id=1, source_target_pairs={{0,4},{4,0},{8,12},{12,8},{16,20},{20,16},{24,28},{28,24},{1,5},{5... | collective-permute-start | bytes 196616 | tf_op jit(solution)/shard_map/ppermute | solution.py:432
  83.7 5.0 %collective-permute-done.10.refs_3_ = f32[64,256]{1,0:T(8,128)S(1)} collective-permute-done((f32[64,256]{1,0:T(8,128)}, f32[64,256]{1,0:T(8,128)S(1)}, u32[]{:S(2)}, u32[]{:S(2)}) %collective-permute-start.10) | collective-permute-done | bytes 65568 | tf_op jit(solution)/shard_map/ppermute | solution.py:432
  88.7 8.8 %all-to-all-done.1 = f32[32,16,256]{2,1,0:T(8,128)S(1)} async-done(((f32[32,16,256]{2,1,0:T(8,128)}), f32[32,16,256]{2,1,0:T(8,128)S(1)}, u32[]{:S(2)}, u32[]{:S(2)}) %all-to-all-start.1) | async-done | bytes 524320 | tf_op jit(solution)/shard_map/all_to_all | solution.py:435
  97.5 0.8 copy-done.1
  98.3 2.1 %final.1 = (f32[2,64,256]{2,1,0:T(8,128)}, f32[128,256]{1,0:T(8,128)}, f32[2]{0:T(128)}, f32[128,256]{1,0:T(8,128)S(1)}, f32[1,256]{1,0:T(1,128)S(1)}, /*index=5*/s32[1]{0:T(128)}) custom-call(s32[7]{0:T(128)S(1)} %stack.23.scal_ref.refs_0_, f32[512,256]{1,0:T(8,128)} %bitcast.32, f32[64,256]{1,0:T(8,128)} %get-tuple-element.74.refs_2_, f32[64,256]{1,0:T(8,128)} %copy-done.5), custom_call_target="tpu_custom_call" | custom-call | tf_op jit(solution)/shard_map/final/pallas_call | solution.py:441
  100.5 0.6 while.12
  (23 shorter events, 1.5 us)
Async XLA Ops:
  0.6 17.2 %copy-start.9 = (s32[2]{0:T(128)S(1)}, s32[2]{0:T(128)}, u32[]{:S(2)}) copy-start(s32[2]{0:T(128)} %param.8) | copy-start | bytes 28
  1.4 4.5 %collective-permute-start = (s32[1,64]{1,0:T(1,128)S(1)}, s32[1,64]{1,0:T(1,128)S(1)}, u32[]{:S(2)}, u32[]{:S(2)}) collective-permute-start(s32[1,64]{1,0:T(1,128)S(1)} %get-tuple-element.104), channel_id=1, source_target_pairs={{0,4},{4,0},{8,12},{12,8},{16,20},{20,16},{24,28},{28,24},{1,5},{5... | collective-permute-start | bytes 776 | tf_op jit(solution)/shard_map/ppermute | solution.py:378
  6.0 2.1 %collective-permute-start.1 = (s32[1,128]{1,0:T(1,128)S(1)}, s32[1,128]{1,0:T(1,128)S(1)}, u32[]{:S(2)}, u32[]{:S(2)}) collective-permute-start(s32[1,128]{1,0:T(1,128)S(1)} %broadcast_select_fusion.2.refs_7_), channel_id=1, source_target_pairs={{0,1},{1,0},{2,3},{3,2},{4,5},{5,4},{6,7},{7,6},{8,9},{9,8},{10,11... | collective-permute-start | bytes 1544 | tf_op jit(solution)/shard_map/ppermute | solution.py:387
  6.1 3.6 %collective-permute-start.2 = (s32[1,128]{1,0:T(1,128)S(1)}, s32[1,128]{1,0:T(1,128)S(1)}, u32[]{:S(2)}, u32[]{:S(2)}) collective-permute-start(s32[1,128]{1,0:T(1,128)S(1)} %broadcast_select_fusion.2.refs_7_), channel_id=1, source_target_pairs={{0,2},{1,3},{2,0},{3,1},{4,6},{5,7},{6,4},{7,5},{8,10},{9,11},{10,... | collective-permute-start | bytes 1544 | tf_op jit(solution)/shard_map/ppermute | solution.py:387
  8.1 3.0 %collective-permute-start.3 = (s32[1,128]{1,0:T(1,128)S(1)}, s32[1,128]{1,0:T(1,128)S(1)}, u32[]{:S(2)}, u32[]{:S(2)}) collective-permute-start(s32[1,128]{1,0:T(1,128)S(1)} %broadcast_select_fusion.2.refs_7_), channel_id=1, source_target_pairs={{0,3},{1,2},{2,1},{3,0},{4,7},{5,6},{6,5},{7,4},{8,11},{9,10},{10,... | collective-permute-start | bytes 1544 | tf_op jit(solution)/shard_map/ppermute | solution.py:387
  15.9 3.9 %collective-permute-start.4 = (f32[128,256]{1,0:T(8,128)S(1)}, f32[128,256]{1,0:T(8,128)S(1)}, u32[]{:S(2)}, u32[]{:S(2)}) collective-permute-start(f32[128,256]{1,0:T(8,128)S(1)} %get-tuple-element.102), channel_id=1, source_target_pairs={{0,1},{1,0},{2,3},{3,2},{4,5},{5,4},{6,7},{7,6},{8,9},{9,8},{10,11... | collective-permute-start | bytes 393224 | tf_op jit(solution)/shard_map/ppermute | solution.py:390
  16.2 6.4 %collective-permute-start.5 = (f32[128,256]{1,0:T(8,128)S(1)}, f32[128,256]{1,0:T(8,128)S(1)}, u32[]{:S(2)}, u32[]{:S(2)}) collective-permute-start(f32[128,256]{1,0:T(8,128)S(1)} %get-tuple-element.101), channel_id=1, source_target_pairs={{0,2},{1,3},{2,0},{3,1},{4,6},{5,7},{6,4},{7,5},{8,10},{9,11},{10,... | collective-permute-start | bytes 393224 | tf_op jit(solution)/shard_map/ppermute | solution.py:390
  16.7 7.5 %collective-permute-start.6 = (f32[128,256]{1,0:T(8,128)S(1)}, f32[128,256]{1,0:T(8,128)S(1)}, u32[]{:S(2)}, u32[]{:S(2)}) collective-permute-start(f32[128,256]{1,0:T(8,128)S(1)} %get-tuple-element.100), channel_id=1, source_target_pairs={{0,3},{1,2},{2,1},{3,0},{4,7},{5,6},{6,5},{7,4},{8,11},{9,10},{10,... | collective-permute-start | bytes 393224 | tf_op jit(solution)/shard_map/ppermute | solution.py:390
  19.9 4.3 %copy-start.2 = (f32[128,256]{1,0:T(8,128)}, f32[128,256]{1,0:T(8,128)S(1)}, u32[]{:S(2)}) copy-start(f32[128,256]{1,0:T(8,128)S(1)} %collective-permute-done.4.refs_0_) | copy-start | bytes 393220
  22.5 1.6 %copy-start.3 = (f32[128,256]{1,0:T(8,128)}, f32[128,256]{1,0:T(8,128)S(1)}, u32[]{:S(2)}) copy-start(f32[128,256]{1,0:T(8,128)S(1)} %collective-permute-done.5.refs_1_) | copy-start | bytes 393220
  24.1 0.6 copy-start.4
  47.1 5.0 %collective-permute-start.7 = (f32[8,256]{1,0:T(8,128)}, f32[8,256]{1,0:T(8,128)S(1)}, u32[]{:S(2)}, u32[]{:S(2)}) collective-permute-start(f32[8,256]{1,0:T(8,128)} %get-tuple-element.65), channel_id=1, source_target_pairs={{0,8},{24,16},{4,12},{28,20},{1,9},{25,17},{5,13},{29,21},{2,10},{... | collective-permute-start | bytes 24584 | tf_op jit(solution)/shard_map/ppermute | solution.py:412
  52.1 0.6 copy-start.8
  54.7 0.7 collective-permute-start.8
  55.3 0.6 copy-start.7
  57.9 10.5 %collective-permute-start.9 = (f32[8,256]{1,0:T(8,128)}, f32[8,256]{1,0:T(8,128)S(1)}, u32[]{:S(2)}, u32[]{:S(2)}) collective-permute-start(f32[8,256]{1,0:T(8,128)} %get-tuple-element.71), channel_id=1, source_target_pairs={{16,24},{8,0},{20,28},{12,4},{17,25},{9,1},{21,29},{13,5},{18,26},... | collective-permute-start | bytes 24584 | tf_op jit(solution)/shard_map/ppermute | solution.py:421
  68.3 0.6 copy-start.6
  78.0 19.5 %all-to-all-start.1 = ((f32[32,16,256]{2,1,0:T(8,128)}), f32[32,16,256]{2,1,0:T(8,128)S(1)}, u32[]{:S(2)}, u32[]{:S(2)}) async-start(f32[32,16,256]{2,1,0:T(8,128)} %bitcast.33), calls=%async_computation.1 | async-start | bytes 1048576 | tf_op jit(solution)/shard_map/all_to_all | solution.py:435
  81.9 6.8 %collective-permute-start.10 = (f32[64,256]{1,0:T(8,128)}, f32[64,256]{1,0:T(8,128)S(1)}, u32[]{:S(2)}, u32[]{:S(2)}) collective-permute-start(f32[64,256]{1,0:T(8,128)} %get-tuple-element.75), channel_id=1, source_target_pairs={{0,4},{4,0},{8,12},{12,8},{16,20},{20,16},{24,28},{28,24},{1,5},{5... | collective-permute-start | bytes 196616 | tf_op jit(solution)/shard_map/ppermute | solution.py:432
  88.7 8.8 %copy-start.5 = (f32[64,256]{1,0:T(8,128)}, f32[64,256]{1,0:T(8,128)S(1)}, u32[]{:S(2)}) copy-start(f32[64,256]{1,0:T(8,128)S(1)} %collective-permute-done.10.refs_3_) | copy-start | bytes 196612
  97.5 0.8 copy-start.1

commit v2 on v1

--- a/solution.py
+++ b/solution.py
@@ -11,6 +11,7 @@
 chunks = 8
 slots = 16
 rows_sent = 14
+granted = 24 << 20
 
 
 def split2(x):
@@ -79,85 +80,110 @@
     return x / jnp.sum(x, axis=1, keepdims=True)
 
 
-def gather_kernel(ids_ref, table_ref, out_ref):
+def diagonal(x):
+    return jnp.sum(jnp.where(iota(x.shape, 0) == iota(x.shape, 1), x, 0.0), axis=0, keepdims=True)
+
+
+def prepare_kernel(table_ref, trans_ref, table1_ref, table2_ref, table3_ref, trans1_ref, trans2_ref, trans3_ref,
+                   exact_ref, sums_ref):
+    table1_ref[...], table2_ref[...], table3_ref[...] = split3(table_ref[...])
+    trans = trans_ref[...]
+    t1, t2, t3 = split3(trans)
+    trans1_ref[...], trans2_ref[...], trans3_ref[...] = t1, t2, t3
+    exact_ref[...] = diagonal(trans) / diagonal(t1.astype(f32) + t2.astype(f32))
+    sums_ref[...] = jnp.sum(trans, axis=0, keepdims=True)
+
+
+def gather_kernel(ids_ref, high_ref, mid_ref, low_ref, mine_ref, other_ref):
     groups, frames = ids_ref.shape
-    rows, states = table_ref.shape
-    high, mid, low = split3(table_ref[...])
+    rows = high_ref.shape[0]
     eye = iota((frames, frames), 0) == iota((frames, frames), 1)
     lanes = iota((frames, rows), 1)
     for k in range(groups):
         wide = jnp.where(eye, jnp.broadcast_to(ids_ref[k : k + 1, :], (frames, frames)), 0)
         column = jnp.sum(wide, axis=1, keepdims=True)
         pick = jnp.where(column == lanes, 1.0, 0.0).astype(bf16)
-        out_ref[k] = dot(pick, high) + (dot(pick, mid) + dot(pick, low))
-
-
-def product_kernel(scal_ref, own_ref, *refs):
-    count = len(refs) - 8
-    recv_refs = refs[:count]
-    trans_ref, init_ref, w_ref, high_ref, low_ref, state_ref, msg_ref, x_ref = refs[count:]
+        taken = dot(pick, high_ref[...]) + (dot(pick, mid_ref[...]) + dot(pick, low_ref[...]))
+        (other_ref if k % 2 else mine_ref)[k // 2] = taken
+
+
+def product_kernel(scal_ref, own_ref, recv_ref, trans_ref, trans1_ref, trans2_ref, trans3_ref, exact_ref, sums_ref,
+                   init_ref, w_ref, lead_ref, high_ref, low_ref, state_ref, msg_ref, scaled_ref, column_ref):
     frames, states = w_ref.shape
     steps = frames // chunks
     first = scal_ref[0]
-    w = own_ref[0]
-    for r in recv_refs:
-        w = w + r[...]
-    w_ref[...] = w
-    trans = trans_ref[...]
-    t1, t2 = split2(trans)
-    eye = jnp.where(iota((states, states), 0) == iota((states, states), 1), 1.0, 0.0)
+    w_ref[...] = own_ref[...] + recv_ref[...]
+    cat = jnp.concatenate([trans1_ref[...], trans2_ref[...], trans3_ref[...]], axis=0)
+    lead_ref[...] = times_col(w_ref[...], cat, states, 3)
+
+    def store(c, y, columns):
+        column_ref[c : c + 1, :] = columns
+        high_ref[c], low_ref[c] = split2(y)
+
+    def reset(c):
+        eye = iota((states, states), 0) == iota((states, states), 1)
+        high_ref[c] = jnp.where(eye, 1.0, 0.0).astype(bf16)
+        low_ref[c] = jnp.zeros((states, states), bf16)
+        column_ref[pl.ds(c, 1), :] = jnp.ones((1, states), f32)
+
+    for c in range(chunks):
+        row = w_ref[c * steps : c * steps + 1, :]
+        row = row / jnp.sum(sums_ref[...] * row, axis=1, keepdims=True)
+        store(c, trans_ref[...] * row, sums_ref[...] * row)
+    start_chunk = lax.div(first, steps)
+    start_step = lax.rem(first, steps)
+
+    def step(k, carried):
+        @pl.when((start_step == k) & (first >= 0) & (first < frames))
+        def _():
+            reset(start_chunk)
+
+        for c in range(chunks):
+            frame = c * steps + k
+            total = jnp.sum(lead_ref[pl.ds(frame, 1), :] * column_ref[c : c + 1, :], axis=1, keepdims=True)
+            scaled_ref[c : c + 1, :] = w_ref[pl.ds(frame, 1), :] * exact_ref[...] / total
+        for c in range(chunks):
+            x1, x2 = high_ref[c], low_ref[c]
+            y = dot(x1, trans1_ref[...]) + (dot(x1, trans2_ref[...]) + dot(x2, trans1_ref[...]))
+            y = y * scaled_ref[c : c + 1, :]
+            store(c, y, jnp.sum(y, axis=0, keepdims=True))
+        return carried
+
+    lax.fori_loop(1, steps, step, 0)
+    for c in range(chunks):
+
+        @pl.when((c + 1) * steps <= first)
+        def _():
+            reset(c)
 
     def inverse_sum(x):
         return 1.0 / jnp.sum(jnp.sum(x, axis=0, keepdims=True), axis=1, keepdims=True)
 
-    scales = []
-    for c in range(chunks):
-        x = jnp.where(c * steps >= first, trans * w_ref[c * steps : c * steps + 1, :], eye)
-        x_ref[c] = x
-        scales.append(inverse_sum(x))
-
-    def step(k, scales):
-        after = []
-        for c in range(chunks):
-            x = x_ref[c] * scales[c]
-            x1, x2 = split2(x)
-            y = dot(x1, t1) + (dot(x1, t2) + dot(x2, t1))
-            y = y * w_ref[pl.ds(c * steps + k, 1), :]
-            y = jnp.where(c * steps + k >= first, y, x)
-            x_ref[c] = y
-            after.append(inverse_sum(y))
-        return tuple(after)
-
-    scales = lax.fori_loop(1, steps, step, tuple(scales))
-    at = 0
-    level = []
-    for c in range(chunks):
-        x1, x2 = split2(x_ref[c] * scales[c])
-        high_ref[at] = x1
-        low_ref[at] = x2
-        level.append(at)
-        at += 1
+    at = chunks
+    level = list(range(chunks))
     while len(level) > 1:
-        upper = []
+        above = []
         for i in range(0, len(level), 2):
             a1, a2 = high_ref[level[i]], low_ref[level[i]]
             b1, b2 = high_ref[level[i + 1]], low_ref[level[i + 1]]
             y = dot(a1, b1) + (dot(a1, b2) + dot(a2, b1))
-            y1, y2 = split2(y * inverse_sum(y))
-            high_ref[at] = y1
-            low_ref[at] = y2
-            upper.append(at)
+            high_ref[at], low_ref[at] = split2(y * inverse_sum(y))
+            above.append(at)
             at += 1
-        level = upper
+        level = above
     init = init_ref[...]
     prior = jnp.broadcast_to(init / jnp.sum(init, axis=1, keepdims=True), (8, states))
     final = jnp.full((8, states), 1.0 / states, f32)
-    root1, root2 = high_ref[level[0]], low_ref[level[0]]
-    ahead = row_times(prior, jnp.concatenate([root1, root2], axis=1), states, 2)
-    behind = times_col(final, jnp.concatenate([root1, root2], axis=0), states, 2)
-    top = iota((8, states), 0) == 0
-    state_ref[...] = jnp.where(top, prior, final)
-    msg_ref[...] = jnp.where(top, normalize(ahead), normalize(behind))
+    state_ref[...] = jnp.where(iota((8, states), 0) == 0, prior, final)
+    carry_over(prior, final, high_ref, low_ref, msg_ref)
+
+
+def carry_over(fore, back, high_ref, low_ref, msg_ref):
+    states = fore.shape[1]
+    root1, root2 = high_ref[2 * chunks - 2], low_ref[2 * chunks - 2]
+    ahead = row_times(fore, jnp.concatenate([root1, root2], axis=1), states, 2)
+    behind = times_col(back, jnp.concatenate([root1, root2], axis=0), states, 2)
+    msg_ref[...] = jnp.where(iota((8, states), 0) == 0, normalize(ahead), normalize(behind))
 
 
 def merge_state(state, recv, part, parts, turn):
@@ -167,13 +193,9 @@
 
 
 def relay_kernel(parts, turn, scal_ref, state_ref, recv_ref, high_ref, low_ref, out_ref, msg_ref):
-    states = state_ref.shape[1]
     state = merge_state(state_ref[...], recv_ref[...], scal_ref[1], parts, turn - 1)
     out_ref[...] = state
-    root1, root2 = high_ref[0], low_ref[0]
-    ahead = row_times(state, jnp.concatenate([root1, root2], axis=1), states, 2)
-    behind = times_col(state, jnp.concatenate([root1, root2], axis=0), states, 2)
-    msg_ref[...] = jnp.where(iota((8, states), 0) == 0, normalize(ahead), normalize(behind))
+    carry_over(state, state, high_ref, low_ref, msg_ref)
 
 
 def place(ids_ref, scal_ref, block, turn):
@@ -199,30 +221,37 @@
     return owner_row[0:1, :], rank_row, fits_row, rank_column, fits_column, local, most
 
 
-def pack(ids_ref, scal_ref, occupancy, send_ref, block, turn, log_sum):
-    frames, states = occupancy.shape
-    devices = send_ref.shape[0] // slots
+def address_kernel(block, scal_ref, turn_ref, ids_ref, pick_ref, meta_ref):
+    frames = ids_ref.shape[1]
+    lines, states = meta_ref.shape
+    turn = turn_ref[0]
     owner, rank, fits, rank_column, fits_column, local, most = place(ids_ref, scal_ref, block, turn)
     spot = jnp.where(fits, owner * slots + rank, -1)
-    lines = iota((devices * slots, frames), 0)
-    pick = lines == spot
-    totals = (lax.bitwise_and(lines, slots - 1) == rows_sent) & (turn == 0)
-    pick = jnp.where(pick | totals, 1.0, 0.0).astype(bf16)
-    high, mid, low = split3(occupancy)
+    across = iota((lines, frames), 0)
+    totals = (lax.bitwise_and(across, slots - 1) == rows_sent) & (turn == 0)
+    pick_ref[...] = jnp.where((across == spot) | totals, 1.0, 0.0).astype(bf16)
     base = scal_ref[2]
     lanes = iota((frames, states), 1)
     ranked = jnp.where(fits_column & (lanes == base + rank_column), (local + 1).astype(f32), 0.0).astype(bf16)
-    mine = jnp.where((lines == owner * slots + slots - 1) & fits, 1.0, 0.0).astype(bf16)
-    sent = dot(pick, high) + (dot(pick, mid) + (dot(pick, low) + dot(mine, ranked)))
-    lines = lax.bitwise_and(iota((devices * slots, 1), 0), slots - 1) == slots - 1
+    mine = jnp.where((across == owner * slots + slots - 1) & fits, 1.0, 0.0).astype(bf16)
+    last = lax.bitwise_and(iota((lines, 1), 0), slots - 1) == slots - 1
     lanes = iota((1, states), 1)
-    sent = jnp.where(lines & (lanes == base + rows_sent), log_sum, sent)
-    send_ref[...] = jnp.where(lines & (lanes == base + rows_sent + 1), most.astype(f32), sent)
-
-
-def chain_kernel(parts, block, scal_ref, state_ref, recv_ref, w_ref, high_ref, low_ref, trans_ref, ids_ref,
-                 keep_ref, away_ref, occ_ref, send_ref, split_ref, fore_ref, back_ref,
-                 start_ref, end_ref, post_ref):
+    meta_ref[...] = jnp.where(last & (lanes == base + rows_sent + 1), most.astype(f32), dot(mine, ranked))
+
+
+def pack(pick_ref, meta_ref, occupancy, send_ref, base, log_sum):
+    high, mid, low = split3(occupancy)
+    pick = pick_ref[...]
+    lines, states = meta_ref.shape
+    last = lax.bitwise_and(iota((lines, 1), 0), slots - 1) == slots - 1
+    meta = jnp.where(last & (iota((1, states), 1) == base + rows_sent), log_sum, meta_ref[...])
+    send_ref[...] = dot(pick, high) + (dot(pick, mid) + (dot(pick, low) + meta))
+
+
+def chain_kernel(parts, scal_ref, state_ref, recv_ref, w_ref, lead_ref, high_ref, low_ref, trans1_ref,
+                 trans2_ref, exact_ref, sums_ref, pick_ref, meta_ref,
+                 keep_ref, away_ref, occ_ref, send_ref, split_ref, leads_ref, fore_ref,
+                 back_ref, start_ref, end_ref, post_ref):
     frames, states = w_ref.shape
     steps = frames // chunks
     first = scal_ref[0]
@@ -251,26 +280,29 @@
             made = normalize(times_col(tail, cat, states, 2))
             end_ref[last - half : last - half + 1, :] = made[0:1, :]
         width = half
-    trans = trans_ref[...]
-    ahead = jnp.concatenate(split3(trans), axis=1)
-    behind = jnp.concatenate(split3(trans), axis=0)
+    ahead = jnp.concatenate([trans1_ref[...], trans2_ref[...]], axis=1)
+    behind = jnp.concatenate([trans1_ref[...], trans2_ref[...]], axis=0)
+    exact = exact_ref[...]
+    sums = sums_ref[...]
     for h in range(states // 128):
         split_ref[h] = w_ref[:, h * 128 : (h + 1) * 128]
+        leads_ref[h] = lead_ref[:, h * 128 : (h + 1) * 128]
     fore = start_ref[...]
     back = end_ref[...]
     logs = jnp.zeros((chunks, 1), f32)
     spots = iota((chunks, 1), 0) * steps
     for k in range(steps):
-        moved = row_times(fore, ahead, states, 3) * take(split_ref, k, steps)
-        scaling = jnp.sum(moved, axis=1, keepdims=True)
+        scaling = jnp.sum(fore * take(leads_ref, k, steps), axis=1, keepdims=True)
+        scaled = take(split_ref, k, steps) * (exact / scaling)
         active = spots + k >= first
-        fore = jnp.where(active, moved / scaling, fore)
+        fore = jnp.where(active, row_times(fore, ahead, states, 2) * scaled, fore)
         logs = logs + jnp.where(active, jnp.log(scaling), 0.0)
         put(fore_ref, k, steps, fore)
         j = steps - 1 - k
         put(back_ref, j, steps, back)
-        moved = times_col(back * take(split_ref, j, steps), behind, states, 3)
-        back = jnp.where(spots + j >= first, normalize(moved), back)
+        weighed = back * take(split_ref, j, steps)
+        inverse = exact / jnp.sum(weighed * sums, axis=1, keepdims=True)
+        back = jnp.where(spots + j >= first, times_col(weighed, behind, states, 2) * inverse, back)
     joint = whole(fore_ref) * whole(back_ref)
     occupancy = jnp.where(iota((frames, 1), 0) >= first, normalize(joint), 0.0)
     occ_ref[...] = occupancy
@@ -279,7 +311,7 @@
     half = frames // 2
     keep_ref[...] = post_ref[pl.ds(pl.multiple_of(side * half, half), half), :]
     away_ref[...] = post_ref[pl.ds(pl.multiple_of((1 - side) * half, half), half), :]
-    pack(ids_ref, scal_ref, occupancy, send_ref, block, 0, jnp.sum(logs))
+    pack(pick_ref, meta_ref, occupancy, send_ref, scal_ref[2], jnp.sum(logs, axis=0, keepdims=True))
 
 
 def counted(recv_ref, block):
@@ -331,8 +363,8 @@
     post_ref[1 - side] = other_ref[...]
 
 
-def pack_kernel(block, scal_ref, turn_ref, occ_ref, ids_ref, send_ref):
-    pack(ids_ref, scal_ref, occ_ref[...], send_ref, block, turn_ref[0], 0.0)
+def pack_kernel(scal_ref, pick_ref, meta_ref, occ_ref, send_ref):
+    pack(pick_ref, meta_ref, occ_ref[...], send_ref, scal_ref[2], 0.0)
 
 
 def more_kernel(block, recv_ref, counts_ref, out_ref):
@@ -344,9 +376,11 @@
 smem = pl.BlockSpec(memory_space=pltpu.MemorySpace.SMEM)
 
 
-def call(kernel, name, in_specs, out_specs, out_shape, scratch=()):
-    return pl.pallas_call(kernel, name=name, in_specs=in_specs, out_specs=out_specs, out_shape=out_shape,
-                          scratch_shapes=scratch)
+def call(kernel, name, in_specs, out_specs, out_shape, scratch=(), cost=None):
+    if cost is not None:
+        cost = pl.CostEstimate(flops=cost, bytes_accessed=cost // 100, transcendentals=0)
+    return pl.pallas_call(kernel, name=name, cost_estimate=cost, in_specs=in_specs, out_specs=out_specs, out_shape=out_shape,
+                          scratch_shapes=scratch, compiler_params=pltpu.CompilerParams(vmem_limit_bytes=granted))
 
 
 def shape(*dims, dtype=f32):
@@ -384,21 +418,36 @@
     def swaps(k):
         return [(i, i ^ k) for i in range(emit_count)]
 
-    others = [lax.ppermute(ids, "emit", swaps(k)) for k in range(1, emit_count)]
-    wanted = jnp.concatenate([ids] + others, axis=0) - emit_place * own_rows
-    rows = call(gather_kernel, "gather", [vmem, vmem], vmem, shape(emit_count, frames, states))(wanted, emission)
-    came = [lax.ppermute(rows[k], "emit", swaps(k)) for k in range(1, emit_count)]
+    narrow = shape(states, states, dtype=bf16)
+    table = shape(own_rows, states, dtype=bf16)
+    prepared = call(prepare_kernel, "prepare", [vmem] * 2, [vmem] * 8,
+                    [table] * 3 + [narrow] * 3 + [shape(1, states)] * 2, cost=400_000_000)(emission, transition)
+    tables, matrices, exact, sums = prepared[:3], prepared[3:6], prepared[6], prepared[7]
+    near = jnp.concatenate([ids, lax.ppermute(ids, "emit", swaps(1))], axis=0)
+    far = [lax.ppermute(near, "emit", swaps(k)) for k in range(2, emit_count, 2)]
+    wanted = jnp.concatenate([near] + far, axis=0) - emit_place * own_rows
+    half = shape(emit_count // 2, frames, states)
+    mine, other = call(gather_kernel, "gather", [vmem] * 4, [vmem, vmem], [half, half])(wanted, *tables)
+    both_cores = mine + lax.ppermute(other, "emit", swaps(1))
+    came = [lax.ppermute(both_cores[k // 2], "emit", swaps(k)) for k in range(2, emit_count, 2)]
+    came = sum(came[1:], came[0])
     nodes = 2 * chunks - 1
-    weights, high, low, state, message = pl.pallas_call(
-        product_kernel, name="product", grid=(1,),
-        in_specs=[smem, pl.BlockSpec((1, frames, states), lambda i: (0, 0, 0))]
-        + [pl.BlockSpec((frames, states), lambda i: (0, 0))] * (emit_count - 1)
-        + [pl.BlockSpec((states, states), lambda i: (0, 0)), pl.BlockSpec((1, states), lambda i: (0, 0))],
-        out_specs=[vmem] * 5,
-        out_shape=[shape(frames, states), shape(nodes, states, states, dtype=bf16),
-                   shape(nodes, states, states, dtype=bf16), shape(8, states), shape(8, states)],
-        scratch_shapes=[pltpu.VMEM((chunks, states, states), f32)],
-    )(scal, rows, *came, transition, initial.reshape(1, states))
+    weights, lead, high, low, state, message = call(
+        product_kernel, "product", [smem] + [vmem] * 9, [vmem] * 6,
+        [shape(frames, states), shape(frames, states), shape(nodes, states, states, dtype=bf16),
+         shape(nodes, states, states, dtype=bf16), shape(8, states), shape(8, states)],
+        [pltpu.VMEM((chunks, states), f32)] * 2,
+    )(scal, both_cores[0], came, transition, *matrices, exact, sums, initial.reshape(1, states))
+
+    def address(turn):
+        def kernel(*refs):
+            address_kernel(block, *refs)
+
+        lines = devices * slots
+        return call(kernel, "address", [smem, smem, vmem], [vmem, vmem],
+                    [shape(lines, frames, dtype=bf16), shape(lines, states)], cost=400_000_000)(scal, turn, ids)
+
+    pick, meta = address(jnp.zeros((1,), jnp.int32))
 
     def relay_pairs(turn):
         pairs = []
@@ -407,28 +456,25 @@
             pairs.append((2 * (parts - 1 - turn) + y, 2 * (parts - 2 - turn) + y))
         return pairs
 
-    root = pl.BlockSpec((1, states, states), lambda i: (nodes - 1, 0, 0))
-    line = pl.BlockSpec((8, states), lambda i: (0, 0))
     recv = lax.ppermute(message, "tm", relay_pairs(0))
     for turn in range(1, parts - 1):
         def relay(*refs, turn=turn):
             relay_kernel(parts, turn, *refs)
 
-        state, message = pl.pallas_call(
-            relay, name="relay", grid=(1,), in_specs=[smem, line, line, root, root],
-            out_specs=[vmem, vmem], out_shape=[shape(8, states), shape(8, states)],
+        state, message = call(
+            relay, "relay", [smem] + [vmem] * 4, [vmem] * 2, [shape(8, states), shape(8, states)]
         )(scal, state, recv, high, low)
         recv = lax.ppermute(message, "tm", relay_pairs(turn))
 
     def chain(*refs):
-        chain_kernel(parts, block, *refs)
+        chain_kernel(parts, *refs)
 
     keep, away, occupancy, send = call(
-        chain, "chain", [smem] + [vmem] * 7, [vmem] * 4,
+        chain, "chain", [smem] + [vmem] * 12, [vmem] * 4,
         [shape(frame_count, states), shape(frame_count, states), shape(frames, states), shape(devices * slots, states)],
-        [pltpu.VMEM((states // 128, frames, 128), f32)] * 3
+        [pltpu.VMEM((states // 128, frames, 128), f32)] * 4
         + [pltpu.VMEM((chunks, states), f32)] * 2 + [pltpu.VMEM((frames, states), f32)],
-    )(scal, state, recv, weights, high, low, transition, ids)
+    )(scal, state, recv, weights, lead, high, low, matrices[0], matrices[1], exact, sums, pick, meta)
     other = lax.ppermute(away, "tm", [(i, i ^ 1) for i in range(tm_count)])
 
     def exchange(sent):
@@ -447,14 +493,11 @@
     def another(carried):
         turn, counts, _ = carried
 
-        def packs(*refs):
-            pack_kernel(block, *refs)
-
         def more(*refs):
             more_kernel(block, *refs)
 
-        sent = call(packs, "pack", [smem, smem, vmem, vmem], vmem, shape(devices * slots, states))(
-            scal, turn.reshape(1), occupancy, ids
+        sent = call(pack_kernel, "pack", [smem] + [vmem] * 3, vmem, shape(devices * slots, states))(
+            scal, *address(turn.reshape(1)), occupancy
         )
         counts = call(more, "more", [vmem, vmem], vmem, shape(block, states))(exchange(sent), counts)
         return turn + 1, counts, emit_update(counts, totals, total_rows)

time: 102 us -> 85.3 us (0.84)
  Pallas kernels: 40.7 us -> 31 us
  waiting for transfers between devices: 33.3 us -> 29.7 us
  local copies, waits for them, and re-layouts: 4.95 us -> 2.87 us
    pallas_call x5 -> x7, Pallas kernels: 38.5 us -> 29.4 us  [the longest x1 19.9 us: shards(): call(product_kernel, 'product', [smem] + [vmem] * 9, [vmem] * 6, [shape(f...]
    ppermute x6 -> x4, waiting for transfers between devices: 7.22 us -> 5.25 us  [the longest x1 2.57 us: shards(): lax.ppermute(both_cores[k // 2], 'emit', swaps(k))]
    ppermute x2, waiting for transfers between devices: 9.17 us -> 7.78 us  [shards(): recv = lax.ppermute(message, 'tm', relay_pairs(turn))]
    squeeze x1, local copies, waits for them, and re-layouts: 1.06 us -> 0.02 us  [shards(): both_cores[k // 2]]
    unnamed x18 -> x10, local copies, waits for them, and re-layouts: 3.22 us -> 2.18 us
    ppermute x6 -> x4, starting transfers between devices: 4.03 us -> 3.12 us  [the longest x1 1.99 us: shards(): lax.ppermute(near, 'emit', swaps(k))]
  transfers between devices with their start and end apart: 12 -> 10, of which waited for: 9 -> 8; matrix products, arithmetic and copies ran while one was open for 1% -> 1% of each run, Pallas kernels for 0% -> 2%
where the time goes in v2:
time: 85.3 us; the launch traced here: 84.9 us
  Pallas kernels  31 us (36%)
  waiting for transfers between devices  29.7 us (35%)
  starting transfers between devices  17.7 us (21%)
  local copies, waits for them, and re-layouts  2.87 us (3%)
  between operations  2.08 us (2%)
  other arithmetic  0.89 us (1%)
    pallas_call x1, Pallas kernels, shards(): call(product_kernel, 'product', [smem] + [vmem] * 9, [vmem] * 6, [shape(f...  19.9 us
    all_to_all x1, waiting for transfers between devices, exchange(): lax.all_to_all(sent.reshape(devices, slots, states), both, 0, 0, tiled=True)  8.8 us
    ppermute x2, waiting for transfers between devices, shards(): recv = lax.ppermute(message, 'tm', relay_pairs(turn))  7.78 us
    pallas_call x1, Pallas kernels, shards(): call(chain, 'chain', [smem] + [vmem] * 12, [vmem] * 4, [shape(frame_count...  5.32 us
    ppermute x1, waiting for transfers between devices, shards(): other = lax.ppermute(away, 'tm', [(i, i ^ 1) for i in range(tm_count)])  4.97 us
    all_to_all x1, starting transfers between devices, exchange(): lax.all_to_all(sent.reshape(devices, slots, states), both, 0, 0, tiled=True)  4.22 us
    ppermute x1, starting transfers between devices, shards(): recv = lax.ppermute(message, 'tm', relay_pairs(0))  3.48 us
    ppermute x1, starting transfers between devices, shards(): taken = lax.ppermute(given, 'tm', [(i, i ^ 1) for i in range(tm_count)])  3 us
  transfers between devices with their start and end apart: 10, of which 8 were waited for; matrix products, arithmetic and copies ran while one was open for 1% of the time, Pallas kernels for 2%

profile of v2, /device:TPU:0, one launch (start us, length us, event | category | flops | bytes accessed | tf_op | source)
XLA Modules:
  0.0 84.9 jit_solution(16681290158357912014)
XLA Ops:
  0.6 0.8 broadcast_select_fusion.1
  1.4 3.0 %collective-permute-start = (s32[1,64]{1,0:T(1,128)S(1)}, s32[1,64]{1,0:T(1,128)S(1)}, u32[]{:S(2)}, u32[]{:S(2)}) collective-permute-start(s32[1,64]{1,0:T(1,128)S(1)} %get-tuple-element.131), channel_id=1, source_target_pairs={{0,4},{4,0},{8,12},{12,8},{16,20},{20,16},{24,28},{28,24},{1,5},{5... | collective-permute-start | bytes 776 | tf_op jit(solution)/shard_map/ppermute | solution.py:412
  4.4 1.5 %collective-permute-done = s32[1,64]{1,0:T(1,128)S(1)} collective-permute-done((s32[1,64]{1,0:T(1,128)S(1)}, s32[1,64]{1,0:T(1,128)S(1)}, u32[]{:S(2)}, u32[]{:S(2)}) %collective-permute-start) | collective-permute-done | bytes 288 | tf_op jit(solution)/shard_map/ppermute | solution.py:412
  5.9 0.1 broadcast_select_fusion.2.refs_2_
  6.0 1.1 %collective-permute-done.1 = s32[1,128]{1,0:T(1,128)S(1)} collective-permute-done((s32[1,128]{1,0:T(1,128)S(1)}, s32[1,128]{1,0:T(1,128)S(1)}, u32[]{:S(2)}, u32[]{:S(2)}) %collective-permute-start.1) | collective-permute-done | bytes 544 | tf_op jit(solution)/shard_map/ppermute | solution.py:426
  7.2 2.0 %collective-permute-start.2 = (s32[2,128]{1,0:T(2,128)S(1)}, s32[2,128]{1,0:T(2,128)S(1)}, u32[]{:S(2)}, u32[]{:S(2)}) collective-permute-start(s32[2,128]{1,0:T(2,128)S(1)} %pad_add_fusion), channel_id=1, source_target_pairs={{0,2},{1,3},{2,0},{3,1},{4,6},{5,7},{6,4},{7,5},{8,10},{9,11},{10,... | collective-permute-start | bytes 3080 | tf_op jit(solution)/shard_map/ppermute | solution.py:427
  9.2 0.9 %copy-done = f32[256,256]{1,0:T(8,128)S(1)} copy-done((f32[256,256]{1,0:T(8,128)S(1)}, f32[256,256]{1,0:T(8,128)}, u32[]{:S(2)}) %copy-start) | copy-done | bytes 262168
  10.1 1.2 %copy-done.3 = f32[1024,256]{1,0:T(8,128)S(1)} copy-done((f32[1024,256]{1,0:T(8,128)S(1)}, f32[1024,256]{1,0:T(8,128)}, u32[]{:S(2)}) %copy-start.3) | copy-done | bytes 1048600
  11.4 0.4 prepare.1
  11.8 1.1 %gather.1 = (f32[2,128,256]{2,1,0:T(8,128)S(1)}, f32[2,128,256]{2,1,0:T(8,128)S(1)}) custom-call(s32[4,128]{1,0:T(4,128)S(1)} %add_subtract_fusion.ids_ref, bf16[1024,256]{1,0:T(8,128)(2,1)S(1)} %get-tuple-element.79.high_ref, bf16[1024,256]{1,0:T(8,128)(2,1)S(1)} %get-tuple-element.80.mid_ref, bf16[1024,256]{1,0:T(8,128)(2,1)S(1)} %get-tuple-element.81.low_ref), custom_call_target="tpu_custom_call" | custom-call | tf_op jit(solution)/shard_map/gather/pallas_call | solution.py:430
  12.9 0.1 collective-permute-start.3
  13.0 1.5 %collective-permute-done.3 = f32[2,128,256]{2,1,0:T(8,128)S(1)} collective-permute-done((f32[2,128,256]{2,1,0:T(8,128)S(1)}, f32[2,128,256]{2,1,0:T(8,128)S(1)}, u32[]{:S(2)}, u32[]{:S(2)}) %collective-permute-start.3) | collective-permute-done | bytes 262176 | tf_op jit(solution)/shard_map/ppermute | solution.py:431
  14.6 1.0 %collective-permute-start.4 = (f32[128,256]{1,0:T(8,128)S(1)}, f32[128,256]{1,0:T(8,128)S(1)}, u32[]{:S(2)}, u32[]{:S(2)}) collective-permute-start(f32[128,256]{1,0:T(8,128)S(1)} %get-tuple-element.128), channel_id=1, source_target_pairs={{0,2},{1,3},{2,0},{3,1},{4,6},{5,7},{6,4},{7,5},{8,10},{9,11},{10,... | collective-permute-start | bytes 393224 | tf_op jit(solution)/shard_map/ppermute | solution.py:432
  15.6 0.6 fusion
  17.5 0.1 stack.23.scal_ref.refs_0_
  17.6 2.6 %collective-permute-done.4.recv_ref = f32[128,256]{1,0:T(8,128)S(1)} collective-permute-done((f32[128,256]{1,0:T(8,128)S(1)}, f32[128,256]{1,0:T(8,128)S(1)}, u32[]{:S(2)}, u32[]{:S(2)}) %collective-permute-start.4) | collective-permute-done | bytes 131104 | tf_op jit(solution)/shard_map/ppermute | solution.py:432
  20.2 19.9 %product.1 = (f32[128,256]{1,0:T(8,128)S(1)}, f32[128,256]{1,0:T(8,128)S(1)}, bf16[15,256,256]{2,1,0:T(8,128)(2,1)S(1)}, bf16[15,256,256]{2,1,0:T(8,128)(2,1)S(1...) custom-call(s32[7]{0:T(128)S(1)} %stack.23.scal_ref.refs_0_, f32[128,256]{1,0:T(8,128)S(1)} %get-tuple-element.129.own_ref, ...), custom_call_target="tpu_custom_call" | custom-call | tf_op jit(solution)/shard_map/product/pallas_call | solution.py:435
  40.1 3.5 %collective-permute-start.5 = (f32[8,256]{1,0:T(8,128)S(1)}, f32[8,256]{1,0:T(8,128)S(1)}, u32[]{:S(2)}, u32[]{:S(2)}) collective-permute-start(f32[8,256]{1,0:T(8,128)S(1)} %get-tuple-element.90), channel_id=1, source_target_pairs={{0,8},{24,16},{4,12},{28,20},{1,9},{25,17},{5,13},{29,21},{2,10},{... | collective-permute-start | bytes 24584 | tf_op jit(solution)/shard_map/ppermute | solution.py:459
  43.6 1.3 %collective-permute-done.5.refs_2_ = f32[8,256]{1,0:T(8,128)S(1)} collective-permute-done((f32[8,256]{1,0:T(8,128)S(1)}, f32[8,256]{1,0:T(8,128)S(1)}, u32[]{:S(2)}, u32[]{:S(2)}) %collective-permute-start.5) | collective-permute-done | bytes 8224 | tf_op jit(solution)/shard_map/ppermute | solution.py:459
  45.0 0.8 relay.2
  45.8 0.7 collective-permute-start.6
  46.5 0.8 relay.3
  47.3 1.3 %collective-permute-start.7 = (f32[8,256]{1,0:T(8,128)S(1)}, f32[8,256]{1,0:T(8,128)S(1)}, u32[]{:S(2)}, u32[]{:S(2)}) collective-permute-start(f32[8,256]{1,0:T(8,128)S(1)} %get-tuple-element.96), channel_id=1, source_target_pairs={{16,24},{8,0},{20,28},{12,4},{17,25},{9,1},{21,29},{13,5},{18,26},... | collective-permute-start | bytes 24584 | tf_op jit(solution)/shard_map/ppermute | solution.py:467
  48.7 1.0 %address.2 = (bf16[512,128]{1,0:T(8,128)(2,1)S(1)}, f32[512,256]{1,0:T(8,128)S(1)}) custom-call(s32[7]{0:T(128)S(1)} %stack.23.scal_ref.refs_0_, s32[1]{0:T(128)} %constant.62.clone.1.refs_1_, s32[1,128]{1,0:T(1,128)S(1)} %broadcast_select_fusion.2.refs_2_), custom_call_target="tpu_custom_call" | custom-call | flops 400000000 | bytes 4000000 | tf_op jit(solution)/shard_map/address/pallas_call | solution.py:447
  49.7 7.8 %collective-permute-done.7.refs_2_ = f32[8,256]{1,0:T(8,128)S(1)} collective-permute-done((f32[8,256]{1,0:T(8,128)S(1)}, f32[8,256]{1,0:T(8,128)S(1)}, u32[]{:S(2)}, u32[]{:S(2)}) %collective-permute-start.7) | collective-permute-done | bytes 8224 | tf_op jit(solution)/shard_map/ppermute | solution.py:467
  57.4 5.3 %chain.1 = (f32[64,256]{1,0:T(8,128)S(1)}, f32[64,256]{1,0:T(8,128)S(1)}, f32[128,256]{1,0:T(8,128)S(1)}, f32[512,256]{1,0:T(8,128)}) custom-call(s32[7]{0:T(128)S(1)} %stack.23.scal_ref.refs_0_, f32[8,256]{1,0:T(8,128)S(1)} %get-tuple-element.95.refs_1_, f32[8,256]{1,0:T(8,128)S(1)} %collective-permute-done.7.refs_2_, ...), custom_call_target="tpu_custom_call" | custom-call | tf_op jit(solution)/shard_map/chain/pallas_call | solution.py:472
  62.7 4.2 %all-to-all-start.1 = ((f32[32,16,256]{2,1,0:T(8,128)}), f32[32,16,256]{2,1,0:T(8,128)S(1)}, u32[]{:S(2)}, u32[]{:S(2)}) async-start(f32[32,16,256]{2,1,0:T(8,128)} %bitcast.15), calls=%async_computation.1 | async-start | bytes 1048576 | tf_op jit(solution)/shard_map/all_to_all | solution.py:481
  67.0 1.8 %collective-permute-start.8 = (f32[64,256]{1,0:T(8,128)S(1)}, f32[64,256]{1,0:T(8,128)S(1)}, u32[]{:S(2)}, u32[]{:S(2)}) collective-permute-start(f32[64,256]{1,0:T(8,128)S(1)} %get-tuple-element.103), channel_id=1, source_target_pairs={{0,4},{4,0},{8,12},{12,8},{16,20},{20,16},{24,28},{28,24},{1,5},{5... | collective-permute-start | bytes 196616 | tf_op jit(solution)/shard_map/ppermute | solution.py:478
  68.8 5.0 %collective-permute-done.8.refs_3_ = f32[64,256]{1,0:T(8,128)S(1)} collective-permute-done((f32[64,256]{1,0:T(8,128)S(1)}, f32[64,256]{1,0:T(8,128)S(1)}, u32[]{:S(2)}, u32[]{:S(2)}) %collective-permute-start.8) | collective-permute-done | bytes 65568 | tf_op jit(solution)/shard_map/ppermute | solution.py:478
  73.8 8.8 %all-to-all-done.1 = f32[32,16,256]{2,1,0:T(8,128)S(1)} async-done(((f32[32,16,256]{2,1,0:T(8,128)}), f32[32,16,256]{2,1,0:T(8,128)S(1)}, u32[]{:S(2)}, u32[]{:S(2)}) %all-to-all-start.1) | async-done | bytes 524320 | tf_op jit(solution)/shard_map/all_to_all | solution.py:481
  82.6 1.6 %final.1 = (f32[2,64,256]{2,1,0:T(8,128)}, f32[128,256]{1,0:T(8,128)}, f32[2]{0:T(128)}, f32[128,256]{1,0:T(8,128)S(1)}, f32[1,256]{1,0:T(1,128)S(1)}, /*index=5*/s32[1]{0:T(128)}) custom-call(s32[7]{0:T(128)S(1)} %stack.23.scal_ref.refs_0_, f32[512,256]{1,0:T(8,128)S(1)} %bitcast.29, f32[64,256]{1,0:T(8,128)S(1)} %get-tuple-element.102.refs_2_, ...), custom_call_target="tpu_custom_call" | custom-call | tf_op jit(solution)/shard_map/final/pallas_call | solution.py:487
  84.2 0.7 while.12
  (15 shorter events, 0.1 us)
Async XLA Ops:
  1.4 4.5 %collective-permute-start = (s32[1,64]{1,0:T(1,128)S(1)}, s32[1,64]{1,0:T(1,128)S(1)}, u32[]{:S(2)}, u32[]{:S(2)}) collective-permute-start(s32[1,64]{1,0:T(1,128)S(1)} %get-tuple-element.131), channel_id=1, source_target_pairs={{0,4},{4,0},{8,12},{12,8},{16,20},{20,16},{24,28},{28,24},{1,5},{5... | collective-permute-start | bytes 776 | tf_op jit(solution)/shard_map/ppermute | solution.py:412
  6.0 1.2 %collective-permute-start.1 = (s32[1,128]{1,0:T(1,128)S(1)}, s32[1,128]{1,0:T(1,128)S(1)}, u32[]{:S(2)}, u32[]{:S(2)}) collective-permute-start(s32[1,128]{1,0:T(1,128)S(1)} %broadcast_select_fusion.2.refs_2_), channel_id=1, source_target_pairs={{0,1},{1,0},{2,3},{3,2},{4,5},{5,4},{6,7},{7,6},{8,9},{9,8},{10,11... | collective-permute-start | bytes 1544 | tf_op jit(solution)/shard_map/ppermute | solution.py:426
  7.2 4.6 %collective-permute-start.2 = (s32[2,128]{1,0:T(2,128)S(1)}, s32[2,128]{1,0:T(2,128)S(1)}, u32[]{:S(2)}, u32[]{:S(2)}) collective-permute-start(s32[2,128]{1,0:T(2,128)S(1)} %pad_add_fusion), channel_id=1, source_target_pairs={{0,2},{1,3},{2,0},{3,1},{4,6},{5,7},{6,4},{7,5},{8,10},{9,11},{10,... | collective-permute-start | bytes 3080 | tf_op jit(solution)/shard_map/ppermute | solution.py:427
  9.2 0.9 %copy-start = (f32[256,256]{1,0:T(8,128)S(1)}, f32[256,256]{1,0:T(8,128)}, u32[]{:S(2)}) copy-start(f32[256,256]{1,0:T(8,128)} %trans_ref.3) | copy-start | bytes 786436
  10.1 1.2 %copy-start.3 = (f32[1024,256]{1,0:T(8,128)S(1)}, f32[1024,256]{1,0:T(8,128)}, u32[]{:S(2)}) copy-start(f32[1024,256]{1,0:T(8,128)} %table_ref.1) | copy-start | bytes 3145732
  11.4 4.3 %copy-start.4 = (s32[2]{0:T(128)S(1)}, s32[2]{0:T(128)}, u32[]{:S(2)}) copy-start(s32[2]{0:T(128)} %param.8) | copy-start | bytes 28
  11.4 8.8 %copy-start.1 = (f32[256,256]{1,0:T(8,128)S(1)}, f32[256,256]{1,0:T(8,128)}, u32[]{:S(2)}) copy-start(f32[256,256]{1,0:T(8,128)} %trans_ref.3) | copy-start | bytes 786436
  11.4 8.8 %copy-start.2 = (f32[256]{0:T(256)S(1)}, f32[256]{0:T(256)}, u32[]{:S(2)}) copy-start(f32[256]{0:T(256)} %param.9) | copy-start | bytes 3076
  12.9 1.6 %collective-permute-start.3 = (f32[2,128,256]{2,1,0:T(8,128)S(1)}, f32[2,128,256]{2,1,0:T(8,128)S(1)}, u32[]{:S(2)}, u32[]{:S(2)}) collective-permute-start(f32[2,128,256]{2,1,0:T(8,128)S(1)} %get-tuple-element.83), channel_id=1, source_target_pairs={{0,1},{1,0},{2,3},{3,2},{4,5},{5,4},{6,7},{7,6},{8,9},{9,8},{10,11... | collective-permute-start | bytes 786440 | tf_op jit(solution)/shard_map/ppermute | solution.py:431
  14.6 5.6 %collective-permute-start.4 = (f32[128,256]{1,0:T(8,128)S(1)}, f32[128,256]{1,0:T(8,128)S(1)}, u32[]{:S(2)}, u32[]{:S(2)}) collective-permute-start(f32[128,256]{1,0:T(8,128)S(1)} %get-tuple-element.128), channel_id=1, source_target_pairs={{0,2},{1,3},{2,0},{3,1},{4,6},{5,7},{6,4},{7,5},{8,10},{9,11},{10,... | collective-permute-start | bytes 393224 | tf_op jit(solution)/shard_map/ppermute | solution.py:432
  40.1 4.8 %collective-permute-start.5 = (f32[8,256]{1,0:T(8,128)S(1)}, f32[8,256]{1,0:T(8,128)S(1)}, u32[]{:S(2)}, u32[]{:S(2)}) collective-permute-start(f32[8,256]{1,0:T(8,128)S(1)} %get-tuple-element.90), channel_id=1, source_target_pairs={{0,8},{24,16},{4,12},{28,20},{1,9},{25,17},{5,13},{29,21},{2,10},{... | collective-permute-start | bytes 24584 | tf_op jit(solution)/shard_map/ppermute | solution.py:459
  45.8 0.7 collective-permute-start.6
  47.3 10.1 %collective-permute-start.7 = (f32[8,256]{1,0:T(8,128)S(1)}, f32[8,256]{1,0:T(8,128)S(1)}, u32[]{:S(2)}, u32[]{:S(2)}) collective-permute-start(f32[8,256]{1,0:T(8,128)S(1)} %get-tuple-element.96), channel_id=1, source_target_pairs={{16,24},{8,0},{20,28},{12,4},{17,25},{9,1},{21,29},{13,5},{18,26},... | collective-permute-start | bytes 24584 | tf_op jit(solution)/shard_map/ppermute | solution.py:467
  62.7 19.8 %all-to-all-start.1 = ((f32[32,16,256]{2,1,0:T(8,128)}), f32[32,16,256]{2,1,0:T(8,128)S(1)}, u32[]{:S(2)}, u32[]{:S(2)}) async-start(f32[32,16,256]{2,1,0:T(8,128)} %bitcast.15), calls=%async_computation.1 | async-start | bytes 1048576 | tf_op jit(solution)/shard_map/all_to_all | solution.py:481
  67.0 6.8 %collective-permute-start.8 = (f32[64,256]{1,0:T(8,128)S(1)}, f32[64,256]{1,0:T(8,128)S(1)}, u32[]{:S(2)}, u32[]{:S(2)}) collective-permute-start(f32[64,256]{1,0:T(8,128)S(1)} %get-tuple-element.103), channel_id=1, source_target_pairs={{0,4},{4,0},{8,12},{12,8},{16,20},{20,16},{24,28},{28,24},{1,5},{5... | collective-permute-start | bytes 196616 | tf_op jit(solution)/shard_map/ppermute | solution.py:478

commit v3 on v2

--- a/solution.py
+++ b/solution.py
@@ -84,9 +84,11 @@
     return jnp.sum(jnp.where(iota(x.shape, 0) == iota(x.shape, 1), x, 0.0), axis=0, keepdims=True)
 
 
-def prepare_kernel(table_ref, trans_ref, table1_ref, table2_ref, table3_ref, trans1_ref, trans2_ref, trans3_ref,
-                   exact_ref, sums_ref):
+def table_kernel(table_ref, table1_ref, table2_ref, table3_ref):
     table1_ref[...], table2_ref[...], table3_ref[...] = split3(table_ref[...])
+
+
+def matrix_kernel(trans_ref, trans1_ref, trans2_ref, trans3_ref, exact_ref, sums_ref):
     trans = trans_ref[...]
     t1, t2, t3 = split3(trans)
     trans1_ref[...], trans2_ref[...], trans3_ref[...] = t1, t2, t3
@@ -108,7 +110,8 @@
 
 
 def product_kernel(scal_ref, own_ref, recv_ref, trans_ref, trans1_ref, trans2_ref, trans3_ref, exact_ref, sums_ref,
-                   init_ref, w_ref, lead_ref, high_ref, low_ref, state_ref, msg_ref, scaled_ref, column_ref):
+                   init_ref, w_ref, lead_ref, high_ref, low_ref, state_ref, msg_ref, root_ref,
+                   scaled_ref, column_ref):
     frames, states = w_ref.shape
     steps = frames // chunks
     first = scal_ref[0]
@@ -156,21 +159,23 @@
         def _():
             reset(c)
 
-    def inverse_sum(x):
-        return 1.0 / jnp.sum(jnp.sum(x, axis=0, keepdims=True), axis=1, keepdims=True)
-
     at = chunks
     level = list(range(chunks))
+    columns = [column_ref[c : c + 1, :] for c in range(chunks)]
     while len(level) > 1:
-        above = []
+        above, found = [], []
         for i in range(0, len(level), 2):
             a1, a2 = high_ref[level[i]], low_ref[level[i]]
             b1, b2 = high_ref[level[i + 1]], low_ref[level[i + 1]]
-            y = dot(a1, b1) + (dot(a1, b2) + dot(a2, b1))
-            high_ref[at], low_ref[at] = split2(y * inverse_sum(y))
+            column = dot(jnp.broadcast_to(columns[i], (16, states)).astype(bf16), b1)[0:1]
+            inverse = 1.0 / jnp.sum(column, axis=1, keepdims=True)
+            y = (dot(a1, b1) + (dot(a1, b2) + dot(a2, b1))) * inverse
+            high_ref[at], low_ref[at] = split2(y)
             above.append(at)
+            found.append(column * inverse)
             at += 1
-        level = above
+        level, columns = above, found
+    root_ref[...] = y
     init = init_ref[...]
     prior = jnp.broadcast_to(init / jnp.sum(init, axis=1, keepdims=True), (8, states))
     final = jnp.full((8, states), 1.0 / states, f32)
@@ -248,16 +253,19 @@
     send_ref[...] = dot(pick, high) + (dot(pick, mid) + (dot(pick, low) + meta))
 
 
-def chain_kernel(parts, scal_ref, state_ref, recv_ref, w_ref, lead_ref, high_ref, low_ref, trans1_ref,
+def chain_kernel(parts, scal_ref, state_ref, recv_ref, jump_ref, edge_ref, w_ref, lead_ref, high_ref, low_ref, trans1_ref,
                  trans2_ref, exact_ref, sums_ref, pick_ref, meta_ref,
                  keep_ref, away_ref, occ_ref, send_ref, split_ref, leads_ref, fore_ref,
                  back_ref, start_ref, end_ref, post_ref):
     frames, states = w_ref.shape
     steps = frames // chunks
     first = scal_ref[0]
-    state = merge_state(state_ref[...], recv_ref[...], scal_ref[1], parts, parts - 2)
-    start_ref[0:1, :] = state[0:1, :]
-    end_ref[chunks - 1 : chunks, :] = state[1:2, :]
+    state = merge_state(state_ref[...], recv_ref[...], scal_ref[1], parts, parts - 3)
+    edge1, edge2 = split2(edge_ref[...])
+    fore = normalize(row_times(jump_ref[...], jnp.concatenate([edge1, edge2], axis=1), states, 2))
+    back = normalize(times_col(jump_ref[...], jnp.concatenate([edge1, edge2], axis=0), states, 2))
+    start_ref[0:1, :] = jnp.where(scal_ref[1] == parts - 1, fore[0:1, :], state[0:1, :])
+    end_ref[chunks - 1 : chunks, :] = jnp.where(scal_ref[1] == 0, back[1:2, :], state[1:2, :])
     width = chunks
     offsets = {}
     at = 0
@@ -376,10 +384,10 @@
 smem = pl.BlockSpec(memory_space=pltpu.MemorySpace.SMEM)
 
 
-def call(kernel, name, in_specs, out_specs, out_shape, scratch=(), cost=None):
+def call(kernel, in_specs, out_specs, out_shape, scratch=(), cost=None):
     if cost is not None:
         cost = pl.CostEstimate(flops=cost, bytes_accessed=cost // 100, transcendentals=0)
-    return pl.pallas_call(kernel, name=name, cost_estimate=cost, in_specs=in_specs, out_specs=out_specs, out_shape=out_shape,
+    return pl.pallas_call(kernel, cost_estimate=cost, in_specs=in_specs, out_specs=out_specs, out_shape=out_shape,
                           scratch_shapes=scratch, compiler_params=pltpu.CompilerParams(vmem_limit_bytes=granted))
 
 
@@ -387,7 +395,7 @@
     return jax.ShapeDtypeStruct(dims, dtype)
 
 
-def shards(observed, starts, initial, transition, emission):
+def update(observed, starts, initial, transition, emission):
     traj_rows, frame_count = observed.shape
     states = transition.shape[0]
     tm_count = lax.axis_size("tm")
@@ -410,6 +418,9 @@
     kept = jnp.where(side == 0, observed[0:1], observed[1:2])
     given = jnp.where(side == 0, observed[1:2], observed[0:1])
     taken = lax.ppermute(given, "tm", [(i, i ^ 1) for i in range(tm_count)])
+    table = shape(own_rows, states, dtype=bf16)
+    tables = call(table_kernel, [vmem], [vmem] * 3, [table] * 3, cost=400_000_000)(emission)
+    taken, tables = lax.optimization_barrier((taken, tables))
     ids = jnp.where(side == 0, jnp.concatenate([kept, taken], axis=1), jnp.concatenate([taken, kept], axis=1))
     first = jnp.where(side == 0, starts[0], starts[1]) - part * frames
     scal = jnp.stack([first, part, (flat % (states // slots)) * slots, side, emit_place, starts[0], starts[1]])
@@ -418,24 +429,25 @@
     def swaps(k):
         return [(i, i ^ k) for i in range(emit_count)]
 
-    narrow = shape(states, states, dtype=bf16)
-    table = shape(own_rows, states, dtype=bf16)
-    prepared = call(prepare_kernel, "prepare", [vmem] * 2, [vmem] * 8,
-                    [table] * 3 + [narrow] * 3 + [shape(1, states)] * 2, cost=400_000_000)(emission, transition)
-    tables, matrices, exact, sums = prepared[:3], prepared[3:6], prepared[6], prepared[7]
     near = jnp.concatenate([ids, lax.ppermute(ids, "emit", swaps(1))], axis=0)
     far = [lax.ppermute(near, "emit", swaps(k)) for k in range(2, emit_count, 2)]
     wanted = jnp.concatenate([near] + far, axis=0) - emit_place * own_rows
     half = shape(emit_count // 2, frames, states)
-    mine, other = call(gather_kernel, "gather", [vmem] * 4, [vmem, vmem], [half, half])(wanted, *tables)
+    mine, other = call(gather_kernel, [vmem] * 4, [vmem, vmem], [half, half])(wanted, *tables)
     both_cores = mine + lax.ppermute(other, "emit", swaps(1))
     came = [lax.ppermute(both_cores[k // 2], "emit", swaps(k)) for k in range(2, emit_count, 2)]
     came = sum(came[1:], came[0])
+    narrow = shape(states, states, dtype=bf16)
+    row = shape(1, states)
+    refined = call(matrix_kernel, [vmem], [vmem] * 5, [narrow] * 3 + [row] * 2, cost=400_000_000)(transition)
+    came, refined = lax.optimization_barrier((came, refined))
+    matrices, exact, sums = refined[:3], refined[3], refined[4]
     nodes = 2 * chunks - 1
-    weights, lead, high, low, state, message = call(
-        product_kernel, "product", [smem] + [vmem] * 9, [vmem] * 6,
+    weights, lead, high, low, state, message, root = call(
+        product_kernel, [smem] + [vmem] * 9, [vmem] * 7,
         [shape(frames, states), shape(frames, states), shape(nodes, states, states, dtype=bf16),
-         shape(nodes, states, states, dtype=bf16), shape(8, states), shape(8, states)],
+         shape(nodes, states, states, dtype=bf16), shape(8, states), shape(8, states),
+         shape(states, states)],
         [pltpu.VMEM((chunks, states), f32)] * 2,
     )(scal, both_cores[0], came, transition, *matrices, exact, sums, initial.reshape(1, states))
 
@@ -444,7 +456,7 @@
             address_kernel(block, *refs)
 
         lines = devices * slots
-        return call(kernel, "address", [smem, smem, vmem], [vmem, vmem],
+        return call(kernel, [smem, smem, vmem], [vmem, vmem],
                     [shape(lines, frames, dtype=bf16), shape(lines, states)], cost=400_000_000)(scal, turn, ids)
 
     pick, meta = address(jnp.zeros((1,), jnp.int32))
@@ -456,25 +468,31 @@
             pairs.append((2 * (parts - 1 - turn) + y, 2 * (parts - 2 - turn) + y))
         return pairs
 
+    def end_pairs(fore, back):
+        return [pair for y in range(2) for pair in ((2 * fore + y, 2 * (parts - 1) + y), (2 * back + y, y))]
+
+    assert parts >= 4
     recv = lax.ppermute(message, "tm", relay_pairs(0))
-    for turn in range(1, parts - 1):
+    edge = lax.ppermute(root, "tm", end_pairs(parts - 2, 1))
+    for turn in range(1, parts - 2):
         def relay(*refs, turn=turn):
             relay_kernel(parts, turn, *refs)
 
         state, message = call(
-            relay, "relay", [smem] + [vmem] * 4, [vmem] * 2, [shape(8, states), shape(8, states)]
+            relay, [smem] + [vmem] * 4, [vmem] * 2, [shape(8, states), shape(8, states)]
         )(scal, state, recv, high, low)
         recv = lax.ppermute(message, "tm", relay_pairs(turn))
+    ahead = lax.ppermute(message, "tm", end_pairs(parts - 3, 2))
 
     def chain(*refs):
         chain_kernel(parts, *refs)
 
     keep, away, occupancy, send = call(
-        chain, "chain", [smem] + [vmem] * 12, [vmem] * 4,
+        chain, [smem] + [vmem] * 14, [vmem] * 4,
         [shape(frame_count, states), shape(frame_count, states), shape(frames, states), shape(devices * slots, states)],
         [pltpu.VMEM((states // 128, frames, 128), f32)] * 4
         + [pltpu.VMEM((chunks, states), f32)] * 2 + [pltpu.VMEM((frames, states), f32)],
-    )(scal, state, recv, weights, lead, high, low, matrices[0], matrices[1], exact, sums, pick, meta)
+    )(scal, state, recv, ahead, edge, weights, lead, high, low, matrices[0], matrices[1], exact, sums, pick, meta)
     other = lax.ppermute(away, "tm", [(i, i ^ 1) for i in range(tm_count)])
 
     def exchange(sent):
@@ -485,7 +503,7 @@
         final_kernel(block, total_rows, emit_count, length, *refs)
 
     posterior, new_emission, loglik, counts, totals, most = call(
-        final, "final", [smem, vmem, vmem, vmem], [vmem, vmem, smem, vmem, vmem, smem],
+        final, [smem, vmem, vmem, vmem], [vmem, vmem, smem, vmem, vmem, smem],
         [shape(2, frame_count, states), shape(block, states), shape(2), shape(block, states), shape(1, states),
          shape(1, dtype=jnp.int32)],
     )(scal, exchange(send), keep, other)
@@ -496,10 +514,10 @@
         def more(*refs):
             more_kernel(block, *refs)
 
-        sent = call(pack_kernel, "pack", [smem] + [vmem] * 3, vmem, shape(devices * slots, states))(
+        sent = call(pack_kernel, [smem] + [vmem] * 3, vmem, shape(devices * slots, states))(
             scal, *address(turn.reshape(1)), occupancy
         )
-        counts = call(more, "more", [vmem, vmem], vmem, shape(block, states))(exchange(sent), counts)
+        counts = call(more, [vmem, vmem], vmem, shape(block, states))(exchange(sent), counts)
         return turn + 1, counts, emit_update(counts, totals, total_rows)
 
     _, _, new_emission = lax.while_loop(
@@ -511,4 +529,4 @@
 def solution(mesh):
     in_specs = (P("emit", "tm"), P("emit"), P(), P(), P("emit", None))
     out_specs = (P("emit", "tm", None), P(("tm", "emit"), None), P("emit"))
-    return jax.shard_map(shards, mesh=mesh, in_specs=in_specs, out_specs=out_specs, check_vma=False)
+    return jax.shard_map(update, mesh=mesh, in_specs=in_specs, out_specs=out_specs, check_vma=False)

time: 85.3 us -> 85.1 us (level)
  starting transfers between devices: 17.7 us -> 22 us
  waiting for transfers between devices: 29.7 us -> 27.6 us
  Pallas kernels: 31 us -> 29.5 us
  local copies, waits for them, and re-layouts: 2.87 us -> 1.93 us
    ppermute x9 -> x10, starting transfers between devices: 13.5 us -> 16.9 us  [the longest x1 4.56 us: update(): recv = lax.ppermute(message, 'tm', relay_pairs(0))]
    ppermute x9 -> x10, waiting for transfers between devices: 20.9 us -> 18.8 us  [the longest x1 6.55 us: update(): ahead = lax.ppermute(message, 'tm', end_pairs(parts - 3, 2))]
    pallas_call x8, Pallas kernels: 31 us -> 29.5 us  [the longest x1 19 us: update(): call(product_kernel, [smem] + [vmem] * 9, [vmem] * 7, [shape(frames, stat...]
    unnamed x10 -> x8, local copies, waits for them, and re-layouts: 2.18 us -> 1.24 us
    all_to_all x1, starting transfers between devices: 4.22 us -> 5.15 us  [exchange(): lax.all_to_all(sent.reshape(devices, slots, states), both, 0, 0, tiled=True)]
  transfers between devices with their start and end apart: 10 -> 11, of which waited for: 8 -> 9; matrix products, arithmetic and copies ran while one was open for 1% -> 1% of each run, Pallas kernels for 2% -> 3%
where the time goes in v3:
time: 85.1 us; the launch traced here: 84.8 us
  Pallas kernels  29.5 us (35%)
  waiting for transfers between devices  27.6 us (32%)
  starting transfers between devices  22 us (26%)
  between operations  2.11 us (2%)
  local copies, waits for them, and re-layouts  1.93 us (2%)
  other arithmetic  0.89 us (1%)
    pallas_call x1, Pallas kernels, update(): call(product_kernel, [smem] + [vmem] * 9, [vmem] * 7, [shape(frames, stat...  19 us
    all_to_all x1, waiting for transfers between devices, exchange(): lax.all_to_all(sent.reshape(devices, slots, states), both, 0, 0, tiled=True)  8.8 us
    ppermute x1, waiting for transfers between devices, update(): ahead = lax.ppermute(message, 'tm', end_pairs(parts - 3, 2))  6.55 us
    pallas_call x1, Pallas kernels, update(): call(chain, [smem] + [vmem] * 14, [vmem] * 4, [shape(frame_count, states)...  5.57 us
    all_to_all x1, starting transfers between devices, exchange(): lax.all_to_all(sent.reshape(devices, slots, states), both, 0, 0, tiled=True)  5.15 us
    ppermute x1, waiting for transfers between devices, update(): other = lax.ppermute(away, 'tm', [(i, i ^ 1) for i in range(tm_count)])  4.97 us
    ppermute x1, starting transfers between devices, update(): recv = lax.ppermute(message, 'tm', relay_pairs(0))  4.56 us
    ppermute x1, starting transfers between devices, update(): taken = lax.ppermute(given, 'tm', [(i, i ^ 1) for i in range(tm_count)])  3 us
  transfers between devices with their start and end apart: 11, of which 9 were waited for; matrix products, arithmetic and copies ran while one was open for 1% of the time, Pallas kernels for 3%

profile of v3, /device:TPU:0, one launch (start us, length us, event | category | flops | bytes accessed | tf_op | source)
XLA Modules:
  0.0 84.8 jit_solution(652243039145318150)
XLA Ops:
  0.6 0.8 broadcast_select_fusion.1
  1.4 3.0 %collective-permute-start = (s32[1,64]{1,0:T(1,128)S(1)}, s32[1,64]{1,0:T(1,128)S(1)}, u32[]{:S(2)}, u32[]{:S(2)}) collective-permute-start(s32[1,64]{1,0:T(1,128)S(1)} %get-tuple-element.149), channel_id=1, source_target_pairs={{0,4},{4,0},{8,12},{12,8},{16,20},{20,16},{24,28},{28,24},{1,5},{5... | collective-permute-start | bytes 776 | tf_op jit(solution)/shard_map/ppermute | solution.py:420
  4.4 1.2 %copy-done.2 = f32[1024,256]{1,0:T(8,128)S(1)} copy-done((f32[1024,256]{1,0:T(8,128)S(1)}, f32[1024,256]{1,0:T(8,128)}, u32[]{:S(2)}) %copy-start.2) | copy-done | bytes 1048600
  5.6 0.3 shard_map.76
  6.0 0.1 broadcast_select_fusion.2.refs_2_
  6.0 1.1 %collective-permute-done.1 = s32[1,128]{1,0:T(1,128)S(1)} collective-permute-done((s32[1,128]{1,0:T(1,128)S(1)}, s32[1,128]{1,0:T(1,128)S(1)}, u32[]{:S(2)}, u32[]{:S(2)}) %collective-permute-start.1) | collective-permute-done | bytes 544 | tf_op jit(solution)/shard_map/ppermute | solution.py:432
  7.2 2.0 %collective-permute-start.2 = (s32[2,128]{1,0:T(2,128)S(1)}, s32[2,128]{1,0:T(2,128)S(1)}, u32[]{:S(2)}, u32[]{:S(2)}) collective-permute-start(s32[2,128]{1,0:T(2,128)S(1)} %pad_add_fusion), channel_id=1, source_target_pairs={{0,2},{1,3},{2,0},{3,1},{4,6},{5,7},{6,4},{7,5},{8,10},{9,11},{10,... | collective-permute-start | bytes 3080 | tf_op jit(solution)/shard_map/ppermute | solution.py:433
  9.2 1.6 %collective-permute-done.2 = s32[2,128]{1,0:T(2,128)S(1)} collective-permute-done((s32[2,128]{1,0:T(2,128)S(1)}, s32[2,128]{1,0:T(2,128)S(1)}, u32[]{:S(2)}, u32[]{:S(2)}) %collective-permute-start.2) | collective-permute-done | bytes 1056 | tf_op jit(solution)/shard_map/ppermute | solution.py:433
  10.8 1.1 %shard_map.77 = (f32[2,128,256]{2,1,0:T(8,128)S(1)}, f32[2,128,256]{2,1,0:T(8,128)S(1)}) custom-call(s32[4,128]{1,0:T(4,128)S(1)} %add_subtract_fusion.ids_ref, bf16[1024,256]{1,0:T(8,128)(2,1)S(1)} %get-tuple-element.92.high_ref, bf16[1024,256]{1,0:T(8,128)(2,1)S(1)} %get-tuple-element.93.mid_ref, bf16[1024,256]{1,0:T(8,128)(2,1)S(1)} %get-tuple-element.94.low_ref), custom_call_target="tpu_custom_call" | custom-call | tf_op jit(solution)/shard_map/pallas_call | solution.py:436
  11.9 0.1 collective-permute-start.3
  12.0 1.5 %collective-permute-done.3 = f32[2,128,256]{2,1,0:T(8,128)S(1)} collective-permute-done((f32[2,128,256]{2,1,0:T(8,128)S(1)}, f32[2,128,256]{2,1,0:T(8,128)S(1)}, u32[]{:S(2)}, u32[]{:S(2)}) %collective-permute-start.3) | collective-permute-done | bytes 262176 | tf_op jit(solution)/shard_map/ppermute | solution.py:437
  13.6 2.1 %collective-permute-start.4 = (f32[128,256]{1,0:T(8,128)S(1)}, f32[128,256]{1,0:T(8,128)S(1)}, u32[]{:S(2)}, u32[]{:S(2)}) collective-permute-start(f32[128,256]{1,0:T(8,128)S(1)} %get-tuple-element.146), channel_id=1, source_target_pairs={{0,2},{1,3},{2,0},{3,1},{4,6},{5,7},{6,4},{7,5},{8,10},{9,11},{10,... | collective-permute-start | bytes 393224 | tf_op jit(solution)/shard_map/ppermute | solution.py:438
  15.7 0.6 fusion
  17.5 0.1 stack.23.scal_ref.refs_0_
  17.6 0.1 shard_map.78
  17.8 1.7 %collective-permute-done.4.recv_ref = f32[128,256]{1,0:T(8,128)S(1)} collective-permute-done((f32[128,256]{1,0:T(8,128)S(1)}, f32[128,256]{1,0:T(8,128)S(1)}, u32[]{:S(2)}, u32[]{:S(2)}) %collective-permute-start.4) | collective-permute-done | bytes 131104 | tf_op jit(solution)/shard_map/ppermute | solution.py:438
  19.4 19.0 %shard_map.79 = (f32[128,256]{1,0:T(8,128)S(1)}, f32[128,256]{1,0:T(8,128)S(1)}, bf16[15,256,256]{2,1,0:T(8,128)(2,1)S(1)}, bf16[15,256,256]{2,1,0:T(8,128)(2,1)...) custom-call(s32[7]{0:T(128)S(1)} %stack.23.scal_ref.refs_0_, ...), custom_call_target="tpu_custom_call" | custom-call | tf_op jit(solution)/shard_map/pallas_call | solution.py:446
  38.5 1.4 %collective-permute-start.8 = (f32[256,256]{1,0:T(8,128)S(1)}, f32[256,256]{1,0:T(8,128)S(1)}, u32[]{:S(2)}, u32[]{:S(2)}) collective-permute-start(f32[256,256]{1,0:T(8,128)S(1)} %get-tuple-element.114), channel_id=1, source_target_pairs={{16,24},{8,0},{20,28},{12,4},{17,25},{9,1},{21,29},{13,5},{18,26},... | collective-permute-start | bytes 786440 | tf_op jit(solution)/shard_map/ppermute | solution.py:476
  39.8 4.6 %collective-permute-start.5 = (f32[8,256]{1,0:T(8,128)S(1)}, f32[8,256]{1,0:T(8,128)S(1)}, u32[]{:S(2)}, u32[]{:S(2)}) collective-permute-start(f32[8,256]{1,0:T(8,128)S(1)} %get-tuple-element.109), channel_id=1, source_target_pairs={{0,8},{24,16},{4,12},{28,20},{1,9},{25,17},{5,13},{29,21},{2,10},{... | collective-permute-start | bytes 24584 | tf_op jit(solution)/shard_map/ppermute | solution.py:475
  44.4 1.3 %collective-permute-done.5.refs_2_ = f32[8,256]{1,0:T(8,128)S(1)} collective-permute-done((f32[8,256]{1,0:T(8,128)S(1)}, f32[8,256]{1,0:T(8,128)S(1)}, u32[]{:S(2)}, u32[]{:S(2)}) %collective-permute-start.5) | collective-permute-done | bytes 8224 | tf_op jit(solution)/shard_map/ppermute | solution.py:475
  45.7 0.8 shard_map.80
  46.6 0.7 collective-permute-start.6
  47.3 1.3 %collective-permute-start.7 = (f32[8,256]{1,0:T(8,128)S(1)}, f32[8,256]{1,0:T(8,128)S(1)}, u32[]{:S(2)}, u32[]{:S(2)}) collective-permute-start(f32[8,256]{1,0:T(8,128)S(1)} %get-tuple-element.113), channel_id=1, source_target_pairs={{8,24},{16,0},{12,28},{20,4},{9,25},{17,1},{13,29},{21,5},{10,26},... | collective-permute-start | bytes 24584 | tf_op jit(solution)/shard_map/ppermute | solution.py:485
  48.6 1.0 %shard_map.81 = (bf16[512,128]{1,0:T(8,128)(2,1)S(1)}, f32[512,256]{1,0:T(8,128)S(1)}) custom-call(s32[7]{0:T(128)S(1)} %stack.23.scal_ref.refs_0_, s32[1]{0:T(128)} %constant.62.clone.1.refs_1_, s32[1,128]{1,0:T(1,128)S(1)} %broadcast_select_fusion.2.refs_2_), custom_call_target="tpu_custom_call" | custom-call | flops 400000000 | bytes 4000000 | tf_op jit(solution)/shard_map/pallas_call | solution.py:459
  49.5 6.6 %collective-permute-done.7.refs_3_ = f32[8,256]{1,0:T(8,128)S(1)} collective-permute-done((f32[8,256]{1,0:T(8,128)S(1)}, f32[8,256]{1,0:T(8,128)S(1)}, u32[]{:S(2)}, u32[]{:S(2)}) %collective-permute-start.7) | collective-permute-done | bytes 8224 | tf_op jit(solution)/shard_map/ppermute | solution.py:485
  56.1 5.6 %shard_map.82 = (f32[64,256]{1,0:T(8,128)S(1)}, f32[64,256]{1,0:T(8,128)S(1)}, f32[128,256]{1,0:T(8,128)S(1)}, f32[512,256]{1,0:T(8,128)}) custom-call(s32[7]{0:T(128)S(1)} %stack.23.scal_ref.refs_0_, f32[8,256]{1,0:T(8,128)S(1)} %get-tuple-element.112.refs_1_, f32[8,256]{1,0:T(8,128)S(1)} %collective-permute-done.6.refs_2_, ...), custom_call_target="tpu_custom_call" | custom-call | tf_op jit(solution)/shard_map/pallas_call | solution.py:490
  61.7 5.2 %all-to-all-start.1 = ((f32[32,16,256]{2,1,0:T(8,128)}), f32[32,16,256]{2,1,0:T(8,128)S(1)}, u32[]{:S(2)}, u32[]{:S(2)}) async-start(f32[32,16,256]{2,1,0:T(8,128)} %bitcast.15), calls=%async_computation.1 | async-start | bytes 1048576 | tf_op jit(solution)/shard_map/all_to_all | solution.py:499
  66.8 1.8 %collective-permute-start.9 = (f32[64,256]{1,0:T(8,128)S(1)}, f32[64,256]{1,0:T(8,128)S(1)}, u32[]{:S(2)}, u32[]{:S(2)}) collective-permute-start(f32[64,256]{1,0:T(8,128)S(1)} %get-tuple-element.121), channel_id=1, source_target_pairs={{0,4},{4,0},{8,12},{12,8},{16,20},{20,16},{24,28},{28,24},{1,5},{5... | collective-permute-start | bytes 196616 | tf_op jit(solution)/shard_map/ppermute | solution.py:496
  68.7 5.0 %collective-permute-done.9.refs_3_ = f32[64,256]{1,0:T(8,128)S(1)} collective-permute-done((f32[64,256]{1,0:T(8,128)S(1)}, f32[64,256]{1,0:T(8,128)S(1)}, u32[]{:S(2)}, u32[]{:S(2)}) %collective-permute-start.9) | collective-permute-done | bytes 65568 | tf_op jit(solution)/shard_map/ppermute | solution.py:496
  73.6 8.8 %all-to-all-done.1 = f32[32,16,256]{2,1,0:T(8,128)S(1)} async-done(((f32[32,16,256]{2,1,0:T(8,128)}), f32[32,16,256]{2,1,0:T(8,128)S(1)}, u32[]{:S(2)}, u32[]{:S(2)}) %all-to-all-start.1) | async-done | bytes 524320 | tf_op jit(solution)/shard_map/all_to_all | solution.py:499
  82.4 1.6 %shard_map.83 = (f32[2,64,256]{2,1,0:T(8,128)}, f32[128,256]{1,0:T(8,128)}, f32[2]{0:T(128)}, f32[128,256]{1,0:T(8,128)S(1)}, f32[1,256]{1,0:T(1,128)S(1)}, /*index=5*/s32[1]{0:T(128)}) custom-call(s32[7]{0:T(128)S(1)} %stack.23.scal_ref.refs_0_, f32[512,256]{1,0:T(8,128)S(1)} %bitcast.29, f32[64,256]{1,0:T(8,128)S(1)} %get-tuple-element.120.refs_2_, ...), custom_call_target="tpu_custom_call" | custom-call | tf_op jit(solution)/shard_map/pallas_call | solution.py:505
  84.1 0.7 while.12
  (15 shorter events, 0.2 us)
Async XLA Ops:
  1.4 16.2 %copy-start = (f32[256,256]{1,0:T(8,128)S(1)}, f32[256,256]{1,0:T(8,128)}, u32[]{:S(2)}) copy-start(f32[256,256]{1,0:T(8,128)} %trans_ref.3) | copy-start | bytes 786436
  1.4 4.5 %collective-permute-start = (s32[1,64]{1,0:T(1,128)S(1)}, s32[1,64]{1,0:T(1,128)S(1)}, u32[]{:S(2)}, u32[]{:S(2)}) collective-permute-start(s32[1,64]{1,0:T(1,128)S(1)} %get-tuple-element.149), channel_id=1, source_target_pairs={{0,4},{4,0},{8,12},{12,8},{16,20},{20,16},{24,28},{28,24},{1,5},{5... | collective-permute-start | bytes 776 | tf_op jit(solution)/shard_map/ppermute | solution.py:420
  4.4 1.2 %copy-start.2 = (f32[1024,256]{1,0:T(8,128)S(1)}, f32[1024,256]{1,0:T(8,128)}, u32[]{:S(2)}) copy-start(f32[1024,256]{1,0:T(8,128)} %table_ref.1) | copy-start | bytes 3145732
  5.6 10.0 %copy-start.3 = (s32[2]{0:T(128)S(1)}, s32[2]{0:T(128)}, u32[]{:S(2)}) copy-start(s32[2]{0:T(128)} %param.8) | copy-start | bytes 28
  6.0 1.2 %collective-permute-start.1 = (s32[1,128]{1,0:T(1,128)S(1)}, s32[1,128]{1,0:T(1,128)S(1)}, u32[]{:S(2)}, u32[]{:S(2)}) collective-permute-start(s32[1,128]{1,0:T(1,128)S(1)} %broadcast_select_fusion.2.refs_2_), channel_id=1, source_target_pairs={{0,1},{1,0},{2,3},{3,2},{4,5},{5,4},{6,7},{7,6},{8,9},{9,8},{10,11... | collective-permute-start | bytes 1544 | tf_op jit(solution)/shard_map/ppermute | solution.py:432
  7.2 3.6 %collective-permute-start.2 = (s32[2,128]{1,0:T(2,128)S(1)}, s32[2,128]{1,0:T(2,128)S(1)}, u32[]{:S(2)}, u32[]{:S(2)}) collective-permute-start(s32[2,128]{1,0:T(2,128)S(1)} %pad_add_fusion), channel_id=1, source_target_pairs={{0,2},{1,3},{2,0},{3,1},{4,6},{5,7},{6,4},{7,5},{8,10},{9,11},{10,... | collective-permute-start | bytes 3080 | tf_op jit(solution)/shard_map/ppermute | solution.py:433
  10.8 8.7 %copy-start.1 = (f32[256]{0:T(256)S(1)}, f32[256]{0:T(256)}, u32[]{:S(2)}) copy-start(f32[256]{0:T(256)} %param.9) | copy-start | bytes 3076
  11.9 1.6 %collective-permute-start.3 = (f32[2,128,256]{2,1,0:T(8,128)S(1)}, f32[2,128,256]{2,1,0:T(8,128)S(1)}, u32[]{:S(2)}, u32[]{:S(2)}) collective-permute-start(f32[2,128,256]{2,1,0:T(8,128)S(1)} %get-tuple-element.96), channel_id=1, source_target_pairs={{0,1},{1,0},{2,3},{3,2},{4,5},{5,4},{6,7},{7,6},{8,9},{9,8},{10,11... | collective-permute-start | bytes 786440 | tf_op jit(solution)/shard_map/ppermute | solution.py:437
  13.6 5.9 %collective-permute-start.4 = (f32[128,256]{1,0:T(8,128)S(1)}, f32[128,256]{1,0:T(8,128)S(1)}, u32[]{:S(2)}, u32[]{:S(2)}) collective-permute-start(f32[128,256]{1,0:T(8,128)S(1)} %get-tuple-element.146), channel_id=1, source_target_pairs={{0,2},{1,3},{2,0},{3,1},{4,6},{5,7},{6,4},{7,5},{8,10},{9,11},{10,... | collective-permute-start | bytes 393224 | tf_op jit(solution)/shard_map/ppermute | solution.py:438
  38.5 17.6 %collective-permute-start.8 = (f32[256,256]{1,0:T(8,128)S(1)}, f32[256,256]{1,0:T(8,128)S(1)}, u32[]{:S(2)}, u32[]{:S(2)}) collective-permute-start(f32[256,256]{1,0:T(8,128)S(1)} %get-tuple-element.114), channel_id=1, source_target_pairs={{16,24},{8,0},{20,28},{12,4},{17,25},{9,1},{21,29},{13,5},{18,26},... | collective-permute-start | bytes 786440 | tf_op jit(solution)/shard_map/ppermute | solution.py:476
  39.8 5.9 %collective-permute-start.5 = (f32[8,256]{1,0:T(8,128)S(1)}, f32[8,256]{1,0:T(8,128)S(1)}, u32[]{:S(2)}, u32[]{:S(2)}) collective-permute-start(f32[8,256]{1,0:T(8,128)S(1)} %get-tuple-element.109), channel_id=1, source_target_pairs={{0,8},{24,16},{4,12},{28,20},{1,9},{25,17},{5,13},{29,21},{2,10},{... | collective-permute-start | bytes 24584 | tf_op jit(solution)/shard_map/ppermute | solution.py:475
  46.6 3.0 %collective-permute-start.6 = (f32[8,256]{1,0:T(8,128)S(1)}, f32[8,256]{1,0:T(8,128)S(1)}, u32[]{:S(2)}, u32[]{:S(2)}) collective-permute-start(f32[8,256]{1,0:T(8,128)S(1)} %get-tuple-element.113), channel_id=1, source_target_pairs={{8,16},{16,8},{12,20},{20,12},{9,17},{17,9},{13,21},{21,13},{10,18... | collective-permute-start | bytes 24584 | tf_op jit(solution)/shard_map/ppermute | solution.py:484
  47.3 8.8 %collective-permute-start.7 = (f32[8,256]{1,0:T(8,128)S(1)}, f32[8,256]{1,0:T(8,128)S(1)}, u32[]{:S(2)}, u32[]{:S(2)}) collective-permute-start(f32[8,256]{1,0:T(8,128)S(1)} %get-tuple-element.113), channel_id=1, source_target_pairs={{8,24},{16,0},{12,28},{20,4},{9,25},{17,1},{13,29},{21,5},{10,26},... | collective-permute-start | bytes 24584 | tf_op jit(solution)/shard_map/ppermute | solution.py:485
  61.7 20.8 %all-to-all-start.1 = ((f32[32,16,256]{2,1,0:T(8,128)}), f32[32,16,256]{2,1,0:T(8,128)S(1)}, u32[]{:S(2)}, u32[]{:S(2)}) async-start(f32[32,16,256]{2,1,0:T(8,128)} %bitcast.15), calls=%async_computation.1 | async-start | bytes 1048576 | tf_op jit(solution)/shard_map/all_to_all | solution.py:499
  66.8 6.8 %collective-permute-start.9 = (f32[64,256]{1,0:T(8,128)S(1)}, f32[64,256]{1,0:T(8,128)S(1)}, u32[]{:S(2)}, u32[]{:S(2)}) collective-permute-start(f32[64,256]{1,0:T(8,128)S(1)} %get-tuple-element.121), channel_id=1, source_target_pairs={{0,4},{4,0},{8,12},{12,8},{16,20},{20,16},{24,28},{28,24},{1,5},{5... | collective-permute-start | bytes 196616 | tf_op jit(solution)/shard_map/ppermute | solution.py:496

commit v4 on v3

--- a/solution.py
+++ b/solution.py
@@ -11,6 +11,7 @@
 chunks = 8
 slots = 16
 rows_sent = 14
+unrolled = 3
 granted = 24 << 20
 
 
@@ -109,73 +110,103 @@
         (other_ref if k % 2 else mine_ref)[k // 2] = taken
 
 
-def product_kernel(scal_ref, own_ref, recv_ref, trans_ref, trans1_ref, trans2_ref, trans3_ref, exact_ref, sums_ref,
-                   init_ref, w_ref, lead_ref, high_ref, low_ref, state_ref, msg_ref, root_ref,
-                   scaled_ref, column_ref):
+def half_product(half, first, mats, w_ref, lead_ref, high_ref, low_ref, scaled_ref, column_ref, eye_ref):
+    trans_ref, trans1_ref, trans2_ref, trans3_ref, exact_ref, sums_ref = mats
     frames, states = w_ref.shape
-    steps = frames // chunks
-    first = scal_ref[0]
-    w_ref[...] = own_ref[...] + recv_ref[...]
+    count = chunks // 2
+    steps = frames // count
+    first = first - half * frames
     cat = jnp.concatenate([trans1_ref[...], trans2_ref[...], trans3_ref[...]], axis=0)
     lead_ref[...] = times_col(w_ref[...], cat, states, 3)
-
-    def store(c, y, columns):
-        column_ref[c : c + 1, :] = columns
-        high_ref[c], low_ref[c] = split2(y)
-
-    def reset(c):
-        eye = iota((states, states), 0) == iota((states, states), 1)
-        high_ref[c] = jnp.where(eye, 1.0, 0.0).astype(bf16)
-        low_ref[c] = jnp.zeros((states, states), bf16)
-        column_ref[pl.ds(c, 1), :] = jnp.ones((1, states), f32)
-
-    for c in range(chunks):
+    eye = iota((states, states), 0) == iota((states, states), 1)
+    eye_ref[...] = jnp.where(eye, 1.0, 0.0).astype(bf16)
+
+    def store(c, k, y, columns):
+        live = c * steps + k >= first
+        column_ref[c : c + 1, :] = jnp.where(live, columns, 1.0)
+        y1, y2 = split2(y)
+        high_ref[half * count + c] = jnp.where(live, y1, eye_ref[...])
+        low_ref[half * count + c] = jnp.where(live, y2, jnp.zeros_like(y2))
+
+    for c in range(count):
         row = w_ref[c * steps : c * steps + 1, :]
         row = row / jnp.sum(sums_ref[...] * row, axis=1, keepdims=True)
-        store(c, trans_ref[...] * row, sums_ref[...] * row)
-    start_chunk = lax.div(first, steps)
-    start_step = lax.rem(first, steps)
-
-    def step(k, carried):
-        @pl.when((start_step == k) & (first >= 0) & (first < frames))
-        def _():
-            reset(start_chunk)
-
-        for c in range(chunks):
-            frame = c * steps + k
-            total = jnp.sum(lead_ref[pl.ds(frame, 1), :] * column_ref[c : c + 1, :], axis=1, keepdims=True)
-            scaled_ref[c : c + 1, :] = w_ref[pl.ds(frame, 1), :] * exact_ref[...] / total
-        for c in range(chunks):
-            x1, x2 = high_ref[c], low_ref[c]
-            y = dot(x1, trans1_ref[...]) + (dot(x1, trans2_ref[...]) + dot(x2, trans1_ref[...]))
-            y = y * scaled_ref[c : c + 1, :]
-            store(c, y, jnp.sum(y, axis=0, keepdims=True))
+        store(c, 0, trans_ref[...] * row, sums_ref[...] * row)
+
+    def several(i, carried):
+        for j in range(unrolled):
+            k = 1 + unrolled * i + j
+            for c in range(count):
+                frame = c * steps + k
+                total = jnp.sum(lead_ref[pl.ds(frame, 1), :] * column_ref[c : c + 1, :], axis=1, keepdims=True)
+                scaled_ref[c : c + 1, :] = w_ref[pl.ds(frame, 1), :] * exact_ref[...] / total
+                x1, x2 = high_ref[half * count + c], low_ref[half * count + c]
+                y = dot(x1, trans1_ref[...]) + (dot(x1, trans2_ref[...]) + dot(x2, trans1_ref[...]))
+                y = y * scaled_ref[c : c + 1, :]
+                store(c, k, y, jnp.sum(y, axis=0, keepdims=True))
         return carried
 
-    lax.fori_loop(1, steps, step, 0)
-    for c in range(chunks):
-
-        @pl.when((c + 1) * steps <= first)
-        def _():
-            reset(c)
-
-    at = chunks
-    level = list(range(chunks))
-    columns = [column_ref[c : c + 1, :] for c in range(chunks)]
-    while len(level) > 1:
-        above, found = [], []
-        for i in range(0, len(level), 2):
-            a1, a2 = high_ref[level[i]], low_ref[level[i]]
-            b1, b2 = high_ref[level[i + 1]], low_ref[level[i + 1]]
-            column = dot(jnp.broadcast_to(columns[i], (16, states)).astype(bf16), b1)[0:1]
-            inverse = 1.0 / jnp.sum(column, axis=1, keepdims=True)
-            y = (dot(a1, b1) + (dot(a1, b2) + dot(a2, b1))) * inverse
-            high_ref[at], low_ref[at] = split2(y)
-            above.append(at)
-            found.append(column * inverse)
-            at += 1
-        level, columns = above, found
-    root_ref[...] = y
+    assert (steps - 1) % unrolled == 0
+    lax.fori_loop(0, (steps - 1) // unrolled, several, 0)
+    columns = [column_ref[c : c + 1, :] for c in range(count)]
+    level, size, base = half * count, count, chunks
+    while size > 1:
+        found = []
+        for i in range(size // 2):
+            to = base + half * (size // 2) + i
+            _, column = join(high_ref, low_ref, level + 2 * i, level + 2 * i + 1, to, columns[2 * i])
+            found.append(column)
+        level = base + half * (size // 2)
+        base += size
+        size //= 2
+        columns = found
+    return columns[0]
+
+
+def join(high_ref, low_ref, left, right, to, column):
+    a1, a2 = high_ref[left], low_ref[left]
+    b1, b2 = high_ref[right], low_ref[right]
+    column = dot(jnp.broadcast_to(column, (16, column.shape[1])).astype(bf16), b1)[0:1]
+    inverse = 1.0 / jnp.sum(column, axis=1, keepdims=True)
+    y = (dot(a1, b1) + (dot(a1, b2) + dot(a2, b1))) * inverse
+    high_ref[to], low_ref[to] = split2(y)
+    return y, column * inverse
+
+
+def split_kernel(scal_ref, own_ref, recv_ref, ids_ref, given_ref):
+    half = own_ref.shape[0] // 2
+    width = ids_ref.shape[1]
+    at = pl.ds(pl.multiple_of((1 - scal_ref[3]) * half, half), half)
+    given_ref[0:half, :] = own_ref[at, :] + recv_ref[at, :]
+    given_ref[half : half + 8, :] = jnp.zeros((8, own_ref.shape[1]), f32)
+    given_ref[half : half + 1, 0:width] = ids_ref[...].astype(f32)
+
+
+def early_kernel(scal_ref, own_ref, recv_ref, *refs):
+    mats, (w_ref, lead_ref, column_out_ref, high_ref, low_ref, scaled_ref, column_ref, eye_ref) = refs[:6], refs[6:]
+    half = own_ref.shape[0] // 2
+    at = pl.ds(pl.multiple_of(scal_ref[3] * half, half), half)
+    w_ref[...] = own_ref[at, :] + recv_ref[at, :]
+    column_out_ref[...] = half_product(scal_ref[3], scal_ref[0], mats, w_ref, lead_ref, high_ref, low_ref,
+                                       scaled_ref, column_ref, eye_ref)
+
+
+def late_kernel(scal_ref, taken_ref, early_w_ref, early_lead_ref, early_column_ref, init_ref, *refs):
+    mats = refs[:6]
+    (w_ref, lead_ref, high_ref, low_ref, state_ref, msg_ref, root_ref, scaled_ref, column_ref, eye_ref,
+     half_w_ref, half_lead_ref) = refs[8:]
+    half, states = early_w_ref.shape
+    side = scal_ref[3]
+    half_w_ref[...] = taken_ref[0:half, :]
+    column = half_product(1 - side, scal_ref[0], mats, half_w_ref, half_lead_ref, high_ref, low_ref,
+                          scaled_ref, column_ref, eye_ref)
+    for spot, w, lead in ((side, early_w_ref, early_lead_ref), (1 - side, half_w_ref, half_lead_ref)):
+        at = pl.ds(pl.multiple_of(spot * half, half), half)
+        w_ref[at, :] = w[...]
+        lead_ref[at, :] = lead[...]
+    root = 2 * chunks - 2
+    column = jnp.where(side == 0, early_column_ref[...], column)
+    root_ref[...], _ = join(high_ref, low_ref, root - 2, root - 1, root, column)
     init = init_ref[...]
     prior = jnp.broadcast_to(init / jnp.sum(init, axis=1, keepdims=True), (8, states))
     final = jnp.full((8, states), 1.0 / states, f32)
@@ -203,12 +234,12 @@
     carry_over(state, state, high_ref, low_ref, msg_ref)
 
 
-def place(ids_ref, scal_ref, block, turn):
-    frames = ids_ref.shape[1]
+def place(ids, scal_ref, block, turn):
+    frames = ids.shape[1]
     square = (frames, frames)
     bits = block.bit_length() - 1
     down, across = iota(square, 0), iota(square, 1)
-    row = jnp.broadcast_to(ids_ref[0:1, :], square)
+    row = jnp.broadcast_to(ids, square)
     live = across >= scal_ref[0]
     column = jnp.broadcast_to(jnp.sum(jnp.where(down == across, row, 0), axis=1, keepdims=True), square)
     live_column = down >= scal_ref[0]
@@ -226,11 +257,17 @@
     return owner_row[0:1, :], rank_row, fits_row, rank_column, fits_column, local, most
 
 
-def address_kernel(block, scal_ref, turn_ref, ids_ref, pick_ref, meta_ref):
+def address_kernel(block, scal_ref, turn_ref, ids_ref, taken_ref, pick_ref, meta_ref):
     frames = ids_ref.shape[1]
+    half = frames // 2
+    away = taken_ref[half : half + 1, 0:frames].astype(jnp.int32)
+    away = jnp.concatenate([away[:, half:], away[:, :half]], axis=1)
+    lower = iota((1, frames), 1) < half
+    near = (lower & (scal_ref[3] == 0)) | (~lower & (scal_ref[3] == 1))
+    ids = jnp.where(near, ids_ref[...], away)
     lines, states = meta_ref.shape
     turn = turn_ref[0]
-    owner, rank, fits, rank_column, fits_column, local, most = place(ids_ref, scal_ref, block, turn)
+    owner, rank, fits, rank_column, fits_column, local, most = place(ids, scal_ref, block, turn)
     spot = jnp.where(fits, owner * slots + rank, -1)
     across = iota((lines, frames), 0)
     totals = (lax.bitwise_and(across, slots - 1) == rows_sent) & (turn == 0)
@@ -384,10 +421,11 @@
 smem = pl.BlockSpec(memory_space=pltpu.MemorySpace.SMEM)
 
 
-def call(kernel, in_specs, out_specs, out_shape, scratch=(), cost=None):
+def call(kernel, in_specs, out_specs, out_shape, scratch=(), cost=None, aliases=None):
     if cost is not None:
         cost = pl.CostEstimate(flops=cost, bytes_accessed=cost // 100, transcendentals=0)
-    return pl.pallas_call(kernel, cost_estimate=cost, in_specs=in_specs, out_specs=out_specs, out_shape=out_shape,
+    return pl.pallas_call(kernel, cost_estimate=cost,
+                          input_output_aliases=aliases or {}, in_specs=in_specs, out_specs=out_specs, out_shape=out_shape,
                           scratch_shapes=scratch, compiler_params=pltpu.CompilerParams(vmem_limit_bytes=granted))
 
 
@@ -415,13 +453,9 @@
     side = tm_place % 2
     flat = tm_place * emit_count + emit_place
 
-    kept = jnp.where(side == 0, observed[0:1], observed[1:2])
-    given = jnp.where(side == 0, observed[1:2], observed[0:1])
-    taken = lax.ppermute(given, "tm", [(i, i ^ 1) for i in range(tm_count)])
+    ids = observed.reshape(1, frames)
     table = shape(own_rows, states, dtype=bf16)
     tables = call(table_kernel, [vmem], [vmem] * 3, [table] * 3, cost=400_000_000)(emission)
-    taken, tables = lax.optimization_barrier((taken, tables))
-    ids = jnp.where(side == 0, jnp.concatenate([kept, taken], axis=1), jnp.concatenate([taken, kept], axis=1))
     first = jnp.where(side == 0, starts[0], starts[1]) - part * frames
     scal = jnp.stack([first, part, (flat % (states // slots)) * slots, side, emit_place, starts[0], starts[1]])
     scal = scal.astype(jnp.int32)
@@ -431,6 +465,7 @@
 
     near = jnp.concatenate([ids, lax.ppermute(ids, "emit", swaps(1))], axis=0)
     far = [lax.ppermute(near, "emit", swaps(k)) for k in range(2, emit_count, 2)]
+    far, tables = lax.optimization_barrier((far, tables))
     wanted = jnp.concatenate([near] + far, axis=0) - emit_place * own_rows
     half = shape(emit_count // 2, frames, states)
     mine, other = call(gather_kernel, [vmem] * 4, [vmem, vmem], [half, half])(wanted, *tables)
@@ -443,21 +478,32 @@
     came, refined = lax.optimization_barrier((came, refined))
     matrices, exact, sums = refined[:3], refined[3], refined[4]
     nodes = 2 * chunks - 1
+    given = call(split_kernel, [smem] + [vmem] * 3, vmem, shape(frame_count + 8, states))(
+        scal, both_cores[0], came, ids
+    )
+    taken = lax.ppermute(given, "tm", [(i, i ^ 1) for i in range(tm_count)])
+    mats = (transition, *matrices, exact, sums)
+    leaves = shape(nodes, states, states, dtype=bf16)
+    early_rows = shape(frame_count, states)
+    scratch = [pltpu.VMEM((chunks, states), f32)] * 2 + [pltpu.VMEM((states, states), bf16)]
+    early_w, early_lead, early_column, high, low = call(
+        early_kernel, [smem] + [vmem] * 8, [vmem] * 5, [early_rows, early_rows, row, leaves, leaves],
+        scratch, cost=12_000_000_000,
+    )(scal, both_cores[0], came, *mats)
     weights, lead, high, low, state, message, root = call(
-        product_kernel, [smem] + [vmem] * 9, [vmem] * 7,
-        [shape(frames, states), shape(frames, states), shape(nodes, states, states, dtype=bf16),
-         shape(nodes, states, states, dtype=bf16), shape(8, states), shape(8, states),
+        late_kernel, [smem] + [vmem] * 13, [vmem] * 7,
+        [shape(frames, states), shape(frames, states), leaves, leaves, shape(8, states), shape(8, states),
          shape(states, states)],
-        [pltpu.VMEM((chunks, states), f32)] * 2,
-    )(scal, both_cores[0], came, transition, *matrices, exact, sums, initial.reshape(1, states))
+        scratch + [pltpu.VMEM((frame_count, states), f32)] * 2, cost=12_000_000_000, aliases={12: 2, 13: 3},
+    )(scal, taken, early_w, early_lead, early_column, initial.reshape(1, states), *mats, high, low)
 
     def address(turn):
         def kernel(*refs):
             address_kernel(block, *refs)
 
         lines = devices * slots
-        return call(kernel, [smem, smem, vmem], [vmem, vmem],
-                    [shape(lines, frames, dtype=bf16), shape(lines, states)], cost=400_000_000)(scal, turn, ids)
+        return call(kernel, [smem, smem, vmem, vmem], [vmem, vmem],
+                    [shape(lines, frames, dtype=bf16), shape(lines, states)], cost=400_000_000)(scal, turn, ids, taken)
 
     pick, meta = address(jnp.zeros((1,), jnp.int32))
 

time: 85.1 us -> 83.4 us (0.980)
  waiting for transfers between devices: 27.6 us -> 25.4 us
  Pallas kernels: 29.5 us -> 30.9 us
    ppermute x1, waiting for transfers between devices: 1.58 us -> 0.05 us  [update(): lax.ppermute(near, 'emit', swaps(k))]
    pallas_call x2 -> x4, Pallas kernels: 20 us -> 21.4 us  [the longest x1 10.3 us: update(): call(late_kernel, [smem] + [vmem] * 13, [vmem] * 7, [shape(frames, states...]
    ppermute x1, starting transfers between devices: 3 us -> 1.84 us  [update(): taken = lax.ppermute(given, 'tm', [(i, i ^ 1) for i in range(tm_count)])]
    all_to_all x1, starting transfers between devices: 5.15 us -> 4.2 us  [exchange(): lax.all_to_all(sent.reshape(devices, slots, states), both, 0, 0, tiled=True)]
  transfers between devices with their start and end apart: 11 -> 11, of which waited for: 9 -> 8; matrix products, arithmetic and copies ran while one was open for 1% -> 1% of each run, Pallas kernels for 3% -> 14%
where the time goes in v4:
time: 83.4 us; the launch traced here: 83 us
  Pallas kernels  30.9 us (37%)
  waiting for transfers between devices  25.4 us (30%)
  starting transfers between devices  21.2 us (25%)
  local copies, waits for them, and re-layouts  2.69 us (3%)
  between operations  2.12 us (3%)
    pallas_call x1, Pallas kernels, update(): call(late_kernel, [smem] + [vmem] * 13, [vmem] * 7, [shape(frames, states...  10.3 us
    pallas_call x1, Pallas kernels, update(): call(early_kernel, [smem] + [vmem] * 8, [vmem] * 5, [early_rows, early_ro...  9.52 us
    all_to_all x1, waiting for transfers between devices, exchange(): lax.all_to_all(sent.reshape(devices, slots, states), both, 0, 0, tiled=True)  8.8 us
    ppermute x1, waiting for transfers between devices, update(): ahead = lax.ppermute(message, 'tm', end_pairs(parts - 3, 2))  6.23 us
    pallas_call x1, Pallas kernels, update(): call(chain, [smem] + [vmem] * 14, [vmem] * 4, [shape(frame_count, states)...  5.55 us
    ppermute x1, waiting for transfers between devices, update(): other = lax.ppermute(away, 'tm', [(i, i ^ 1) for i in range(tm_count)])  4.97 us
    ppermute x1, starting transfers between devices, update(): recv = lax.ppermute(message, 'tm', relay_pairs(0))  4.56 us
    all_to_all x1, starting transfers between devices, exchange(): lax.all_to_all(sent.reshape(devices, slots, states), both, 0, 0, tiled=True)  4.2 us
  transfers between devices with their start and end apart: 11, of which 8 were waited for; matrix products, arithmetic and copies ran while one was open for 1% of the time, Pallas kernels for 14%

profile of v4, /device:TPU:0, one launch (start us, length us, event | category | flops | bytes accessed | tf_op | source)
XLA Modules:
  0.0 83.0 jit_solution(5510224756458860501)
XLA Ops:
  0.6 0.8 reshape.34.ids_ref.refs_2_
  1.4 0.5 collective-permute-start
  1.9 0.8 collective-permute-done
  2.7 2.8 %collective-permute-start.1 = (s32[2,128]{1,0:T(2,128)S(1)}, s32[2,128]{1,0:T(2,128)S(1)}, u32[]{:S(2)}, u32[]{:S(2)}) collective-permute-start(s32[2,128]{1,0:T(2,128)S(1)} %pad_add_fusion), channel_id=1, source_target_pairs={{0,2},{1,3},{2,0},{3,1},{4,6},{5,7},{6,4},{7,5},{8,10},{9,11},{10,... | collective-permute-start | bytes 3080 | tf_op jit(solution)/shard_map/ppermute | solution.py:467
  5.5 1.2 %copy-done = f32[1024,256]{1,0:T(8,128)S(1)} copy-done((f32[1024,256]{1,0:T(8,128)S(1)}, f32[1024,256]{1,0:T(8,128)}, u32[]{:S(2)}) %copy-start) | copy-done | bytes 1048600
  6.8 0.3 shard_map.76
  7.1 1.1 %shard_map.77 = (f32[2,128,256]{2,1,0:T(8,128)S(1)}, f32[2,128,256]{2,1,0:T(8,128)S(1)}) custom-call(s32[4,128]{1,0:T(4,128)S(1)} %add_subtract_fusion.ids_ref, bf16[1024,256]{1,0:T(8,128)(2,1)S(1)} %get-tuple-element.102.high_ref, bf16[1024,256]{1,0:T(8,128)(2,1)S(1)} %get-tuple-element.103.mid_ref, bf16[1024,256]{1,0:T(8,128)(2,1)S(1)} %get-tuple-element.104.low_ref), custom_call_target="tpu_custom_call" | custom-call | tf_op jit(solution)/shard_map/pallas_call | solution.py:471
  8.3 1.5 %collective-permute-done.2 = f32[2,128,256]{2,1,0:T(8,128)S(1)} collective-permute-done((f32[2,128,256]{2,1,0:T(8,128)S(1)}, f32[2,128,256]{2,1,0:T(8,128)S(1)}, u32[]{:S(2)}, u32[]{:S(2)}) %collective-permute-start.2) | collective-permute-done | bytes 262176 | tf_op jit(solution)/shard_map/ppermute | solution.py:472
  9.9 2.1 %collective-permute-start.3 = (f32[128,256]{1,0:T(8,128)S(1)}, f32[128,256]{1,0:T(8,128)S(1)}, u32[]{:S(2)}, u32[]{:S(2)}) collective-permute-start(f32[128,256]{1,0:T(8,128)S(1)} %get-tuple-element.163), channel_id=1, source_target_pairs={{0,2},{1,3},{2,0},{3,1},{4,6},{5,7},{6,4},{7,5},{8,10},{9,11},{10,... | collective-permute-start | bytes 393224 | tf_op jit(solution)/shard_map/ppermute | solution.py:473
  12.0 0.6 fusion
  13.9 0.1 stack.23.scal_ref.refs_0_
  14.0 0.1 shard_map.78
  14.1 1.7 %collective-permute-done.3.recv_ref = f32[128,256]{1,0:T(8,128)S(1)} collective-permute-done((f32[128,256]{1,0:T(8,128)S(1)}, f32[128,256]{1,0:T(8,128)S(1)}, u32[]{:S(2)}, u32[]{:S(2)}) %collective-permute-start.3) | collective-permute-done | bytes 131104 | tf_op jit(solution)/shard_map/ppermute | solution.py:473
  15.8 0.6 shard_map.79
  16.3 1.8 %collective-permute-start.4 = (f32[72,256]{1,0:T(8,128)S(1)}, f32[72,256]{1,0:T(8,128)S(1)}, u32[]{:S(2)}, u32[]{:S(2)}) collective-permute-start(f32[72,256]{1,0:T(8,128)S(1)} %shard_map.79), channel_id=1, source_target_pairs={{0,4},{4,0},{8,12},{12,8},{16,20},{20,16},{24,28},{28,24},{1,5},{5... | collective-permute-start | bytes 221192 | tf_op jit(solution)/shard_map/ppermute | solution.py:484
  18.2 9.5 %shard_map.80 = (f32[64,256]{1,0:T(8,128)S(1)}, f32[64,256]{1,0:T(8,128)S(1)}, f32[1,256]{1,0:T(1,128)S(1)}, bf16[15,256,256]{2,1,0:T(8,128)(2,1)S(1)}, bf16[15,256,256]{2,1,0:T(8,128)(2,1)S(1)}) custom-call(s32[7]{0:T(128)S(1)} %stack.23.scal_ref.refs_0_, f32[128,256]{1,0:T(8,128)S(1)} %get-tuple-element.164.own_ref, ...), custom_call_target="tpu_custom_call" | custom-call | flops 12000000000 | bytes 120000000 | tf_op jit(solution)/shard_map/pallas_call | solution.py:489
  27.7 10.3 %shard_map.81 = (f32[128,256]{1,0:T(8,128)S(1)}, f32[128,256]{1,0:T(8,128)S(1)}, bf16[15,256,256]{2,1,0:T(8,128)(2,1)S(1)}, bf16[15,256,256]{2,1,0:T(8,128)(2,1)...) custom-call(s32[7]{0:T(128)S(1)} %stack.23.scal_ref.refs_0_, ...), custom_call_target="tpu_custom_call", output_to_operand_aliasing={{2}: (12, {}), {3}: (13, {})} | custom-call | flops 12000000000 | bytes 120000000 | tf_op jit(solution)/shard_map/pallas_call | solution.py:493
  38.0 1.3 %collective-permute-start.8 = (f32[256,256]{1,0:T(8,128)S(1)}, f32[256,256]{1,0:T(8,128)S(1)}, u32[]{:S(2)}, u32[]{:S(2)}) collective-permute-start(f32[256,256]{1,0:T(8,128)S(1)} %get-tuple-element.129), channel_id=1, source_target_pairs={{16,24},{8,0},{20,28},{12,4},{17,25},{9,1},{21,29},{13,5},{18,26},... | collective-permute-start | bytes 786440 | tf_op jit(solution)/shard_map/ppermute | solution.py:522
  39.3 4.6 %collective-permute-start.5 = (f32[8,256]{1,0:T(8,128)S(1)}, f32[8,256]{1,0:T(8,128)S(1)}, u32[]{:S(2)}, u32[]{:S(2)}) collective-permute-start(f32[8,256]{1,0:T(8,128)S(1)} %get-tuple-element.124), channel_id=1, source_target_pairs={{0,8},{24,16},{4,12},{28,20},{1,9},{25,17},{5,13},{29,21},{2,10},{... | collective-permute-start | bytes 24584 | tf_op jit(solution)/shard_map/ppermute | solution.py:521
  43.9 1.3 %collective-permute-done.5.refs_2_ = f32[8,256]{1,0:T(8,128)S(1)} collective-permute-done((f32[8,256]{1,0:T(8,128)S(1)}, f32[8,256]{1,0:T(8,128)S(1)}, u32[]{:S(2)}, u32[]{:S(2)}) %collective-permute-start.5) | collective-permute-done | bytes 8224 | tf_op jit(solution)/shard_map/ppermute | solution.py:521
  45.3 0.8 shard_map.82
  46.1 0.7 collective-permute-start.6
  46.8 1.3 %collective-permute-start.7 = (f32[8,256]{1,0:T(8,128)S(1)}, f32[8,256]{1,0:T(8,128)S(1)}, u32[]{:S(2)}, u32[]{:S(2)}) collective-permute-start(f32[8,256]{1,0:T(8,128)S(1)} %get-tuple-element.128), channel_id=1, source_target_pairs={{8,24},{16,0},{12,28},{20,4},{9,25},{17,1},{13,29},{21,5},{10,26},... | collective-permute-start | bytes 24584 | tf_op jit(solution)/shard_map/ppermute | solution.py:531
  48.1 1.0 %shard_map.83 = (bf16[512,128]{1,0:T(8,128)(2,1)S(1)}, f32[512,256]{1,0:T(8,128)S(1)}) custom-call(s32[7]{0:T(128)S(1)} %stack.23.scal_ref.refs_0_, s32[1]{0:T(128)} %constant.62.clone.1.refs_1_, s32[1,128]{1,0:T(1,128)S(1)} %reshape.34.ids_ref.refs_2_, f32[72,256]{1,0:T(8,128)S(1)} %collective-permute-done.4.taken_ref.refs_3_), custom_call_target="tpu_custom_call" | custom-call | flops 400000000 | bytes 4000000 | tf_op jit(solution)/shard_map/pallas_call | solution.py:505
  49.1 6.2 %collective-permute-done.7.refs_3_ = f32[8,256]{1,0:T(8,128)S(1)} collective-permute-done((f32[8,256]{1,0:T(8,128)S(1)}, f32[8,256]{1,0:T(8,128)S(1)}, u32[]{:S(2)}, u32[]{:S(2)}) %collective-permute-start.7) | collective-permute-done | bytes 8224 | tf_op jit(solution)/shard_map/ppermute | solution.py:531
  55.4 5.5 %shard_map.84 = (f32[64,256]{1,0:T(8,128)S(1)}, f32[64,256]{1,0:T(8,128)S(1)}, f32[128,256]{1,0:T(8,128)S(1)}, f32[512,256]{1,0:T(8,128)}) custom-call(s32[7]{0:T(128)S(1)} %stack.23.scal_ref.refs_0_, f32[8,256]{1,0:T(8,128)S(1)} %get-tuple-element.127.refs_1_, f32[8,256]{1,0:T(8,128)S(1)} %collective-permute-done.6.refs_2_, ...), custom_call_target="tpu_custom_call" | custom-call | tf_op jit(solution)/shard_map/pallas_call | solution.py:536
  60.9 4.2 %all-to-all-start.1 = ((f32[32,16,256]{2,1,0:T(8,128)}), f32[32,16,256]{2,1,0:T(8,128)S(1)}, u32[]{:S(2)}, u32[]{:S(2)}) async-start(f32[32,16,256]{2,1,0:T(8,128)} %bitcast.15), calls=%async_computation.1 | async-start | bytes 1048576 | tf_op jit(solution)/shard_map/all_to_all | solution.py:545
  65.1 1.8 %collective-permute-start.9 = (f32[64,256]{1,0:T(8,128)S(1)}, f32[64,256]{1,0:T(8,128)S(1)}, u32[]{:S(2)}, u32[]{:S(2)}) collective-permute-start(f32[64,256]{1,0:T(8,128)S(1)} %get-tuple-element.136), channel_id=1, source_target_pairs={{0,4},{4,0},{8,12},{12,8},{16,20},{20,16},{24,28},{28,24},{1,5},{5... | collective-permute-start | bytes 196616 | tf_op jit(solution)/shard_map/ppermute | solution.py:542
  67.0 5.0 %collective-permute-done.9.refs_3_ = f32[64,256]{1,0:T(8,128)S(1)} collective-permute-done((f32[64,256]{1,0:T(8,128)S(1)}, f32[64,256]{1,0:T(8,128)S(1)}, u32[]{:S(2)}, u32[]{:S(2)}) %collective-permute-start.9) | collective-permute-done | bytes 65568 | tf_op jit(solution)/shard_map/ppermute | solution.py:542
  71.9 8.8 %all-to-all-done.1 = f32[32,16,256]{2,1,0:T(8,128)S(1)} async-done(((f32[32,16,256]{2,1,0:T(8,128)}), f32[32,16,256]{2,1,0:T(8,128)S(1)}, u32[]{:S(2)}, u32[]{:S(2)}) %all-to-all-start.1) | async-done | bytes 524320 | tf_op jit(solution)/shard_map/all_to_all | solution.py:545
  80.7 1.6 %shard_map.85 = (f32[2,64,256]{2,1,0:T(8,128)}, f32[128,256]{1,0:T(8,128)}, f32[2]{0:T(128)}, f32[128,256]{1,0:T(8,128)S(1)}, f32[1,256]{1,0:T(1,128)S(1)}, /*index=5*/s32[1]{0:T(128)}) custom-call(s32[7]{0:T(128)S(1)} %stack.23.scal_ref.refs_0_, f32[512,256]{1,0:T(8,128)S(1)} %bitcast.29, f32[64,256]{1,0:T(8,128)S(1)} %get-tuple-element.135.refs_2_, ...), custom_call_target="tpu_custom_call" | custom-call | tf_op jit(solution)/shard_map/pallas_call | solution.py:551
  82.3 0.7 while.12
  (16 shorter events, 0.2 us)
Async XLA Ops:
  1.4 1.3 %collective-permute-start = (s32[1,128]{1,0:T(1,128)S(1)}, s32[1,128]{1,0:T(1,128)S(1)}, u32[]{:S(2)}, u32[]{:S(2)}) collective-permute-start(s32[1,128]{1,0:T(1,128)S(1)} %reshape.34.ids_ref.refs_2_), channel_id=1, source_target_pairs={{0,1},{1,0},{2,3},{3,2},{4,5},{5,4},{6,7},{7,6},{8,9},{9,8},{10,11... | collective-permute-start | bytes 1544 | tf_op jit(solution)/shard_map/ppermute | solution.py:466
  2.7 4.4 %collective-permute-start.1 = (s32[2,128]{1,0:T(2,128)S(1)}, s32[2,128]{1,0:T(2,128)S(1)}, u32[]{:S(2)}, u32[]{:S(2)}) collective-permute-start(s32[2,128]{1,0:T(2,128)S(1)} %pad_add_fusion), channel_id=1, source_target_pairs={{0,2},{1,3},{2,0},{3,1},{4,6},{5,7},{6,4},{7,5},{8,10},{9,11},{10,... | collective-permute-start | bytes 3080 | tf_op jit(solution)/shard_map/ppermute | solution.py:467
  5.5 1.2 %copy-start = (f32[1024,256]{1,0:T(8,128)S(1)}, f32[1024,256]{1,0:T(8,128)}, u32[]{:S(2)}) copy-start(f32[1024,256]{1,0:T(8,128)} %table_ref.1) | copy-start | bytes 3145732
  6.8 5.2 %copy-start.3 = (s32[2]{0:T(128)S(1)}, s32[2]{0:T(128)}, u32[]{:S(2)}) copy-start(s32[2]{0:T(128)} %param.8) | copy-start | bytes 28
  6.8 7.2 %copy-start.1 = (f32[256,256]{1,0:T(8,128)S(1)}, f32[256,256]{1,0:T(8,128)}, u32[]{:S(2)}) copy-start(f32[256,256]{1,0:T(8,128)} %refs_0_.3) | copy-start | bytes 786436
  8.2 1.6 %collective-permute-start.2 = (f32[2,128,256]{2,1,0:T(8,128)S(1)}, f32[2,128,256]{2,1,0:T(8,128)S(1)}, u32[]{:S(2)}, u32[]{:S(2)}) collective-permute-start(f32[2,128,256]{2,1,0:T(8,128)S(1)} %get-tuple-element.106), channel_id=1, source_target_pairs={{0,1},{1,0},{2,3},{3,2},{4,5},{5,4},{6,7},{7,6},{8,9},{9,8},{10,11... | collective-permute-start | bytes 786440 | tf_op jit(solution)/shard_map/ppermute | solution.py:472
  9.9 5.9 %collective-permute-start.3 = (f32[128,256]{1,0:T(8,128)S(1)}, f32[128,256]{1,0:T(8,128)S(1)}, u32[]{:S(2)}, u32[]{:S(2)}) collective-permute-start(f32[128,256]{1,0:T(8,128)S(1)} %get-tuple-element.163), channel_id=1, source_target_pairs={{0,2},{1,3},{2,0},{3,1},{4,6},{5,7},{6,4},{7,5},{8,10},{9,11},{10,... | collective-permute-start | bytes 393224 | tf_op jit(solution)/shard_map/ppermute | solution.py:473
  16.3 11.4 %copy-start.2 = (f32[256]{0:T(256)S(1)}, f32[256]{0:T(256)}, u32[]{:S(2)}) copy-start(f32[256]{0:T(256)} %param.9) | copy-start | bytes 3076
  16.3 11.4 %collective-permute-start.4 = (f32[72,256]{1,0:T(8,128)S(1)}, f32[72,256]{1,0:T(8,128)S(1)}, u32[]{:S(2)}, u32[]{:S(2)}) collective-permute-start(f32[72,256]{1,0:T(8,128)S(1)} %shard_map.79), channel_id=1, source_target_pairs={{0,4},{4,0},{8,12},{12,8},{16,20},{20,16},{24,28},{28,24},{1,5},{5... | collective-permute-start | bytes 221192 | tf_op jit(solution)/shard_map/ppermute | solution.py:484
  38.0 17.3 %collective-permute-start.8 = (f32[256,256]{1,0:T(8,128)S(1)}, f32[256,256]{1,0:T(8,128)S(1)}, u32[]{:S(2)}, u32[]{:S(2)}) collective-permute-start(f32[256,256]{1,0:T(8,128)S(1)} %get-tuple-element.129), channel_id=1, source_target_pairs={{16,24},{8,0},{20,28},{12,4},{17,25},{9,1},{21,29},{13,5},{18,26},... | collective-permute-start | bytes 786440 | tf_op jit(solution)/shard_map/ppermute | solution.py:522
  39.3 5.9 %collective-permute-start.5 = (f32[8,256]{1,0:T(8,128)S(1)}, f32[8,256]{1,0:T(8,128)S(1)}, u32[]{:S(2)}, u32[]{:S(2)}) collective-permute-start(f32[8,256]{1,0:T(8,128)S(1)} %get-tuple-element.124), channel_id=1, source_target_pairs={{0,8},{24,16},{4,12},{28,20},{1,9},{25,17},{5,13},{29,21},{2,10},{... | collective-permute-start | bytes 24584 | tf_op jit(solution)/shard_map/ppermute | solution.py:521
  46.1 3.1 %collective-permute-start.6 = (f32[8,256]{1,0:T(8,128)S(1)}, f32[8,256]{1,0:T(8,128)S(1)}, u32[]{:S(2)}, u32[]{:S(2)}) collective-permute-start(f32[8,256]{1,0:T(8,128)S(1)} %get-tuple-element.128), channel_id=1, source_target_pairs={{8,16},{16,8},{12,20},{20,12},{9,17},{17,9},{13,21},{21,13},{10,18... | collective-permute-start | bytes 24584 | tf_op jit(solution)/shard_map/ppermute | solution.py:530
  46.8 8.6 %collective-permute-start.7 = (f32[8,256]{1,0:T(8,128)S(1)}, f32[8,256]{1,0:T(8,128)S(1)}, u32[]{:S(2)}, u32[]{:S(2)}) collective-permute-start(f32[8,256]{1,0:T(8,128)S(1)} %get-tuple-element.128), channel_id=1, source_target_pairs={{8,24},{16,0},{12,28},{20,4},{9,25},{17,1},{13,29},{21,5},{10,26},... | collective-permute-start | bytes 24584 | tf_op jit(solution)/shard_map/ppermute | solution.py:531
  60.9 19.8 %all-to-all-start.1 = ((f32[32,16,256]{2,1,0:T(8,128)}), f32[32,16,256]{2,1,0:T(8,128)S(1)}, u32[]{:S(2)}, u32[]{:S(2)}) async-start(f32[32,16,256]{2,1,0:T(8,128)} %bitcast.15), calls=%async_computation.1 | async-start | bytes 1048576 | tf_op jit(solution)/shard_map/all_to_all | solution.py:545
  65.1 6.8 %collective-permute-start.9 = (f32[64,256]{1,0:T(8,128)S(1)}, f32[64,256]{1,0:T(8,128)S(1)}, u32[]{:S(2)}, u32[]{:S(2)}) collective-permute-start(f32[64,256]{1,0:T(8,128)S(1)} %get-tuple-element.136), channel_id=1, source_target_pairs={{0,4},{4,0},{8,12},{12,8},{16,20},{20,16},{24,28},{28,24},{1,5},{5... | collective-permute-start | bytes 196616 | tf_op jit(solution)/shard_map/ppermute | solution.py:542

commit v5 on v4

--- a/solution.py
+++ b/solution.py
@@ -98,16 +98,27 @@
 
 
 def gather_kernel(ids_ref, high_ref, mid_ref, low_ref, mine_ref, other_ref):
-    groups, frames = ids_ref.shape
-    rows = high_ref.shape[0]
-    eye = iota((frames, frames), 0) == iota((frames, frames), 1)
-    lanes = iota((frames, rows), 1)
+    groups, half = ids_ref.shape[0], ids_ref.shape[1] // 2
+    rows, states = high_ref.shape
+    side = lax.rem(lax.axis_index("tm"), 2)
+    eye = iota((half, half), 0) == iota((half, half), 1)
+    lanes = iota((half, rows), 1)
     for k in range(groups):
-        wide = jnp.where(eye, jnp.broadcast_to(ids_ref[k : k + 1, :], (frames, frames)), 0)
-        column = jnp.sum(wide, axis=1, keepdims=True)
-        pick = jnp.where(column == lanes, 1.0, 0.0).astype(bf16)
+        one, two = ids_ref[k : k + 1, 0:half], ids_ref[k : k + 1, half : 2 * half]
+        picks = []
+        for row in (jnp.where(side == 0, one, two), jnp.where(side == 0, two, one)):
+            wide = jnp.where(eye, jnp.broadcast_to(row, (half, half)), 0)
+            column = jnp.sum(wide, axis=1, keepdims=True)
+            picks.append(jnp.where(column == lanes, 1.0, 0.0))
+            if k == 0:
+                away = row
+        pick = jnp.concatenate(picks, axis=0).astype(bf16)
         taken = dot(pick, high_ref[...]) + (dot(pick, mid_ref[...]) + dot(pick, low_ref[...]))
-        (other_ref if k % 2 else mine_ref)[k // 2] = taken
+        out_ref = other_ref if k % 2 else mine_ref
+        out_ref[k // 2, 0 : 2 * half, :] = taken
+        out_ref[k // 2, 2 * half : 2 * half + 8, :] = jnp.zeros((8, states), f32)
+        if k == 0:
+            out_ref[0, 2 * half : 2 * half + 1, 0:half] = away.astype(f32)
 
 
 def half_product(half, first, mats, w_ref, lead_ref, high_ref, low_ref, scaled_ref, column_ref, eye_ref):
@@ -173,31 +184,28 @@
     return y, column * inverse
 
 
-def split_kernel(scal_ref, own_ref, recv_ref, ids_ref, given_ref):
-    half = own_ref.shape[0] // 2
-    width = ids_ref.shape[1]
-    at = pl.ds(pl.multiple_of((1 - scal_ref[3]) * half, half), half)
-    given_ref[0:half, :] = own_ref[at, :] + recv_ref[at, :]
-    given_ref[half : half + 8, :] = jnp.zeros((8, own_ref.shape[1]), f32)
-    given_ref[half : half + 1, 0:width] = ids_ref[...].astype(f32)
-
-
-def early_kernel(scal_ref, own_ref, recv_ref, *refs):
-    mats, (w_ref, lead_ref, column_out_ref, high_ref, low_ref, scaled_ref, column_ref, eye_ref) = refs[:6], refs[6:]
-    half = own_ref.shape[0] // 2
-    at = pl.ds(pl.multiple_of(scal_ref[3] * half, half), half)
-    w_ref[...] = own_ref[at, :] + recv_ref[at, :]
+def early_kernel(count, scal_ref, own_ref, *refs):
+    recv_refs, mats = refs[:count], refs[count : count + 6]
+    w_ref, lead_ref, column_out_ref, high_ref, low_ref, scaled_ref, column_ref, eye_ref = refs[count + 6 :]
+    w = own_ref[0, 0 : w_ref.shape[0], :]
+    for r in recv_refs:
+        w = w + r[...]
+    w_ref[...] = w
     column_out_ref[...] = half_product(scal_ref[3], scal_ref[0], mats, w_ref, lead_ref, high_ref, low_ref,
                                        scaled_ref, column_ref, eye_ref)
 
 
-def late_kernel(scal_ref, taken_ref, early_w_ref, early_lead_ref, early_column_ref, init_ref, *refs):
+def late_kernel(count, scal_ref, taken_ref, early_w_ref, early_lead_ref, early_column_ref, init_ref, *refs):
+    more_refs, refs = refs[:count], refs[count:]
     mats = refs[:6]
     (w_ref, lead_ref, high_ref, low_ref, state_ref, msg_ref, root_ref, scaled_ref, column_ref, eye_ref,
      half_w_ref, half_lead_ref) = refs[8:]
     half, states = early_w_ref.shape
     side = scal_ref[3]
-    half_w_ref[...] = taken_ref[0:half, :]
+    w = taken_ref[0:half, :]
+    for r in more_refs:
+        w = w + r[...]
+    half_w_ref[...] = w
     column = half_product(1 - side, scal_ref[0], mats, half_w_ref, half_lead_ref, high_ref, low_ref,
                           scaled_ref, column_ref, eye_ref)
     for spot, w, lead in ((side, early_w_ref, early_lead_ref), (1 - side, half_w_ref, half_lead_ref)):
@@ -257,14 +265,13 @@
     return owner_row[0:1, :], rank_row, fits_row, rank_column, fits_column, local, most
 
 
-def address_kernel(block, scal_ref, turn_ref, ids_ref, taken_ref, pick_ref, meta_ref):
+def address_kernel(block, own_rows, scal_ref, turn_ref, ids_ref, taken_ref, pick_ref, meta_ref):
     frames = ids_ref.shape[1]
     half = frames // 2
-    away = taken_ref[half : half + 1, 0:frames].astype(jnp.int32)
-    away = jnp.concatenate([away[:, half:], away[:, :half]], axis=1)
-    lower = iota((1, frames), 1) < half
-    near = (lower & (scal_ref[3] == 0)) | (~lower & (scal_ref[3] == 1))
-    ids = jnp.where(near, ids_ref[...], away)
+    first = scal_ref[3] == 0
+    near = jnp.where(first, ids_ref[:, 0:half], ids_ref[:, half:frames])
+    away = taken_ref[half : half + 1, 0:half].astype(jnp.int32) + scal_ref[4] * own_rows
+    ids = jnp.concatenate([jnp.where(first, near, away), jnp.where(first, away, near)], axis=1)
     lines, states = meta_ref.shape
     turn = turn_ref[0]
     owner, rank, fits, rank_column, fits_column, local, most = place(ids, scal_ref, block, turn)
@@ -382,8 +389,8 @@
     return total_rows * (counts + pseudo_count) / (totals + total_rows * pseudo_count)
 
 
-def final_kernel(block, total_rows, emit_count, length, scal_ref, recv_ref, keep_ref, other_ref,
-                 post_ref, new_ref, log_ref, counts_ref, totals_ref, most_ref):
+def final_kernel(block, total_rows, emit_count, length, scal_ref, recv_ref, new_ref, log_ref,
+                 counts_ref, totals_ref, most_ref):
     states = recv_ref.shape[1]
     counts, totals, metas = counted(recv_ref, block)
     counts_ref[...] = counts
@@ -403,6 +410,9 @@
     most_ref[0] = most.astype(jnp.int32)
     for j in range(2):
         log_ref[j] = sums[j] / (length - scal_ref[5 + j]).astype(f32)
+
+
+def posterior_kernel(scal_ref, keep_ref, other_ref, post_ref):
     side = scal_ref[3]
     post_ref[side] = keep_ref[...]
     post_ref[1 - side] = other_ref[...]
@@ -467,39 +477,48 @@
     far = [lax.ppermute(near, "emit", swaps(k)) for k in range(2, emit_count, 2)]
     far, tables = lax.optimization_barrier((far, tables))
     wanted = jnp.concatenate([near] + far, axis=0) - emit_place * own_rows
-    half = shape(emit_count // 2, frames, states)
-    mine, other = call(gather_kernel, [vmem] * 4, [vmem, vmem], [half, half])(wanted, *tables)
-    both_cores = mine + lax.ppermute(other, "emit", swaps(1))
-    came = [lax.ppermute(both_cores[k // 2], "emit", swaps(k)) for k in range(2, emit_count, 2)]
-    came = sum(came[1:], came[0])
+    gathered = shape(emit_count // 2, frames + 8, states)
+    mine, other = call(gather_kernel, [vmem] * 4, [vmem, vmem], [gathered] * 2)(wanted, *tables)
+    summed = mine + lax.ppermute(other, "emit", swaps(1))
+    came, more = [], []
+    for k in range(2, emit_count, 2):
+        came.append(lax.ppermute(summed[k // 2, 0:frame_count], "emit", swaps(k)))
+    taken = lax.ppermute(summed[0, frame_count:], "tm", [(i, i ^ 1) for i in range(tm_count)])
+    for k in range(2, emit_count, 2):
+        pairs = [(i, (i // emit_count ^ 1) * emit_count + (i % emit_count ^ k)) for i in range(devices)]
+        more.append(lax.ppermute(summed[k // 2, frame_count:frames], both, pairs))
     narrow = shape(states, states, dtype=bf16)
     row = shape(1, states)
     refined = call(matrix_kernel, [vmem], [vmem] * 5, [narrow] * 3 + [row] * 2, cost=400_000_000)(transition)
     came, refined = lax.optimization_barrier((came, refined))
     matrices, exact, sums = refined[:3], refined[3], refined[4]
     nodes = 2 * chunks - 1
-    given = call(split_kernel, [smem] + [vmem] * 3, vmem, shape(frame_count + 8, states))(
-        scal, both_cores[0], came, ids
-    )
-    taken = lax.ppermute(given, "tm", [(i, i ^ 1) for i in range(tm_count)])
+    count = len(came)
+
+    def early(*refs):
+        early_kernel(count, *refs)
+
+    def late(*refs):
+        late_kernel(count, *refs)
+
     mats = (transition, *matrices, exact, sums)
     leaves = shape(nodes, states, states, dtype=bf16)
     early_rows = shape(frame_count, states)
     scratch = [pltpu.VMEM((chunks, states), f32)] * 2 + [pltpu.VMEM((states, states), bf16)]
     early_w, early_lead, early_column, high, low = call(
-        early_kernel, [smem] + [vmem] * 8, [vmem] * 5, [early_rows, early_rows, row, leaves, leaves],
+        early, [smem] + [vmem] * (7 + count), [vmem] * 5, [early_rows, early_rows, row, leaves, leaves],
         scratch, cost=12_000_000_000,
-    )(scal, both_cores[0], came, *mats)
+    )(scal, summed, *came, *mats)
     weights, lead, high, low, state, message, root = call(
-        late_kernel, [smem] + [vmem] * 13, [vmem] * 7,
+        late, [smem] + [vmem] * (13 + count), [vmem] * 7,
         [shape(frames, states), shape(frames, states), leaves, leaves, shape(8, states), shape(8, states),
          shape(states, states)],
-        scratch + [pltpu.VMEM((frame_count, states), f32)] * 2, cost=12_000_000_000, aliases={12: 2, 13: 3},
-    )(scal, taken, early_w, early_lead, early_column, initial.reshape(1, states), *mats, high, low)
+        scratch + [pltpu.VMEM((frame_count, states), f32)] * 2, cost=12_000_000_000, aliases={12 + count: 2, 13 + count: 3},
+    )(scal, taken, early_w, early_lead, early_column, initial.reshape(1, states), *more, *mats, high, low)
 
     def address(turn):
         def kernel(*refs):
-            address_kernel(block, *refs)
+            address_kernel(block, own_rows, *refs)
 
         lines = devices * slots
         return call(kernel, [smem, smem, vmem, vmem], [vmem, vmem],
@@ -548,11 +567,13 @@
     def final(*refs):
         final_kernel(block, total_rows, emit_count, length, *refs)
 
-    posterior, new_emission, loglik, counts, totals, most = call(
-        final, [smem, vmem, vmem, vmem], [vmem, vmem, smem, vmem, vmem, smem],
-        [shape(2, frame_count, states), shape(block, states), shape(2), shape(block, states), shape(1, states),
-         shape(1, dtype=jnp.int32)],
-    )(scal, exchange(send), keep, other)
+    sent = exchange(send)
+    posterior = call(posterior_kernel, [smem, vmem, vmem], vmem, shape(2, frame_count, states),
+                     cost=100_000_000)(scal, keep, other)
+    new_emission, loglik, counts, totals, most = call(
+        final, [smem, vmem], [vmem, smem, vmem, vmem, smem],
+        [shape(block, states), shape(2), shape(block, states), shape(1, states), shape(1, dtype=jnp.int32)],
+    )(scal, sent)
 
     def another(carried):
         turn, counts, _ = carried

time: 83.4 us -> 82.6 us (level)
  waiting for transfers between devices: 25.4 us -> 22.3 us
  starting transfers between devices: 21.2 us -> 22.4 us
  Pallas kernels: 30.9 us -> 31.9 us
    ppermute x3 -> x4, waiting for transfers between devices: 3.18 us -> 1.12 us  [the longest x1 1.11 us: update(): came.append(lax.ppermute(summed[k // 2, 0:frame_count], 'emit', swaps(k)))]
    all_to_all x1, starting transfers between devices: 4.2 us -> 5.68 us  [exchange(): lax.all_to_all(sent.reshape(devices, slots, states), both, 0, 0, tiled=True)]
    all_to_all x1, waiting for transfers between devices: 8.8 us -> 7.6 us  [exchange(): lax.all_to_all(sent.reshape(devices, slots, states), both, 0, 0, tiled=True)]
    pallas_call x5, Pallas kernels: 23.1 us -> 24.1 us  [the longest x1 10.4 us: update(): call(late, [smem] + [vmem] * (13 + count), [vmem] * 7, [shape(frames, sta...]
    ppermute x3 -> x4, starting transfers between devices: 4 us -> 3.75 us  [the longest x1 2.09 us: update(): came.append(lax.ppermute(summed[k // 2, 0:frame_count], 'emit', swaps(k)))]
  transfers between devices with their start and end apart: 11 -> 12, of which waited for: 8 -> 7; matrix products, arithmetic and copies ran while one was open for 1% -> 1% of each run, Pallas kernels for 14% -> 16%
where the time goes in v5:
time: 82.6 us; the launch traced here: 82.3 us
  Pallas kernels  31.9 us (39%)
  starting transfers between devices  22.4 us (27%)
  waiting for transfers between devices  22.3 us (27%)
  local copies, waits for them, and re-layouts  2.69 us (3%)
  between operations  2.14 us (3%)
    pallas_call x1, Pallas kernels, update(): call(late, [smem] + [vmem] * (13 + count), [vmem] * 7, [shape(frames, sta...  10.4 us
    pallas_call x1, Pallas kernels, update(): call(early, [smem] + [vmem] * (7 + count), [vmem] * 5, [early_rows, early...  9.63 us
    all_to_all x1, waiting for transfers between devices, exchange(): lax.all_to_all(sent.reshape(devices, slots, states), both, 0, 0, tiled=True)  7.6 us
    ppermute x1, waiting for transfers between devices, update(): ahead = lax.ppermute(message, 'tm', end_pairs(parts - 3, 2))  6.41 us
    all_to_all x1, starting transfers between devices, exchange(): lax.all_to_all(sent.reshape(devices, slots, states), both, 0, 0, tiled=True)  5.68 us
    pallas_call x1, Pallas kernels, update(): call(chain, [smem] + [vmem] * 14, [vmem] * 4, [shape(frame_count, states)...  5.55 us
    ppermute x1, waiting for transfers between devices, update(): other = lax.ppermute(away, 'tm', [(i, i ^ 1) for i in range(tm_count)])  4.97 us
    ppermute x1, starting transfers between devices, update(): recv = lax.ppermute(message, 'tm', relay_pairs(0))  4.56 us
  transfers between devices with their start and end apart: 12, of which 7 were waited for; matrix products, arithmetic and copies ran while one was open for 1% of the time, Pallas kernels for 16%

profile of v5, /device:TPU:0, one launch (start us, length us, event | category | flops | bytes accessed | tf_op | source)
XLA Modules:
  0.0 82.3 jit_solution(2136304678317405729)
XLA Ops:
  0.6 0.8 reshape.34.refs_2_
  1.4 0.5 collective-permute-start
  1.9 0.8 collective-permute-done
  2.7 2.8 %collective-permute-start.1 = (s32[2,128]{1,0:T(2,128)S(1)}, s32[2,128]{1,0:T(2,128)S(1)}, u32[]{:S(2)}, u32[]{:S(2)}) collective-permute-start(s32[2,128]{1,0:T(2,128)S(1)} %pad_add_fusion), channel_id=1, source_target_pairs={{0,2},{1,3},{2,0},{3,1},{4,6},{5,7},{6,4},{7,5},{8,10},{9,11},{10,... | collective-permute-start | bytes 3080 | tf_op jit(solution)/shard_map/ppermute | solution.py:477
  5.5 1.2 %copy-done = f32[1024,256]{1,0:T(8,128)S(1)} copy-done((f32[1024,256]{1,0:T(8,128)S(1)}, f32[1024,256]{1,0:T(8,128)}, u32[]{:S(2)}) %copy-start) | copy-done | bytes 1048600
  6.8 0.3 shard_map.76
  7.1 1.2 %shard_map.77 = (f32[2,136,256]{2,1,0:T(8,128)S(1)}, f32[2,136,256]{2,1,0:T(8,128)S(1)}) custom-call(s32[4,128]{1,0:T(4,128)S(1)} %add_subtract_fusion.ids_ref, bf16[1024,256]{1,0:T(8,128)(2,1)S(1)} %get-tuple-element.101.high_ref, bf16[1024,256]{1,0:T(8,128)(2,1)S(1)} %get-tuple-element.102.mid_ref, bf16[1024,256]{1,0:T(8,128)(2,1)S(1)} %get-tuple-element.103.low_ref), custom_call_target="tpu_custom_call" | custom-call | tf_op jit(solution)/shard_map/pallas_call | solution.py:481
  8.4 0.6 fusion
  10.3 0.1 stack.23.refs_0_.scal_ref
  10.4 0.1 shard_map.78
  10.6 2.1 %collective-permute-start.4 = (f32[64,256]{1,0:T(8,128)S(1)}, f32[64,256]{1,0:T(8,128)S(1)}, u32[]{:S(2)}, u32[]{:S(2)}) collective-permute-start(f32[64,256]{1,0:T(8,128)S(1)} %get-tuple-element.162), channel_id=1, source_target_pairs={{0,2},{1,3},{2,0},{3,1},{4,6},{5,7},{6,4},{7,5},{8,10},{9,11},{10,... | collective-permute-start | bytes 196616 | tf_op jit(solution)/shard_map/ppermute | solution.py:485
  12.7 1.5 %collective-permute-start.5 = (f32[64,256]{1,0:T(8,128)S(1)}, f32[64,256]{1,0:T(8,128)S(1)}, u32[]{:S(2)}, u32[]{:S(2)}) collective-permute-start(f32[64,256]{1,0:T(8,128)S(1)} %get-tuple-element.161), channel_id=1, source_target_pairs={{0,6},{1,7},{2,4},{3,5},{4,2},{5,3},{6,0},{7,1},{8,14},{9,15},{10,... | collective-permute-start | bytes 196616 | tf_op jit(solution)/shard_map/ppermute | solution.py:489
  14.2 0.1 collective-permute-start.3
  14.3 1.1 %collective-permute-done.4.refs_2_ = f32[64,256]{1,0:T(8,128)S(1)} collective-permute-done((f32[64,256]{1,0:T(8,128)S(1)}, f32[64,256]{1,0:T(8,128)S(1)}, u32[]{:S(2)}, u32[]{:S(2)}) %collective-permute-start.4) | collective-permute-done | bytes 65568 | tf_op jit(solution)/shard_map/ppermute | solution.py:485
  15.4 9.6 %shard_map.79 = (f32[64,256]{1,0:T(8,128)S(1)}, f32[64,256]{1,0:T(8,128)S(1)}, f32[1,256]{1,0:T(1,128)S(1)}, bf16[15,256,256]{2,1,0:T(8,128)(2,1)S(1)}, bf16[15,256,256]{2,1,0:T(8,128)(2,1)S(1)}) custom-call(s32[7]{0:T(128)S(1)} %stack.23.refs_0_.scal_ref, f32[2,136,256]{2,1,0:T(8,128)S(1)} %add.34.refs_1_, f32[64,256]{1,0:T(8,128)S(1)} %collective-permute-done.4.refs_2_, ...), custom_call_target="tpu_custom_call" | custom-call | flops 12000000000 | bytes 120000000 | tf_op jit(solution)/shard_map/pallas_call | solution.py:508
  25.1 10.4 %shard_map.80 = (f32[128,256]{1,0:T(8,128)S(1)}, f32[128,256]{1,0:T(8,128)S(1)}, bf16[15,256,256]{2,1,0:T(8,128)(2,1)S(1)}, bf16[15,256,256]{2,1,0:T(8,128)(2,1)...) custom-call(s32[7]{0:T(128)S(1)} %stack.23.refs_0_.scal_ref, ...), custom_call_target="tpu_custom_call", output_to_operand_aliasing={{2}: (13, {}), {3}: (14, {})} | custom-call | flops 12000000000 | bytes 120000000 | tf_op jit(solution)/shard_map/pallas_call | solution.py:512
  35.5 1.3 %collective-permute-start.9 = (f32[256,256]{1,0:T(8,128)S(1)}, f32[256,256]{1,0:T(8,128)S(1)}, u32[]{:S(2)}, u32[]{:S(2)}) collective-permute-start(f32[256,256]{1,0:T(8,128)S(1)} %get-tuple-element.128), channel_id=1, source_target_pairs={{16,24},{8,0},{20,28},{12,4},{17,25},{9,1},{21,29},{13,5},{18,26},... | collective-permute-start | bytes 786440 | tf_op jit(solution)/shard_map/ppermute | solution.py:541
  36.8 4.6 %collective-permute-start.6 = (f32[8,256]{1,0:T(8,128)S(1)}, f32[8,256]{1,0:T(8,128)S(1)}, u32[]{:S(2)}, u32[]{:S(2)}) collective-permute-start(f32[8,256]{1,0:T(8,128)S(1)} %get-tuple-element.123), channel_id=1, source_target_pairs={{0,8},{24,16},{4,12},{28,20},{1,9},{25,17},{5,13},{29,21},{2,10},{... | collective-permute-start | bytes 24584 | tf_op jit(solution)/shard_map/ppermute | solution.py:540
  41.4 1.3 %collective-permute-done.6.refs_2_ = f32[8,256]{1,0:T(8,128)S(1)} collective-permute-done((f32[8,256]{1,0:T(8,128)S(1)}, f32[8,256]{1,0:T(8,128)S(1)}, u32[]{:S(2)}, u32[]{:S(2)}) %collective-permute-start.6) | collective-permute-done | bytes 8224 | tf_op jit(solution)/shard_map/ppermute | solution.py:540
  42.7 0.8 shard_map.81
  43.6 0.7 collective-permute-start.7
  44.3 1.3 %collective-permute-start.8 = (f32[8,256]{1,0:T(8,128)S(1)}, f32[8,256]{1,0:T(8,128)S(1)}, u32[]{:S(2)}, u32[]{:S(2)}) collective-permute-start(f32[8,256]{1,0:T(8,128)S(1)} %get-tuple-element.127), channel_id=1, source_target_pairs={{8,24},{16,0},{12,28},{20,4},{9,25},{17,1},{13,29},{21,5},{10,26},... | collective-permute-start | bytes 24584 | tf_op jit(solution)/shard_map/ppermute | solution.py:550
  45.6 1.1 %shard_map.82 = (bf16[512,128]{1,0:T(8,128)(2,1)S(1)}, f32[512,256]{1,0:T(8,128)S(1)}) custom-call(s32[7]{0:T(128)S(1)} %stack.23.refs_0_.scal_ref, s32[1]{0:T(128)} %constant.62.clone.1.refs_1_, s32[1,128]{1,0:T(1,128)S(1)} %reshape.34.refs_2_, f32[72,256]{1,0:T(8,128)S(1)} %collective-permute-done.3.refs_1_.refs_3_), custom_call_target="tpu_custom_call" | custom-call | flops 400000000 | bytes 4000000 | tf_op jit(solution)/shard_map/pallas_call | solution.py:524
  46.7 6.4 %collective-permute-done.8.refs_3_ = f32[8,256]{1,0:T(8,128)S(1)} collective-permute-done((f32[8,256]{1,0:T(8,128)S(1)}, f32[8,256]{1,0:T(8,128)S(1)}, u32[]{:S(2)}, u32[]{:S(2)}) %collective-permute-start.8) | collective-permute-done | bytes 8224 | tf_op jit(solution)/shard_map/ppermute | solution.py:550
  53.1 5.5 %shard_map.83 = (f32[64,256]{1,0:T(8,128)S(1)}, f32[64,256]{1,0:T(8,128)S(1)}, f32[128,256]{1,0:T(8,128)S(1)}, f32[512,256]{1,0:T(8,128)}) custom-call(s32[7]{0:T(128)S(1)} %stack.23.refs_0_.scal_ref, f32[8,256]{1,0:T(8,128)S(1)} %get-tuple-element.126.refs_1_, f32[8,256]{1,0:T(8,128)S(1)} %collective-permute-done.7.refs_2_, ...), custom_call_target="tpu_custom_call" | custom-call | tf_op jit(solution)/shard_map/pallas_call | solution.py:555
  58.6 5.7 %all-to-all-start.1 = ((f32[32,16,256]{2,1,0:T(8,128)}), f32[32,16,256]{2,1,0:T(8,128)S(1)}, u32[]{:S(2)}, u32[]{:S(2)}) async-start(f32[32,16,256]{2,1,0:T(8,128)} %bitcast.16), calls=%async_computation.1 | async-start | bytes 1048576 | tf_op jit(solution)/shard_map/all_to_all | solution.py:564
  64.3 1.8 %collective-permute-start.10 = (f32[64,256]{1,0:T(8,128)S(1)}, f32[64,256]{1,0:T(8,128)S(1)}, u32[]{:S(2)}, u32[]{:S(2)}) collective-permute-start(f32[64,256]{1,0:T(8,128)S(1)} %get-tuple-element.134), channel_id=1, source_target_pairs={{0,4},{4,0},{8,12},{12,8},{16,20},{20,16},{24,28},{28,24},{1,5},{5... | collective-permute-start | bytes 196616 | tf_op jit(solution)/shard_map/ppermute | solution.py:561
  66.2 5.0 %collective-permute-done.10.other_ref = f32[64,256]{1,0:T(8,128)S(1)} collective-permute-done((f32[64,256]{1,0:T(8,128)S(1)}, f32[64,256]{1,0:T(8,128)S(1)}, u32[]{:S(2)}, u32[]{:S(2)}) %collective-permute-start.10) | collective-permute-done | bytes 65568 | tf_op jit(solution)/shard_map/ppermute | solution.py:561
  71.1 1.2 %shard_map.84 = f32[2,64,256]{2,1,0:T(8,128)} custom-call(s32[7]{0:T(128)S(1)} %stack.23.refs_0_.scal_ref, f32[64,256]{1,0:T(8,128)S(1)} %get-tuple-element.133.keep_ref, f32[64,256]{1,0:T(8,128)S(1)} %collective-permute-done.10.other_ref), custom_call_target="tpu_custom_call" | custom-call | flops 100000000 | bytes 1000000 | tf_op jit(solution)/shard_map/pallas_call | solution.py:571
  72.4 7.6 %all-to-all-done.1 = f32[32,16,256]{2,1,0:T(8,128)S(1)} async-done(((f32[32,16,256]{2,1,0:T(8,128)}), f32[32,16,256]{2,1,0:T(8,128)S(1)}, u32[]{:S(2)}, u32[]{:S(2)}) %all-to-all-start.1) | async-done | bytes 524320 | tf_op jit(solution)/shard_map/all_to_all | solution.py:564
  80.0 1.6 %shard_map.85 = (f32[128,256]{1,0:T(8,128)}, f32[2]{0:T(128)}, f32[128,256]{1,0:T(8,128)S(1)}, f32[1,256]{1,0:T(1,128)S(1)}, s32[1]{0:T(128)}) custom-call(s32[7]{0:T(128)S(1)} %stack.23.refs_0_.scal_ref, f32[512,256]{1,0:T(8,128)S(1)} %bitcast.31), custom_call_target="tpu_custom_call" | custom-call | tf_op jit(solution)/shard_map/pallas_call | solution.py:573
  81.6 0.7 while.12
  (19 shorter events, 0.2 us)
Async XLA Ops:
  0.6 7.8 %copy-start.3 = (s32[2]{0:T(128)S(1)}, s32[2]{0:T(128)}, u32[]{:S(2)}) copy-start(s32[2]{0:T(128)} %param.8) | copy-start | bytes 28
  1.4 1.3 %collective-permute-start = (s32[1,128]{1,0:T(1,128)S(1)}, s32[1,128]{1,0:T(1,128)S(1)}, u32[]{:S(2)}, u32[]{:S(2)}) collective-permute-start(s32[1,128]{1,0:T(1,128)S(1)} %reshape.34.refs_2_), channel_id=1, source_target_pairs={{0,1},{1,0},{2,3},{3,2},{4,5},{5,4},{6,7},{7,6},{8,9},{9,8},{10,11... | collective-permute-start | bytes 1544 | tf_op jit(solution)/shard_map/ppermute | solution.py:476
  2.7 4.4 %collective-permute-start.1 = (s32[2,128]{1,0:T(2,128)S(1)}, s32[2,128]{1,0:T(2,128)S(1)}, u32[]{:S(2)}, u32[]{:S(2)}) collective-permute-start(s32[2,128]{1,0:T(2,128)S(1)} %pad_add_fusion), channel_id=1, source_target_pairs={{0,2},{1,3},{2,0},{3,1},{4,6},{5,7},{6,4},{7,5},{8,10},{9,11},{10,... | collective-permute-start | bytes 3080 | tf_op jit(solution)/shard_map/ppermute | solution.py:477
  5.5 1.2 %copy-start = (f32[1024,256]{1,0:T(8,128)S(1)}, f32[1024,256]{1,0:T(8,128)}, u32[]{:S(2)}) copy-start(f32[1024,256]{1,0:T(8,128)} %table_ref.1) | copy-start | bytes 3145732
  6.8 3.7 %copy-start.1 = (f32[256,256]{1,0:T(8,128)S(1)}, f32[256,256]{1,0:T(8,128)}, u32[]{:S(2)}) copy-start(f32[256,256]{1,0:T(8,128)} %refs_7_.1) | copy-start | bytes 786436
  8.3 2.2 %collective-permute-start.2 = (f32[2,136,256]{2,1,0:T(8,128)S(1)}, f32[2,136,256]{2,1,0:T(8,128)S(1)}, u32[]{:S(2)}, u32[]{:S(2)}) collective-permute-start(f32[2,136,256]{2,1,0:T(8,128)S(1)} %get-tuple-element.105), channel_id=1, source_target_pairs={{0,1},{1,0},{2,3},{3,2},{4,5},{5,4},{6,7},{7,6},{8,9},{9,8},{10,11... | collective-permute-start | bytes 835592 | tf_op jit(solution)/shard_map/ppermute | solution.py:482
  10.6 4.8 %collective-permute-start.4 = (f32[64,256]{1,0:T(8,128)S(1)}, f32[64,256]{1,0:T(8,128)S(1)}, u32[]{:S(2)}, u32[]{:S(2)}) collective-permute-start(f32[64,256]{1,0:T(8,128)S(1)} %get-tuple-element.162), channel_id=1, source_target_pairs={{0,2},{1,3},{2,0},{3,1},{4,6},{5,7},{6,4},{7,5},{8,10},{9,11},{10,... | collective-permute-start | bytes 196616 | tf_op jit(solution)/shard_map/ppermute | solution.py:485
  12.7 12.3 %collective-permute-start.5 = (f32[64,256]{1,0:T(8,128)S(1)}, f32[64,256]{1,0:T(8,128)S(1)}, u32[]{:S(2)}, u32[]{:S(2)}) collective-permute-start(f32[64,256]{1,0:T(8,128)S(1)} %get-tuple-element.161), channel_id=1, source_target_pairs={{0,6},{1,7},{2,4},{3,5},{4,2},{5,3},{6,0},{7,1},{8,14},{9,15},{10,... | collective-permute-start | bytes 196616 | tf_op jit(solution)/shard_map/ppermute | solution.py:489
  14.2 10.9 %collective-permute-start.3 = (f32[72,256]{1,0:T(8,128)S(1)}, f32[72,256]{1,0:T(8,128)S(1)}, u32[]{:S(2)}, u32[]{:S(2)}) collective-permute-start(f32[72,256]{1,0:T(8,128)S(1)} %slice_bitcast_fusion), channel_id=1, source_target_pairs={{0,4},{4,0},{8,12},{12,8},{16,20},{20,16},{24,28},{28,24},{1,5},{5... | collective-permute-start | bytes 221192 | tf_op jit(solution)/shard_map/ppermute | solution.py:486
  15.4 9.7 %copy-start.2 = (f32[256]{0:T(256)S(1)}, f32[256]{0:T(256)}, u32[]{:S(2)}) copy-start(f32[256]{0:T(256)} %param.9) | copy-start | bytes 3076
  35.5 17.6 %collective-permute-start.9 = (f32[256,256]{1,0:T(8,128)S(1)}, f32[256,256]{1,0:T(8,128)S(1)}, u32[]{:S(2)}, u32[]{:S(2)}) collective-permute-start(f32[256,256]{1,0:T(8,128)S(1)} %get-tuple-element.128), channel_id=1, source_target_pairs={{16,24},{8,0},{20,28},{12,4},{17,25},{9,1},{21,29},{13,5},{18,26},... | collective-permute-start | bytes 786440 | tf_op jit(solution)/shard_map/ppermute | solution.py:541
  36.8 5.9 %collective-permute-start.6 = (f32[8,256]{1,0:T(8,128)S(1)}, f32[8,256]{1,0:T(8,128)S(1)}, u32[]{:S(2)}, u32[]{:S(2)}) collective-permute-start(f32[8,256]{1,0:T(8,128)S(1)} %get-tuple-element.123), channel_id=1, source_target_pairs={{0,8},{24,16},{4,12},{28,20},{1,9},{25,17},{5,13},{29,21},{2,10},{... | collective-permute-start | bytes 24584 | tf_op jit(solution)/shard_map/ppermute | solution.py:540
  43.6 3.1 %collective-permute-start.7 = (f32[8,256]{1,0:T(8,128)S(1)}, f32[8,256]{1,0:T(8,128)S(1)}, u32[]{:S(2)}, u32[]{:S(2)}) collective-permute-start(f32[8,256]{1,0:T(8,128)S(1)} %get-tuple-element.127), channel_id=1, source_target_pairs={{8,16},{16,8},{12,20},{20,12},{9,17},{17,9},{13,21},{21,13},{10,18... | collective-permute-start | bytes 24584 | tf_op jit(solution)/shard_map/ppermute | solution.py:549
  44.3 8.8 %collective-permute-start.8 = (f32[8,256]{1,0:T(8,128)S(1)}, f32[8,256]{1,0:T(8,128)S(1)}, u32[]{:S(2)}, u32[]{:S(2)}) collective-permute-start(f32[8,256]{1,0:T(8,128)S(1)} %get-tuple-element.127), channel_id=1, source_target_pairs={{8,24},{16,0},{12,28},{20,4},{9,25},{17,1},{13,29},{21,5},{10,26},... | collective-permute-start | bytes 24584 | tf_op jit(solution)/shard_map/ppermute | solution.py:550
  58.6 21.3 %all-to-all-start.1 = ((f32[32,16,256]{2,1,0:T(8,128)}), f32[32,16,256]{2,1,0:T(8,128)S(1)}, u32[]{:S(2)}, u32[]{:S(2)}) async-start(f32[32,16,256]{2,1,0:T(8,128)} %bitcast.16), calls=%async_computation.1 | async-start | bytes 1048576 | tf_op jit(solution)/shard_map/all_to_all | solution.py:564
  64.3 6.8 %collective-permute-start.10 = (f32[64,256]{1,0:T(8,128)S(1)}, f32[64,256]{1,0:T(8,128)S(1)}, u32[]{:S(2)}, u32[]{:S(2)}) collective-permute-start(f32[64,256]{1,0:T(8,128)S(1)} %get-tuple-element.134), channel_id=1, source_target_pairs={{0,4},{4,0},{8,12},{12,8},{16,20},{20,16},{24,28},{28,24},{1,5},{5... | collective-permute-start | bytes 196616 | tf_op jit(solution)/shard_map/ppermute | solution.py:561

commit v6 on v5

--- a/solution.py
+++ b/solution.py
@@ -11,7 +11,7 @@
 chunks = 8
 slots = 16
 rows_sent = 14
-unrolled = 3
+unrolled = 5
 granted = 24 << 20
 
 
@@ -447,7 +447,6 @@
     traj_rows, frame_count = observed.shape
     states = transition.shape[0]
     tm_count = lax.axis_size("tm")
-    tm_place = lax.axis_index("tm")
     emit_count = lax.axis_size("emit")
     emit_place = lax.axis_index("emit")
     both = ("tm", "emit")
@@ -459,16 +458,21 @@
     assert traj_rows == 2 and tm_count % 2 == 0
     frames = 2 * frame_count
     parts = tm_count // 2
-    part = tm_place // 2
-    side = tm_place % 2
-    flat = tm_place * emit_count + emit_place
 
     ids = observed.reshape(1, frames)
     table = shape(own_rows, states, dtype=bf16)
     tables = call(table_kernel, [vmem], [vmem] * 3, [table] * 3, cost=400_000_000)(emission)
-    first = jnp.where(side == 0, starts[0], starts[1]) - part * frames
-    scal = jnp.stack([first, part, (flat % (states // slots)) * slots, side, emit_place, starts[0], starts[1]])
-    scal = scal.astype(jnp.int32)
+    scal = starts
+
+    def placed(kernel, *fixed):
+        def run(starts_ref, *refs):
+            tm, emit = lax.axis_index("tm"), lax.axis_index("emit")
+            odd, at = lax.rem(tm, 2), lax.div(tm, 2)
+            base = lax.rem(tm * emit_count + emit, states // slots) * slots
+            spot = (starts_ref[odd] - at * frames, at, base, odd, emit, starts_ref[0], starts_ref[1])
+            kernel(*fixed, spot, *refs)
+
+        return run
 
     def swaps(k):
         return [(i, i ^ k) for i in range(emit_count)]
@@ -495,12 +499,7 @@
     nodes = 2 * chunks - 1
     count = len(came)
 
-    def early(*refs):
-        early_kernel(count, *refs)
-
-    def late(*refs):
-        late_kernel(count, *refs)
-
+    early, late = placed(early_kernel, count), placed(late_kernel, count)
     mats = (transition, *matrices, exact, sums)
     leaves = shape(nodes, states, states, dtype=bf16)
     early_rows = shape(frame_count, states)
@@ -517,9 +516,7 @@
     )(scal, taken, early_w, early_lead, early_column, initial.reshape(1, states), *more, *mats, high, low)
 
     def address(turn):
-        def kernel(*refs):
-            address_kernel(block, own_rows, *refs)
-
+        kernel = placed(address_kernel, block, own_rows)
         lines = devices * slots
         return call(kernel, [smem, smem, vmem, vmem], [vmem, vmem],
                     [shape(lines, frames, dtype=bf16), shape(lines, states)], cost=400_000_000)(scal, turn, ids, taken)
@@ -540,18 +537,14 @@
     recv = lax.ppermute(message, "tm", relay_pairs(0))
     edge = lax.ppermute(root, "tm", end_pairs(parts - 2, 1))
     for turn in range(1, parts - 2):
-        def relay(*refs, turn=turn):
-            relay_kernel(parts, turn, *refs)
-
+        relay = placed(relay_kernel, parts, turn)
         state, message = call(
             relay, [smem] + [vmem] * 4, [vmem] * 2, [shape(8, states), shape(8, states)]
         )(scal, state, recv, high, low)
         recv = lax.ppermute(message, "tm", relay_pairs(turn))
     ahead = lax.ppermute(message, "tm", end_pairs(parts - 3, 2))
 
-    def chain(*refs):
-        chain_kernel(parts, *refs)
-
+    chain = placed(chain_kernel, parts)
     keep, away, occupancy, send = call(
         chain, [smem] + [vmem] * 14, [vmem] * 4,
         [shape(frame_count, states), shape(frame_count, states), shape(frames, states), shape(devices * slots, states)],
@@ -564,11 +557,9 @@
         got = lax.all_to_all(sent.reshape(devices, slots, states), both, 0, 0, tiled=True)
         return got.reshape(devices * slots, states)
 
-    def final(*refs):
-        final_kernel(block, total_rows, emit_count, length, *refs)
-
+    final = placed(final_kernel, block, total_rows, emit_count, length)
     sent = exchange(send)
-    posterior = call(posterior_kernel, [smem, vmem, vmem], vmem, shape(2, frame_count, states),
+    posterior = call(placed(posterior_kernel), [smem, vmem, vmem], vmem, shape(2, frame_count, states),
                      cost=100_000_000)(scal, keep, other)
     new_emission, loglik, counts, totals, most = call(
         final, [smem, vmem], [vmem, smem, vmem, vmem, smem],
@@ -581,7 +572,7 @@
         def more(*refs):
             more_kernel(block, *refs)
 
-        sent = call(pack_kernel, [smem] + [vmem] * 3, vmem, shape(devices * slots, states))(
+        sent = call(placed(pack_kernel), [smem] + [vmem] * 3, vmem, shape(devices * slots, states))(
             scal, *address(turn.reshape(1)), occupancy
         )
         counts = call(more, [vmem, vmem], vmem, shape(block, states))(exchange(sent), counts)

time: 82.6 us -> 80.9 us (0.979)
  between operations: 2.14 us -> 0.79 us
  waiting for transfers between devices: 22.3 us -> 23.5 us
    ppermute x1, waiting for transfers between devices: 0.01 us -> 1.4 us  [update(): summed = mine + lax.ppermute(other, 'emit', swaps(1))]
  transfers between devices with their start and end apart: 12 -> 12, of which waited for: 7 -> 8; matrix products, arithmetic and copies ran while one was open for 1% -> 0% of each run, Pallas kernels for 16% -> 16%
where the time goes in v6:
time: 80.9 us; the launch traced here: 80.6 us
  Pallas kernels  31.1 us (38%)
  waiting for transfers between devices  23.5 us (29%)
  starting transfers between devices  22.4 us (28%)
  local copies, waits for them, and re-layouts  2.01 us (2%)
    pallas_call x1, Pallas kernels, update(): call(late, [smem] + [vmem] * (13 + count), [vmem] * 7, [shape(frames, sta...  9.97 us
    pallas_call x1, Pallas kernels, update(): call(early, [smem] + [vmem] * (7 + count), [vmem] * 5, [early_rows, early...  9.2 us
    all_to_all x1, waiting for transfers between devices, exchange(): lax.all_to_all(sent.reshape(devices, slots, states), both, 0, 0, tiled=True)  7.59 us
    ppermute x1, waiting for transfers between devices, update(): ahead = lax.ppermute(message, 'tm', end_pairs(parts - 3, 2))  6.56 us
    all_to_all x1, starting transfers between devices, exchange(): lax.all_to_all(sent.reshape(devices, slots, states), both, 0, 0, tiled=True)  5.7 us
    pallas_call x1, Pallas kernels, update(): call(chain, [smem] + [vmem] * 14, [vmem] * 4, [shape(frame_count, states)...  5.56 us
    ppermute x1, waiting for transfers between devices, update(): other = lax.ppermute(away, 'tm', [(i, i ^ 1) for i in range(tm_count)])  4.97 us
    ppermute x1, starting transfers between devices, update(): recv = lax.ppermute(message, 'tm', relay_pairs(0))  4.56 us
  transfers between devices with their start and end apart: 12, of which 8 were waited for; matrix products, arithmetic and copies ran while one was open for 0% of the time, Pallas kernels for 16%

profile of v6, /device:TPU:0, one launch (start us, length us, event | category | flops | bytes accessed | tf_op | source)
XLA Modules:
  0.0 80.6 jit_solution(17548325765565434892)
XLA Ops:
  0.6 0.8 reshape.34.refs_1_
  1.4 0.5 collective-permute-start
  1.9 0.8 %collective-permute-done = s32[1,128]{1,0:T(1,128)S(1)} collective-permute-done((s32[1,128]{1,0:T(1,128)S(1)}, s32[1,128]{1,0:T(1,128)S(1)}, u32[]{:S(2)}, u32[]{:S(2)}) %collective-permute-start) | collective-permute-done | bytes 544 | tf_op jit(solution)/shard_map/ppermute | solution.py:480
  2.7 2.8 %collective-permute-start.1 = (s32[2,128]{1,0:T(2,128)S(1)}, s32[2,128]{1,0:T(2,128)S(1)}, u32[]{:S(2)}, u32[]{:S(2)}) collective-permute-start(s32[2,128]{1,0:T(2,128)S(1)} %pad_add_fusion), channel_id=1, source_target_pairs={{0,2},{1,3},{2,0},{3,1},{4,6},{5,7},{6,4},{7,5},{8,10},{9,11},{10,... | collective-permute-start | bytes 3080 | tf_op jit(solution)/shard_map/ppermute | solution.py:481
  5.5 1.2 %copy-done = f32[1024,256]{1,0:T(8,128)S(1)} copy-done((f32[1024,256]{1,0:T(8,128)S(1)}, f32[1024,256]{1,0:T(8,128)}, u32[]{:S(2)}) %copy-start) | copy-done | bytes 1048600
  6.8 0.3 shard_map.76
  7.1 1.2 %shard_map.77 = (f32[2,136,256]{2,1,0:T(8,128)S(1)}, f32[2,136,256]{2,1,0:T(8,128)S(1)}) custom-call(s32[4,128]{1,0:T(4,128)S(1)} %add_subtract_fusion.ids_ref, bf16[1024,256]{1,0:T(8,128)(2,1)S(1)} %get-tuple-element.101.high_ref, bf16[1024,256]{1,0:T(8,128)(2,1)S(1)} %get-tuple-element.102.mid_ref, bf16[1024,256]{1,0:T(8,128)(2,1)S(1)} %get-tuple-element.103.low_ref), custom_call_target="tpu_custom_call" | custom-call | tf_op jit(solution)/shard_map/pallas_call | solution.py:485
  8.3 0.1 collective-permute-start.2
  8.4 0.1 shard_map.78
  8.5 1.4 %collective-permute-done.2 = f32[2,136,256]{2,1,0:T(8,128)S(1)} collective-permute-done((f32[2,136,256]{2,1,0:T(8,128)S(1)}, f32[2,136,256]{2,1,0:T(8,128)S(1)}, u32[]{:S(2)}, u32[]{:S(2)}) %collective-permute-start.2) | collective-permute-done | bytes 278560 | tf_op jit(solution)/shard_map/ppermute | solution.py:486
  10.0 2.1 %collective-permute-start.4 = (f32[64,256]{1,0:T(8,128)S(1)}, f32[64,256]{1,0:T(8,128)S(1)}, u32[]{:S(2)}, u32[]{:S(2)}) collective-permute-start(f32[64,256]{1,0:T(8,128)S(1)} %get-tuple-element.162), channel_id=1, source_target_pairs={{0,2},{1,3},{2,0},{3,1},{4,6},{5,7},{6,4},{7,5},{8,10},{9,11},{10,... | collective-permute-start | bytes 196616 | tf_op jit(solution)/shard_map/ppermute | solution.py:489
  12.1 1.5 %collective-permute-start.5 = (f32[64,256]{1,0:T(8,128)S(1)}, f32[64,256]{1,0:T(8,128)S(1)}, u32[]{:S(2)}, u32[]{:S(2)}) collective-permute-start(f32[64,256]{1,0:T(8,128)S(1)} %get-tuple-element.161), channel_id=1, source_target_pairs={{0,6},{1,7},{2,4},{3,5},{4,2},{5,3},{6,0},{7,1},{8,14},{9,15},{10,... | collective-permute-start | bytes 196616 | tf_op jit(solution)/shard_map/ppermute | solution.py:493
  13.6 0.1 collective-permute-start.3
  13.7 0.8 collective-permute-done.4.refs_1_
  14.5 9.2 %shard_map.79 = (f32[64,256]{1,0:T(8,128)S(1)}, f32[64,256]{1,0:T(8,128)S(1)}, f32[1,256]{1,0:T(1,128)S(1)}, bf16[15,256,256]{2,1,0:T(8,128)(2,1)S(1)}, bf16[15,256,256]{2,1,0:T(8,128)(2,1)S(1)}) custom-call(s32[2]{0:T(128)S(1)} %copy-done.3, f32[2,136,256]{2,1,0:T(8,128)S(1)} %add.20.refs_0_, f32[64,256]{1,0:T(8,128)S(1)} %collective-permute-done.4.refs_1_, ...), custom_call_target="tpu_custom_call" | custom-call | flops 12000000000 | bytes 120000000 | tf_op jit(solution)/shard_map/pallas_call | solution.py:507
  23.7 10.0 %shard_map.80 = (f32[128,256]{1,0:T(8,128)S(1)}, f32[128,256]{1,0:T(8,128)S(1)}, bf16[15,256,256]{2,1,0:T(8,128)(2,1)S(1)}, bf16[15,256,256]{2,1,0:T(8,128)(2,1)...) custom-call(s32[2]{0:T(128)S(1)} %copy-done.3, ...), custom_call_target="tpu_custom_call", output_to_operand_aliasing={{2}: (13, {}), {3}: (14, {})} | custom-call | flops 12000000000 | bytes 120000000 | tf_op jit(solution)/shard_map/pallas_call | solution.py:511
  33.7 1.3 %collective-permute-start.9 = (f32[256,256]{1,0:T(8,128)S(1)}, f32[256,256]{1,0:T(8,128)S(1)}, u32[]{:S(2)}, u32[]{:S(2)}) collective-permute-start(f32[256,256]{1,0:T(8,128)S(1)} %get-tuple-element.128), channel_id=1, source_target_pairs={{16,24},{8,0},{20,28},{12,4},{17,25},{9,1},{21,29},{13,5},{18,26},... | collective-permute-start | bytes 786440 | tf_op jit(solution)/shard_map/ppermute | solution.py:538
  35.0 4.6 %collective-permute-start.6 = (f32[8,256]{1,0:T(8,128)S(1)}, f32[8,256]{1,0:T(8,128)S(1)}, u32[]{:S(2)}, u32[]{:S(2)}) collective-permute-start(f32[8,256]{1,0:T(8,128)S(1)} %get-tuple-element.123), channel_id=1, source_target_pairs={{0,8},{24,16},{4,12},{28,20},{1,9},{25,17},{5,13},{29,21},{2,10},{... | collective-permute-start | bytes 24584 | tf_op jit(solution)/shard_map/ppermute | solution.py:537
  39.6 1.3 %collective-permute-done.6.refs_1_ = f32[8,256]{1,0:T(8,128)S(1)} collective-permute-done((f32[8,256]{1,0:T(8,128)S(1)}, f32[8,256]{1,0:T(8,128)S(1)}, u32[]{:S(2)}, u32[]{:S(2)}) %collective-permute-start.6) | collective-permute-done | bytes 8224 | tf_op jit(solution)/shard_map/ppermute | solution.py:537
  40.9 0.8 %shard_map.81 = (f32[8,256]{1,0:T(8,128)S(1)}, f32[8,256]{1,0:T(8,128)S(1)}) custom-call(s32[2]{0:T(128)S(1)} %copy-done.3, f32[8,256]{1,0:T(8,128)S(1)} %get-tuple-element.122.refs_0_, f32[8,256]{1,0:T(8,128)S(1)} %collective-permute-done.6.refs_1_, bf16[15,256,256]{2,1,0:T(8,128)(2,1)S(1)} %get-tuple-element.124.refs_2_.refs_6_, ...), custom_call_target="tpu_custom_call" | custom-call | tf_op jit(solution)/shard_map/pallas_call | solution.py:541
  41.7 0.7 collective-permute-start.7
  42.5 1.3 %collective-permute-start.8 = (f32[8,256]{1,0:T(8,128)S(1)}, f32[8,256]{1,0:T(8,128)S(1)}, u32[]{:S(2)}, u32[]{:S(2)}) collective-permute-start(f32[8,256]{1,0:T(8,128)S(1)} %get-tuple-element.127), channel_id=1, source_target_pairs={{8,24},{16,0},{12,28},{20,4},{9,25},{17,1},{13,29},{21,5},{10,26},... | collective-permute-start | bytes 24584 | tf_op jit(solution)/shard_map/ppermute | solution.py:545
  43.8 1.1 %shard_map.82 = (bf16[512,128]{1,0:T(8,128)(2,1)S(1)}, f32[512,256]{1,0:T(8,128)S(1)}) custom-call(s32[2]{0:T(128)S(1)} %copy-done.3, s32[1]{0:T(128)} %constant.6.clone.1.refs_0_, s32[1,128]{1,0:T(1,128)S(1)} %reshape.34.refs_1_, f32[72,256]{1,0:T(8,128)S(1)} %collective-permute-done.3.refs_0_.refs_2_), custom_call_target="tpu_custom_call" | custom-call | flops 400000000 | bytes 4000000 | tf_op jit(solution)/shard_map/pallas_call | solution.py:521
  44.9 6.6 %collective-permute-done.8.refs_2_ = f32[8,256]{1,0:T(8,128)S(1)} collective-permute-done((f32[8,256]{1,0:T(8,128)S(1)}, f32[8,256]{1,0:T(8,128)S(1)}, u32[]{:S(2)}, u32[]{:S(2)}) %collective-permute-start.8) | collective-permute-done | bytes 8224 | tf_op jit(solution)/shard_map/ppermute | solution.py:545
  51.4 5.6 %shard_map.83 = (f32[64,256]{1,0:T(8,128)S(1)}, f32[64,256]{1,0:T(8,128)S(1)}, f32[128,256]{1,0:T(8,128)S(1)}, f32[512,256]{1,0:T(8,128)}) custom-call(s32[2]{0:T(128)S(1)} %copy-done.3, f32[8,256]{1,0:T(8,128)S(1)} %get-tuple-element.126.refs_0_, f32[8,256]{1,0:T(8,128)S(1)} %collective-permute-done.7.refs_1_, f32[8,256]{1,0:T(8,128)S(1)} %collective-permute-done.8.refs_2_, ...), custom_call_target="tpu_custom_call" | custom-call | tf_op jit(solution)/shard_map/pallas_call | solution.py:548
  57.0 5.7 %all-to-all-start.1 = ((f32[32,16,256]{2,1,0:T(8,128)}), f32[32,16,256]{2,1,0:T(8,128)S(1)}, u32[]{:S(2)}, u32[]{:S(2)}) async-start(f32[32,16,256]{2,1,0:T(8,128)} %bitcast.9), calls=%async_computation.1 | async-start | bytes 1048576 | tf_op jit(solution)/shard_map/all_to_all | solution.py:557
  62.7 1.8 %collective-permute-start.10 = (f32[64,256]{1,0:T(8,128)S(1)}, f32[64,256]{1,0:T(8,128)S(1)}, u32[]{:S(2)}, u32[]{:S(2)}) collective-permute-start(f32[64,256]{1,0:T(8,128)S(1)} %get-tuple-element.134), channel_id=1, source_target_pairs={{0,4},{4,0},{8,12},{12,8},{16,20},{20,16},{24,28},{28,24},{1,5},{5... | collective-permute-start | bytes 196616 | tf_op jit(solution)/shard_map/ppermute | solution.py:554
  64.5 5.0 %collective-permute-done.10.refs_1_ = f32[64,256]{1,0:T(8,128)S(1)} collective-permute-done((f32[64,256]{1,0:T(8,128)S(1)}, f32[64,256]{1,0:T(8,128)S(1)}, u32[]{:S(2)}, u32[]{:S(2)}) %collective-permute-start.10) | collective-permute-done | bytes 65568 | tf_op jit(solution)/shard_map/ppermute | solution.py:554
  69.5 1.2 %shard_map.84 = f32[2,64,256]{2,1,0:T(8,128)} custom-call(s32[2]{0:T(128)S(1)} %copy-done.3, f32[64,256]{1,0:T(8,128)S(1)} %get-tuple-element.133.refs_0_, f32[64,256]{1,0:T(8,128)S(1)} %collective-permute-done.10.refs_1_), custom_call_target="tpu_custom_call" | custom-call | flops 100000000 | bytes 1000000 | tf_op jit(solution)/shard_map/pallas_call | solution.py:562
  70.7 7.6 %all-to-all-done.1 = f32[32,16,256]{2,1,0:T(8,128)S(1)} async-done(((f32[32,16,256]{2,1,0:T(8,128)}), f32[32,16,256]{2,1,0:T(8,128)S(1)}, u32[]{:S(2)}, u32[]{:S(2)}) %all-to-all-start.1) | async-done | bytes 524320 | tf_op jit(solution)/shard_map/all_to_all | solution.py:557
  78.3 1.6 %shard_map.85 = (f32[128,256]{1,0:T(8,128)}, f32[2]{0:T(128)}, f32[128,256]{1,0:T(8,128)S(1)}, f32[1,256]{1,0:T(1,128)S(1)}, s32[1]{0:T(128)}) custom-call(s32[2]{0:T(128)S(1)} %copy-done.3, f32[512,256]{1,0:T(8,128)S(1)} %bitcast.24), custom_call_target="tpu_custom_call" | custom-call | tf_op jit(solution)/shard_map/pallas_call | solution.py:564
  79.9 0.7 while.12
  (17 shorter events, 0.2 us)
Async XLA Ops:
  1.4 1.3 %collective-permute-start = (s32[1,128]{1,0:T(1,128)S(1)}, s32[1,128]{1,0:T(1,128)S(1)}, u32[]{:S(2)}, u32[]{:S(2)}) collective-permute-start(s32[1,128]{1,0:T(1,128)S(1)} %reshape.34.refs_1_), channel_id=1, source_target_pairs={{0,1},{1,0},{2,3},{3,2},{4,5},{5,4},{6,7},{7,6},{8,9},{9,8},{10,11... | collective-permute-start | bytes 1544 | tf_op jit(solution)/shard_map/ppermute | solution.py:480
  2.7 4.4 %collective-permute-start.1 = (s32[2,128]{1,0:T(2,128)S(1)}, s32[2,128]{1,0:T(2,128)S(1)}, u32[]{:S(2)}, u32[]{:S(2)}) collective-permute-start(s32[2,128]{1,0:T(2,128)S(1)} %pad_add_fusion), channel_id=1, source_target_pairs={{0,2},{1,3},{2,0},{3,1},{4,6},{5,7},{6,4},{7,5},{8,10},{9,11},{10,... | collective-permute-start | bytes 3080 | tf_op jit(solution)/shard_map/ppermute | solution.py:481
  5.5 1.2 %copy-start = (f32[1024,256]{1,0:T(8,128)S(1)}, f32[1024,256]{1,0:T(8,128)}, u32[]{:S(2)}) copy-start(f32[1024,256]{1,0:T(8,128)} %table_ref.1) | copy-start | bytes 3145732
  6.8 1.6 %copy-start.1 = (f32[256,256]{1,0:T(8,128)S(1)}, f32[256,256]{1,0:T(8,128)}, u32[]{:S(2)}) copy-start(f32[256,256]{1,0:T(8,128)} %refs_6_.1) | copy-start | bytes 786436
  7.1 7.4 %copy-start.3 = (s32[2]{0:T(128)S(1)}, s32[2]{0:T(128)}, u32[]{:S(2)}) copy-start(s32[2]{0:T(128)} %starts_ref.13) | copy-start | bytes 28
  8.3 1.6 %collective-permute-start.2 = (f32[2,136,256]{2,1,0:T(8,128)S(1)}, f32[2,136,256]{2,1,0:T(8,128)S(1)}, u32[]{:S(2)}, u32[]{:S(2)}) collective-permute-start(f32[2,136,256]{2,1,0:T(8,128)S(1)} %get-tuple-element.105), channel_id=1, source_target_pairs={{0,1},{1,0},{2,3},{3,2},{4,5},{5,4},{6,7},{7,6},{8,9},{9,8},{10,11... | collective-permute-start | bytes 835592 | tf_op jit(solution)/shard_map/ppermute | solution.py:486
  10.0 4.5 %collective-permute-start.4 = (f32[64,256]{1,0:T(8,128)S(1)}, f32[64,256]{1,0:T(8,128)S(1)}, u32[]{:S(2)}, u32[]{:S(2)}) collective-permute-start(f32[64,256]{1,0:T(8,128)S(1)} %get-tuple-element.162), channel_id=1, source_target_pairs={{0,2},{1,3},{2,0},{3,1},{4,6},{5,7},{6,4},{7,5},{8,10},{9,11},{10,... | collective-permute-start | bytes 196616 | tf_op jit(solution)/shard_map/ppermute | solution.py:489
  12.1 11.6 %collective-permute-start.5 = (f32[64,256]{1,0:T(8,128)S(1)}, f32[64,256]{1,0:T(8,128)S(1)}, u32[]{:S(2)}, u32[]{:S(2)}) collective-permute-start(f32[64,256]{1,0:T(8,128)S(1)} %get-tuple-element.161), channel_id=1, source_target_pairs={{0,6},{1,7},{2,4},{3,5},{4,2},{5,3},{6,0},{7,1},{8,14},{9,15},{10,... | collective-permute-start | bytes 196616 | tf_op jit(solution)/shard_map/ppermute | solution.py:493
  13.6 10.1 %collective-permute-start.3 = (f32[72,256]{1,0:T(8,128)S(1)}, f32[72,256]{1,0:T(8,128)S(1)}, u32[]{:S(2)}, u32[]{:S(2)}) collective-permute-start(f32[72,256]{1,0:T(8,128)S(1)} %slice_bitcast_fusion), channel_id=1, source_target_pairs={{0,4},{4,0},{8,12},{12,8},{16,20},{20,16},{24,28},{28,24},{1,5},{5... | collective-permute-start | bytes 221192 | tf_op jit(solution)/shard_map/ppermute | solution.py:490
  14.5 9.2 %copy-start.2 = (f32[256]{0:T(256)S(1)}, f32[256]{0:T(256)}, u32[]{:S(2)}) copy-start(f32[256]{0:T(256)} %param.9) | copy-start | bytes 3076
  33.7 17.7 %collective-permute-start.9 = (f32[256,256]{1,0:T(8,128)S(1)}, f32[256,256]{1,0:T(8,128)S(1)}, u32[]{:S(2)}, u32[]{:S(2)}) collective-permute-start(f32[256,256]{1,0:T(8,128)S(1)} %get-tuple-element.128), channel_id=1, source_target_pairs={{16,24},{8,0},{20,28},{12,4},{17,25},{9,1},{21,29},{13,5},{18,26},... | collective-permute-start | bytes 786440 | tf_op jit(solution)/shard_map/ppermute | solution.py:538
  35.0 5.9 %collective-permute-start.6 = (f32[8,256]{1,0:T(8,128)S(1)}, f32[8,256]{1,0:T(8,128)S(1)}, u32[]{:S(2)}, u32[]{:S(2)}) collective-permute-start(f32[8,256]{1,0:T(8,128)S(1)} %get-tuple-element.123), channel_id=1, source_target_pairs={{0,8},{24,16},{4,12},{28,20},{1,9},{25,17},{5,13},{29,21},{2,10},{... | collective-permute-start | bytes 24584 | tf_op jit(solution)/shard_map/ppermute | solution.py:537
  41.7 3.1 %collective-permute-start.7 = (f32[8,256]{1,0:T(8,128)S(1)}, f32[8,256]{1,0:T(8,128)S(1)}, u32[]{:S(2)}, u32[]{:S(2)}) collective-permute-start(f32[8,256]{1,0:T(8,128)S(1)} %get-tuple-element.127), channel_id=1, source_target_pairs={{8,16},{16,8},{12,20},{20,12},{9,17},{17,9},{13,21},{21,13},{10,18... | collective-permute-start | bytes 24584 | tf_op jit(solution)/shard_map/ppermute | solution.py:544
  42.5 9.0 %collective-permute-start.8 = (f32[8,256]{1,0:T(8,128)S(1)}, f32[8,256]{1,0:T(8,128)S(1)}, u32[]{:S(2)}, u32[]{:S(2)}) collective-permute-start(f32[8,256]{1,0:T(8,128)S(1)} %get-tuple-element.127), channel_id=1, source_target_pairs={{8,24},{16,0},{12,28},{20,4},{9,25},{17,1},{13,29},{21,5},{10,26},... | collective-permute-start | bytes 24584 | tf_op jit(solution)/shard_map/ppermute | solution.py:545
  57.0 21.3 %all-to-all-start.1 = ((f32[32,16,256]{2,1,0:T(8,128)}), f32[32,16,256]{2,1,0:T(8,128)S(1)}, u32[]{:S(2)}, u32[]{:S(2)}) async-start(f32[32,16,256]{2,1,0:T(8,128)} %bitcast.9), calls=%async_computation.1 | async-start | bytes 1048576 | tf_op jit(solution)/shard_map/all_to_all | solution.py:557
  62.7 6.8 %collective-permute-start.10 = (f32[64,256]{1,0:T(8,128)S(1)}, f32[64,256]{1,0:T(8,128)S(1)}, u32[]{:S(2)}, u32[]{:S(2)}) collective-permute-start(f32[64,256]{1,0:T(8,128)S(1)} %get-tuple-element.134), channel_id=1, source_target_pairs={{0,4},{4,0},{8,12},{12,8},{16,20},{20,16},{24,28},{28,24},{1,5},{5... | collective-permute-start | bytes 196616 | tf_op jit(solution)/shard_map/ppermute | solution.py:554
